TPU v7x, 32 devices: a whole 2x2x4 slice. The times are simulated.
32 devices in a mesh: axial: 8 (over y, x, core), azim: 4 (over z).
Axes of the slice: x: 2, y: 2, z: 4, core: 2. Of those that a mesh axis runs over, the one named last changes fastest.
Arguments:
- displace: float32 [3, 128, 12, 512], P(None, 'axial', None, 'azim'), may hold values from -6 to 6
- velocity: float32 [3, 128, 12, 512], P(None, 'axial', None, 'azim'), may hold values from -4 to 4
- micro_modulus_values: float32 [128, 12, 512], P('axial', None, 'azim'), may hold values from 0.5 to 2
- thermal: float32 [192, 512], P('axial', 'azim'), may hold values from 0 to 2
- owner_of: int32 [8, 4, 48, 1], P('axial', 'azim'), may hold values from 0 to 7; in each aligned block of 48 rows (0 to 47, 48 to 95, ..., all dimensions but the last counted through in order) at most 12 rows name the same one
- row_of: int32 [8, 4, 48], P('axial', 'azim'), may hold values from 0 to 23
- breaks: int32 [4, 8, 4, 512], P(None, 'axial', 'azim'), may hold values from 0 to 368639, as said below
Outputs:
- disp_out: float32 [3, 128, 12, 512], P(None, 'axial', None, 'azim')
- veloc_out: float32 [3, 128, 12, 512], P(None, 'axial', None, 'azim')
- heat_source: float32 [192, 512], P('axial', 'azim')
Inputs may be any that keep to these rules, and one draw needn't show every extreme that they name: `owner_of`: among the 48 requests of one device, no owner is named more than 12 times, a bound that some block reaches. `breaks`: Codes may repeat.
All inputs are finite; a program needn't handle non-finite values.
Results may differ from a plain program's by a relative error of at most 0.00011.
Values sent between devices are 32-bit elements; how exact they have to be, the bound alone decides.
No kernel may reach another device: no remote copies, remote signals or barrier semaphores. Data moves between devices by JAX's collectives and lax.ppermute only.
A program may use at most 128 MiB of HBM per device.

v0:
```python
import math

import jax
import jax.numpy as jnp
from jax import lax
from jax.experimental import pallas as pl
from jax.experimental.pallas import tpu as pltpu
from jax.sharding import PartitionSpec as P

DILATION = 0.25
DT = 0.2
CA, NR, CZ = 16, 12, 128
REACH = 3
SLOT = 16
PAIR = 2 * NR
NFIELD = 7
NEXACT = lax.Precision.HIGHEST
F32 = jnp.float32


def offset_table():
    table = []
    for da in range(REACH + 1):
        for dz in range(-REACH, REACH + 1):
            if da * da + dz * dz <= REACH * REACH and (da > 0 or dz > 0):
                table.append((da, 0, dz))
    table.append((0, 1, 0))
    return table


OFFSETS = offset_table()
NBOND = len(OFFSETS)
NUMBER = {o: i for i, o in enumerate(OFFSETS)}


def scales(o):
    return sum(x * x for x in o), math.gcd(math.gcd(o[0], o[1]), abs(o[2]))


def roll(x, shift, axis=1):
    shift %= x.shape[axis]
    return pltpu.roll(x, shift, axis) if shift else x


def lanes_of(shape=(NR, CZ)):
    return lax.broadcasted_iota(jnp.int32, shape, 1)


def dot_nt(a, b):
    return lax.dot_general(a, b, (((1,), (1,)), ((), ())), preferred_element_type=F32)


class Sizes:
    def __init__(self, sections):
        self.sections = sections
        self.halo = REACH * sections
        self.ext = CA + 2 * self.halo
        self.code_at = NFIELD * self.halo * NR
        self.code_rows = sections * 4
        self.tab_at = self.code_at + self.code_rows
        self.tab_rows = CA // 2 * NR
        self.edge_rows = self.tab_at + self.tab_rows
        self.tiles = self.ext * SLOT // CZ
        self.strip_code_at = (NFIELD + 1) * self.tiles * NR
        self.strip_rows = self.strip_code_at + 3 * self.code_rows

    def source(self, a):
        if a < self.halo:
            return 0, CA - self.halo + a, a
        if a < self.halo + CA:
            return 1, a - self.halo, None
        return 2, a - self.halo - CA, a - self.halo - CA


def own_plane(refs, f, a):
    disp, velo, stiff = refs
    if f < 3:
        return disp[f, a]
    if f < 6:
        return velo[f - 3, a]
    return stiff[a]


def field_plane(sz, refs, low, high, temp, f, a):
    if f == NFIELD:
        return temp[pl.ds(a // 2 * NR, NR), :]
    which, there, edge = sz.source(a)
    if which == 1:
        return own_plane(refs, f, there)
    src = low if which == 0 else high
    return src[pl.ds((f * sz.halo + edge) * NR, NR), :]


def pack_axial(sz, disp, velo, stiff, codes, table, up, down):
    refs = (disp, velo, stiff)
    for f in range(NFIELD):
        for i in range(sz.halo):
            at = pl.ds((f * sz.halo + i) * NR, NR)
            up[at, :] = own_plane(refs, f, CA - sz.halo + i)
            down[at, :] = own_plane(refs, f, i)
    for out in (up, down):
        out[pl.ds(sz.code_at, sz.code_rows), :] = codes[...].astype(F32)
        out[pl.ds(sz.tab_at, sz.tab_rows), :] = table[...].astype(F32)


def pack_azimuth(sz, disp, velo, stiff, codes, table, low, high, thermal, left, right, temp):
    refs = (disp, velo, stiff)
    rows = thermal.shape[0]
    at = 0
    for which in range(3):
        if which == 1:
            tab = table[...].astype(F32)
        else:
            tab = (low if which == 0 else high)[pl.ds(sz.tab_at, sz.tab_rows), :]
        column = lax.broadcasted_iota(jnp.int32, (sz.tab_rows, rows), 1).astype(F32)
        hot = (tab[:, 0:1] == column).astype(F32)
        got = jnp.dot(hot, thermal[...], precision=NEXACT, preferred_element_type=F32)
        first = (CA - sz.halo) // 2 * NR if which == 0 else 0
        count = (CA if which == 1 else sz.halo) // 2 * NR
        temp[pl.ds(at, count), :] = got[first : first + count]
        at += count
    lane = lanes_of()
    per = CZ // SLOT
    for f in range(NFIELD + 1):
        for t in range(sz.tiles):
            to_left = to_right = None
            for s in range(per):
                x = field_plane(sz, refs, low, high, temp, f, t * per + s)
                a = roll(x, SLOT * s)
                b = roll(x, SLOT * s + SLOT)
                if s == 0:
                    to_left, to_right = a, b
                else:
                    here = lane >= SLOT * s
                    to_left = jnp.where(here, a, to_left)
                    to_right = jnp.where(here, b, to_right)
            here = pl.ds((f * sz.tiles + t) * NR, NR)
            left[here, :] = to_left
            right[here, :] = to_right
    for out in (left, right):
        at = sz.strip_code_at
        n = sz.code_rows
        out[pl.ds(at, n), :] = low[pl.ds(sz.code_at, n), :]
        out[pl.ds(at + n, n), :] = codes[...].astype(F32)
        out[pl.ds(at + 2 * n, n), :] = high[pl.ds(sz.code_at, n), :]


def decode(codes):
    hi = jnp.floor(codes * (1.0 / CZ))
    z = codes - hi * CZ
    k = jnp.floor((hi + 0.5) * (1.0 / (CA * NR)))
    rest = hi - k * (CA * NR)
    a = jnp.floor((rest + 0.5) * (1.0 / NR))
    return k, a, rest - a * NR, z


def spread(ref, index, weights, rows):
    at = lax.broadcasted_iota(jnp.int32, (rows, CZ), 0).astype(F32)
    for i in range(index.shape[0]):
        w = 1.0 if weights is None else weights[i]
        ref[pl.ds(0, rows), pl.ds(i * CZ, CZ)] = jnp.where(at == index[i : i + 1, :], w, 0.0).astype(
            jnp.bfloat16
        )


def read_breaks(sz, codes, from_left, from_right, broken, rows_ref, cols_ref, main, sl, sr):
    weights = [2.0 ** (-12 * (i // 4)) for i in range(sz.code_rows)]
    lane = lanes_of()
    n = sz.code_rows * CZ
    per = CZ // SLOT
    for which in range(3):
        k, a, r, z = decode(codes[which])
        group = jnp.floor(a * 0.25)
        spread(rows_ref, k * (4 * NR) + group * NR + r, None, NBOND * 4 * NR)
        spread(cols_ref, (a - 4 * group) * CZ + z, weights, 4 * CZ)
        main[...] = dot_nt(rows_ref[...], cols_ref[...])
        for side, out in ((from_left[which], sl), (from_right[which], sr)):
            k, a, r, z = decode(side)
            if out is sl:
                slot = jnp.where(z >= CZ - SLOT, a * SLOT + z - (CZ - SLOT), -1.0)
            else:
                slot = jnp.where(z < SLOT, a * SLOT + z, -1.0)
            spread(rows_ref, k * 16 + r, None, NBOND * 16)
            spread(cols_ref, slot, weights, CA * SLOT)
            out[...] = dot_nt(
                rows_ref[pl.ds(0, NBOND * 16), :], cols_ref[pl.ds(0, CA * SLOT), :]
            )
        planes = [p for p in range(sz.ext) if sz.source(p)[0] == which]

        def place(b, carry):
            block = main[pl.ds(pl.multiple_of(b * 4 * NR, 16), 4 * NR), :]
            left = sl[pl.ds(pl.multiple_of(b * 16, 16), 16), :]
            right = sr[pl.ds(pl.multiple_of(b * 16, 16), 16), :]
            for p in planes:
                a = sz.source(p)[1]
                x = block[a // 4 * NR : a // 4 * NR + NR, a % 4 * CZ : a % 4 * CZ + CZ]
                t, s = a // per, a % per
                one = roll(left[0:NR, t * CZ : (t + 1) * CZ], SLOT - SLOT * s)
                two = roll(right[0:NR, t * CZ : (t + 1) * CZ], CZ - 2 * SLOT - SLOT * s)
                broken[b, p, pl.ds(0, NR), :] = jnp.where(lane >= 32, roll(x, 32), one)
                broken[b, p, pl.ds(NR, NR), :] = jnp.where(lane < 96, roll(x, -32), two)
            return carry

        lax.fori_loop(0, NBOND, place, 0)


def march(
    sz, total, first, disp, velo, stiff, low, high, temp, strip_l, strip_r, codes, wanted,
    out_d, out_v, out_e, fld, stiffk, heatk, broken, fa, fz, energy, rows_ref, cols_ref, main, sl, sr,
):
    refs = (disp, velo, stiff)
    lane = lanes_of()
    per = CZ // SLOT
    n = sz.code_rows
    read_breaks(
        sz,
        [low[pl.ds(sz.code_at, n), :], codes[...].astype(F32), high[pl.ds(sz.code_at, n), :]],
        [strip_l[pl.ds(sz.strip_code_at + i * n, n), :] for i in range(3)],
        [strip_r[pl.ds(sz.strip_code_at + i * n, n), :] for i in range(3)],
        broken, rows_ref, cols_ref, main, sl, sr,
    )
    for f in range(NFIELD + 1):
        for p in range(sz.ext):
            x = field_plane(sz, refs, low, high, temp, f, p)
            t, s = p // per, p % per
            here = pl.ds((f * sz.tiles + t) * NR, NR)
            one = roll(strip_l[here, :], SLOT - SLOT * s)
            two = roll(strip_r[here, :], CZ - 2 * SLOT - SLOT * s)
            fld[f, p, pl.ds(0, NR), :] = jnp.where(lane >= 32, roll(x, 32), one)
            fld[f, p, pl.ds(NR, NR), :] = jnp.where(lane < 96, roll(x, -32), two)

    row = lax.broadcasted_iota(jnp.int32, (PAIR, CZ), 0)
    not_top = jnp.where((row == NR - 1) | (row == PAIR - 1), 0.0, 1.0)
    start = first[0]

    def prepare(p, carry):
        at = start + p
        live = [
            jnp.where((at >= 0) & (at + da < total), 1.0, 0.0).astype(F32) for da in range(REACH + 1)
        ]
        for k, (da, dr, dz) in enumerate(OFFSETS):
            n2, d = scales((da, dr, dz))
            c = fld[6, p]
            h = fld[7, p]
            if dr:
                c2, h2 = roll(c, -1, 0), roll(h, -1, 0)
            else:
                c2, h2 = roll(fld[6, p + da], -dz), roll(fld[7, p + da], -dz)
            m = (c + c2) * (live[da] * (0.5 * d * d / (n2 * n2)))
            stiffk[k, p] = m * not_top if dr else m
            heatk[k, p] = (h + h2) * (DILATION * 0.5 * n2 / d)
        return carry

    last = sz.ext - REACH
    lax.fori_loop(0, last, prepare, 0)
    energy[...] = jnp.zeros_like(energy)

    def advance(p, limit, with_energy):
        ua, ur, uz = fld[0, p], fld[1, p], fld[2, p]
        sums = {}

        def bond(o, elongation):
            k = NUMBER[o]
            q = elongation - heatk[k, p]
            g = jnp.where(broken[k, p] >= limit, 0.0, stiffk[k, p]) * q
            if with_energy:
                n2 = scales(o)[0]
                sums[n2] = sums[n2] + g * q if n2 in sums else g * q
            return g

        force_a = fa[p]
        force_z = fz[p]
        for dz in (1, 2, 3):
            g = bond((0, 0, dz), roll(uz, -dz) - uz)
            force_z = force_z + (g - roll(g, dz))
        g = bond((0, 1, 0), roll(ur, -1, 0) - ur)
        force_r = g - roll(g, 1, 0)
        for da in (1, 2):
            ua2, uz2 = fld[0, p + da], fld[2, p + da]
            g = bond((da, 0, 0), ua2 - ua)
            force_a = force_a + g
            push_a = g
            push_z = None
            for dz in (1, 2):
                gs = []
                for sign in (1, -1):
                    dua = roll(ua2, -sign * dz) - ua
                    duz = roll(uz2, -sign * dz) - uz
                    if da == dz:
                        e = dua + duz if sign > 0 else dua - duz
                    elif dz == 2:
                        e = dua + (2.0 * sign) * duz
                    else:
                        e = 2.0 * dua + duz if sign > 0 else 2.0 * dua - duz
                    gs.append(bond((da, 0, sign * dz), e))
                ma = 1.0 if da == dz else float(da)
                mz = 1.0 if da == dz else float(dz)
                own_s, own_d = gs[0] + gs[1], gs[0] - gs[1]
                plus, minus = roll(gs[0], dz), roll(gs[1], -dz)
                far_s, far_d = plus + minus, plus - minus
                if ma != 1.0:
                    own_s, far_s = ma * own_s, ma * far_s
                if mz != 1.0:
                    own_d, far_d = mz * own_d, mz * far_d
                force_a = force_a + own_s
                force_z = force_z + own_d
                push_a = push_a + far_s
                push_z = far_d if push_z is None else push_z + far_d
            fa[p + da] = fa[p + da] - push_a
            fz[p + da] = fz[p + da] - push_z
        g = bond((3, 0, 0), fld[0, p + 3] - ua)
        force_a = force_a + g
        fa[p + 3] = -g
        fz[p + 3] = jnp.zeros_like(g)
        for f, u, force in ((0, ua, force_a), (1, ur, force_r), (2, uz, force_z)):
            v = fld[3 + f, p] + DT * force
            fld[3 + f, p] = v
            fld[f, p] = u + DT * v
        if with_energy:
            e = None
            for n2, x in sums.items():
                y = x * (0.5 / math.sqrt(n2))
                e = y if e is None else e + y
            energy[p - sz.halo] = energy[p - sz.halo] + e

    def step(s, limit):
        def quiet(p, c):
            advance(p, limit, False)
            return c

        def counted(p, c):
            advance(p, limit, True)
            return c

        lax.fori_loop(REACH * s, sz.halo, quiet, 0)
        lax.fori_loop(sz.halo, sz.halo + CA, counted, 0)
        lax.fori_loop(sz.halo + CA, last - REACH * s, quiet, 0)
        return limit * (2.0**-12)

    fa[...] = jnp.zeros_like(fa)
    fz[...] = jnp.zeros_like(fz)
    lax.fori_loop(0, sz.sections, step, jnp.float32(1.0))

    def joined(plane):
        return jnp.where(lane < CZ // 2, roll(plane[0:NR], -32), roll(plane[NR:PAIR], 32))

    for c in range(3):
        for a in range(CA):
            out_d[c, a] = joined(fld[c, sz.halo + a])
            out_v[c, a] = joined(fld[3 + c, sz.halo + a])
    pooled = jnp.concatenate(
        [joined(energy[2 * b] + energy[2 * b + 1]) for b in range(CA // 2)], axis=0
    ) * (0.25 / sz.sections)
    rows = out_e.shape[0]
    row_id = lax.broadcasted_iota(jnp.int32, (rows, sz.tab_rows), 0)
    hot = (row_id == wanted[0:1, 0 : sz.tab_rows]).astype(F32)
    out_e[...] = jnp.dot(hot, pooled, precision=NEXACT, preferred_element_type=F32)


def call(body, out_shape, scratch=(), smem_first=False, n_in=0):
    spec = [pl.BlockSpec(memory_space=pltpu.VMEM)] * n_in
    if smem_first:
        spec[0] = pl.BlockSpec(memory_space=pltpu.SMEM)
    return pl.pallas_call(
        body,
        out_shape=[jax.ShapeDtypeStruct(s, F32) for s in out_shape],
        in_specs=spec,
        out_specs=[pl.BlockSpec(memory_space=pltpu.VMEM)] * len(out_shape),
        scratch_shapes=list(scratch),
        compiler_params=pltpu.CompilerParams(vmem_limit_bytes=58 << 20),
    )


def on_device(displace, velocity, stiff, thermal, owner_of, row_of, breaks):
    sz = Sizes(breaks.shape[0])
    groups = lax.axis_size("axial")
    around = lax.axis_size("azim")
    held = thermal.shape[0]
    codes = breaks.reshape(sz.code_rows, CZ)
    wanted = (owner_of.reshape(-1) * held + row_of.reshape(-1)).reshape(CA // 2, NR // 2, 1)
    wanted = jnp.broadcast_to(wanted, (CA // 2, NR // 2, 2)).reshape(sz.tab_rows)
    table = jnp.broadcast_to(wanted[:, None], (sz.tab_rows, CZ))
    lanes = jnp.pad(wanted, (0, CZ - sz.tab_rows))[None, :]

    def body(f):
        return lambda *refs: f(sz, *refs)

    edge = (sz.edge_rows, CZ)
    up, down = call(body(pack_axial), [edge, edge], n_in=5)(displace, velocity, stiff, codes, table)
    low = lax.ppermute(up, "axial", [(i, i + 1) for i in range(groups - 1)])
    high = lax.ppermute(down, "axial", [(i + 1, i) for i in range(groups - 1)])
    everyone = lax.all_gather(thermal, "axial", tiled=True)
    strip = (sz.strip_rows, CZ)
    left, right, temp = call(
        body(pack_azimuth), [strip, strip, (sz.ext // 2 * NR, CZ)], n_in=8
    )(displace, velocity, stiff, codes, table, low, high, everyone)
    strip_r = lax.ppermute(left, "azim", [(i, (i - 1) % around) for i in range(around)])
    strip_l = lax.ppermute(right, "azim", [(i, (i + 1) % around) for i in range(around)])
    first = (lax.axis_index("axial") * CA - sz.halo).astype(jnp.int32).reshape(1)
    plane = (PAIR, CZ)
    n = sz.code_rows * CZ
    scratch = [
        pltpu.VMEM((NFIELD + 1, sz.ext) + plane, F32),
        pltpu.VMEM((NBOND, sz.ext) + plane, F32),
        pltpu.VMEM((NBOND, sz.ext) + plane, F32),
        pltpu.VMEM((NBOND, sz.ext) + plane, F32),
        pltpu.VMEM((sz.ext,) + plane, F32),
        pltpu.VMEM((sz.ext,) + plane, F32),
        pltpu.VMEM((CA,) + plane, F32),
        pltpu.VMEM((NBOND * 4 * NR, n), jnp.bfloat16),
        pltpu.VMEM((4 * CZ, n), jnp.bfloat16),
        pltpu.VMEM((NBOND * 4 * NR, 4 * CZ), F32),
        pltpu.VMEM((NBOND * 16, CA * SLOT), F32),
        pltpu.VMEM((NBOND * 16, CA * SLOT), F32),
    ]
    total = groups * CA
    out_d, out_v, out_e = call(
        lambda *refs: march(sz, total, *refs),
        [displace.shape, velocity.shape, (groups * held, CZ)],
        scratch,
        smem_first=True,
        n_in=11,
    )(first, displace, velocity, stiff, low, high, temp, strip_l, strip_r, codes, lanes)
    parts = out_e.reshape(groups, held, CZ)
    arrived = lax.all_to_all(parts, "axial", split_axis=0, concat_axis=0, tiled=True)
    return out_d, out_v, jnp.sum(arrived, axis=0)


def solution(mesh):
    return jax.shard_map(
        on_device,
        mesh=mesh,
        in_specs=(
            P(None, "axial", None, "azim"),
            P(None, "axial", None, "azim"),
            P("axial", None, "azim"),
            P("axial", "azim"),
            P("axial", "azim", None, None),
            P("axial", "azim", None),
            P(None, "axial", "azim", None),
        ),
        out_specs=(
            P(None, "axial", None, "azim"),
            P(None, "axial", None, "azim"),
            P("axial", "azim"),
        ),
        check_vma=False,
    )
```

profile of v0, /device:TPU:0, one launch (start us, length us, event | category | flops | bytes accessed | tf_op | source)
XLA Modules:
  0.0 116.4 jit_solution(11125278301540624832)
XLA Ops:
  0.6 0.7 multiply_reduce_fusion
  1.4 0.1 mul.19
  1.4 0.5 broadcast.14
  2.0 1.3 %reduce.7 = s32[48]{0:T(128)S(1)} reduce(s32[1,1,48]{2,1,0:T(1,128)} %param.12, s32[]{:T(128)} %broadcast.14), dimensions={0,1}, to_apply=%param.12.reduce_sub_computation.3 | reduce | bytes 388 | tf_op args[5]
  3.3 0.1 reshape.36
  3.4 0.1 broadcast_in_dim.15
  3.4 0.1 broadcast_in_dim.16
  3.6 1.6 %copy.29.refs_2_.refs_3_ = f32[16,12,128]{2,1,0:T(8,128)} copy(f32[16,12,128]{2,0,1:T(8,128)} %param.9) | data formatting | bytes 196608 | tf_op args[2]
  5.1 0.9 copy.27.refs_0_.refs_1_
  6.0 0.1 copy-done.4
  6.1 0.9 copy.28.refs_1_.refs_2_
  7.0 0.7 broadcast_in_dim.17.refs_4_
  7.7 2.3 %shard_map.94 = (f32[1120,128]{1,0:T(8,128)}, f32[1120,128]{1,0:T(8,128)}) custom-call(f32[3,16,12,128]{3,2,1,0:T(8,128)} %copy.27.refs_0_.refs_1_, f32[3,16,12,128]{3,2,1,0:T(8,128)} %copy.28.refs_1_.refs_2_, f32[16,12,128]{2,1,0:T(8,128)} %copy.29.refs_2_.refs_3_, s32[16,128]{1,0:T(8,128)} %bitcast.6, s32[96,128]{1,0:T(8,128)} %broadcast_in_dim.17.refs_4_), custom_call_target="tpu_custom_call" | custom-call | tf_op jit(solution)/shard_map/pallas_call | solution.py:389
  9.9 2.4 %collective-permute-start = (f32[1120,128]{1,0:T(8,128)}, f32[1120,128]{1,0:T(8,128)S(1)}, u32[]{:S(2)}, u32[]{:S(2)}) collective-permute-start(f32[1120,128]{1,0:T(8,128)} %get-tuple-element.11), channel_id=1, source_target_pairs={{0,4},{4,8},{8,12},{12,16},{16,20},{20,24},{24,28},{1,5},{5,9},{9,... | collective-permute-start | bytes 1720328 | tf_op jit(solution)/shard_map/ppermute | solution.py:390
  12.3 1.3 %collective-permute-start.1 = (f32[1120,128]{1,0:T(8,128)}, f32[1120,128]{1,0:T(8,128)S(1)}, u32[]{:S(2)}, u32[]{:S(2)}) collective-permute-start(f32[1120,128]{1,0:T(8,128)} %get-tuple-element.12), channel_id=1, source_target_pairs={{4,0},{8,4},{12,8},{16,12},{20,16},{24,20},{28,24},{5,1},{9,5},{13... | collective-permute-start | bytes 1720328 | tf_op jit(solution)/shard_map/ppermute | solution.py:391
  13.6 19.3 %all_gather.3.refs_7_ = f32[192,128]{1,0:T(8,128)} all-gather(f32[24,128]{1,0:T(8,128)S(1)} %copy-done.7), channel_id=1, replica_groups=mesh['axial'=8,'azim'=4] {'axial'}, dimensions={0}, use_global_device_ids=true | all-gather | bytes 110592 | tf_op jit(solution)/shard_map/all_gather | solution.py:392
  32.9 0.0 collective-permute-done.refs_5_.refs_4_
  32.9 0.8 copy-done
  33.7 0.8 copy-done.1
  34.5 3.7 %shard_map.95 = (f32[528,128]{1,0:T(8,128)}, f32[528,128]{1,0:T(8,128)}, f32[240,128]{1,0:T(8,128)}) custom-call(f32[3,16,12,128]{3,2,1,0:T(8,128)} %copy.27.refs_0_.refs_1_, f32[3,16,12,128]{3,2,1,0:T(8,128)} %copy.28.refs_1_.refs_2_, f32[16,12,128]{2,1,0:T(8,128)} %copy.29.refs_2_.refs_3_, s32[16,128]{1,0:T(8,128)} %bitcast.7, ...), custom_call_target="tpu_custom_call" | custom-call | tf_op jit(solution)/shard_map/pallas_call | solution.py:394
  38.2 1.6 %collective-permute-start.2 = (f32[528,128]{1,0:T(8,128)}, f32[528,128]{1,0:T(8,128)S(1)}, u32[]{:S(2)}, u32[]{:S(2)}) collective-permute-start(f32[528,128]{1,0:T(8,128)} %get-tuple-element.14), channel_id=1, source_target_pairs={{0,1},{1,2},{2,3},{3,0},{4,5},{5,6},{6,7},{7,4},{8,9},{9,10},{10,1... | collective-permute-start | bytes 811016 | tf_op jit(solution)/shard_map/ppermute | solution.py:398
  39.8 2.2 %collective-permute-start.3 = (f32[528,128]{1,0:T(8,128)}, f32[528,128]{1,0:T(8,128)S(1)}, u32[]{:S(2)}, u32[]{:S(2)}) collective-permute-start(f32[528,128]{1,0:T(8,128)} %get-tuple-element.15), channel_id=1, source_target_pairs={{0,3},{1,0},{2,1},{3,2},{4,7},{5,4},{6,5},{7,6},{8,11},{9,8},{10,9... | collective-permute-start | bytes 811016 | tf_op jit(solution)/shard_map/ppermute | solution.py:397
  42.1 0.6 pad_bitcast_fusion.refs_10_
  42.6 7.0 %collective-permute-done.2.refs_7_ = f32[528,128]{1,0:T(8,128)S(1)} collective-permute-done((f32[528,128]{1,0:T(8,128)}, f32[528,128]{1,0:T(8,128)S(1)}, u32[]{:S(2)}, u32[]{:S(2)}) %collective-permute-start.2) | collective-permute-done | bytes 270368 | tf_op jit(solution)/shard_map/ppermute | solution.py:398
  49.6 4.5 %collective-permute-done.3.refs_8_ = f32[528,128]{1,0:T(8,128)S(1)} collective-permute-done((f32[528,128]{1,0:T(8,128)}, f32[528,128]{1,0:T(8,128)S(1)}, u32[]{:S(2)}, u32[]{:S(2)}) %collective-permute-start.3) | collective-permute-done | bytes 270368 | tf_op jit(solution)/shard_map/ppermute | solution.py:397
  54.1 0.7 copy-done.6
  54.8 51.7 %shard_map.96 = (f32[3,16,12,128]{3,2,1,0:T(8,128)}, f32[3,16,12,128]{3,2,1,0:T(8,128)}, f32[192,128]{1,0:T(8,128)}) custom-call(s32[1]{0:T(128)} %bitcast.refs_0_, f32[3,16,12,128]{3,2,1,0:T(8,128)} %copy.27.refs_0_.refs_1_, f32[3,16,12,128]{3,2,1,0:T(8,128)} %copy.28.refs_1_.refs_2_, f32[16,12,128]{2,1,0:T(8,128)} %copy.29.refs_2_.refs_3_, ...), custom_call_target="tpu_custom_call" | custom-call | tf_op jit(solution)/shard_map/pallas_call | solution.py:417
  106.5 4.1 %all-to-all-start = ((f32[8,24,128]{2,1,0:T(8,128)}), f32[8,24,128]{2,1,0:T(8,128)S(1)}, u32[]{:S(2)}, u32[]{:S(2)}) async-start(f32[8,24,128]{2,1,0:T(8,128)} %bitcast.5), calls=%async_computation | async-start | bytes 196608 | tf_op jit(solution)/shard_map/all_to_all | solution.py:425
  110.6 1.9 %copy.30 = f32[3,16,12,128]{3,1,2,0:T(8,128)} copy(f32[3,16,12,128]{3,2,1,0:T(8,128)} %get-tuple-element.22) | data formatting | bytes 589824
  112.5 0.8 copy.31
  113.3 2.5 %all-to-all-done = f32[8,24,128]{2,1,0:T(8,128)S(1)} async-done(((f32[8,24,128]{2,1,0:T(8,128)}), f32[8,24,128]{2,1,0:T(8,128)S(1)}, u32[]{:S(2)}, u32[]{:S(2)}) %all-to-all-start) | async-done | bytes 98336 | tf_op jit(solution)/shard_map/all_to_all | solution.py:425
  115.8 0.6 reduce_sum.9
  (14 shorter events, 0.0 us)
Async XLA Ops:
  0.6 4.5 %copy-start.3 = (f32[3,16,12,128]{3,1,2,0:T(8,128)S(1)}, f32[3,16,12,128]{3,1,2,0:T(8,128)}, u32[]{:S(2)}) copy-start(f32[3,16,12,128]{3,1,2,0:T(8,128)} %param.7) | copy-start | bytes 884740
  5.1 1.0 copy-start.4
  7.7 6.0 %copy-start.7 = (f32[24,128]{1,0:T(8,128)S(1)}, f32[24,128]{1,0:T(8,128)}, u32[]{:S(2)}) copy-start(f32[24,128]{1,0:T(8,128)} %param.10) | copy-start | bytes 36868
  9.9 23.0 %collective-permute-start = (f32[1120,128]{1,0:T(8,128)}, f32[1120,128]{1,0:T(8,128)S(1)}, u32[]{:S(2)}, u32[]{:S(2)}) collective-permute-start(f32[1120,128]{1,0:T(8,128)} %get-tuple-element.11), channel_id=1, source_target_pairs={{0,4},{4,8},{8,12},{12,16},{16,20},{20,24},{24,28},{1,5},{5,9},{9,... | collective-permute-start | bytes 1720328 | tf_op jit(solution)/shard_map/ppermute | solution.py:390
  12.3 20.6 %collective-permute-start.1 = (f32[1120,128]{1,0:T(8,128)}, f32[1120,128]{1,0:T(8,128)S(1)}, u32[]{:S(2)}, u32[]{:S(2)}) collective-permute-start(f32[1120,128]{1,0:T(8,128)} %get-tuple-element.12), channel_id=1, source_target_pairs={{4,0},{8,4},{12,8},{16,12},{20,16},{24,20},{28,24},{5,1},{9,5},{13... | collective-permute-start | bytes 1720328 | tf_op jit(solution)/shard_map/ppermute | solution.py:391
  32.9 0.8 copy-start
  33.7 0.8 copy-start.1
  38.2 11.4 %collective-permute-start.2 = (f32[528,128]{1,0:T(8,128)}, f32[528,128]{1,0:T(8,128)S(1)}, u32[]{:S(2)}, u32[]{:S(2)}) collective-permute-start(f32[528,128]{1,0:T(8,128)} %get-tuple-element.14), channel_id=1, source_target_pairs={{0,1},{1,2},{2,3},{3,0},{4,5},{5,6},{6,7},{7,4},{8,9},{9,10},{10,1... | collective-permute-start | bytes 811016 | tf_op jit(solution)/shard_map/ppermute | solution.py:398
  39.8 14.3 %collective-permute-start.3 = (f32[528,128]{1,0:T(8,128)}, f32[528,128]{1,0:T(8,128)S(1)}, u32[]{:S(2)}, u32[]{:S(2)}) collective-permute-start(f32[528,128]{1,0:T(8,128)} %get-tuple-element.15), channel_id=1, source_target_pairs={{0,3},{1,0},{2,1},{3,2},{4,7},{5,4},{6,5},{7,6},{8,11},{9,8},{10,9... | collective-permute-start | bytes 811016 | tf_op jit(solution)/shard_map/ppermute | solution.py:397
  49.6 4.5 %copy-start.5 = (f32[528,128]{1,0:T(8,128)}, f32[528,128]{1,0:T(8,128)S(1)}, u32[]{:S(2)}) copy-start(f32[528,128]{1,0:T(8,128)S(1)} %collective-permute-done.2.refs_7_) | copy-start | bytes 811012
  54.1 0.7 copy-start.6
  106.5 9.3 %all-to-all-start = ((f32[8,24,128]{2,1,0:T(8,128)}), f32[8,24,128]{2,1,0:T(8,128)S(1)}, u32[]{:S(2)}, u32[]{:S(2)}) async-start(f32[8,24,128]{2,1,0:T(8,128)} %bitcast.5), calls=%async_computation | async-start | bytes 196608 | tf_op jit(solution)/shard_map/all_to_all | solution.py:425
  110.6 1.9 %copy-start.2 = (f32[3,16,12,128]{3,2,1,0:T(8,128)S(1)}, f32[3,16,12,128]{3,2,1,0:T(8,128)}, u32[]{:S(2)}) copy-start(f32[3,16,12,128]{3,2,1,0:T(8,128)} %get-tuple-element.23) | copy-start | bytes 884740
where the time goes:
time: 117 us; the launch traced here: 116 us
  Pallas kernels  57.6 us (49%)
  blocking collectives  19.3 us (16%)
  waiting for transfers between devices  14 us (12%)
  starting transfers between devices  11.6 us (10%)
  local copies, waits for them, and re-layouts  10.5 us (9%)
  other arithmetic  2.65 us (2%)
    pallas_call x1, Pallas kernels, on_device(): call(lambda *refs: march(sz, total, *refs), [displace.shape, velocity.sha...  51.7 us
    all_gather x1, blocking collectives, on_device(): everyone = lax.all_gather(thermal, 'axial', tiled=True)  19.3 us
    unnamed x22, local copies, waits for them, and re-layouts  8.9 us
    ppermute x1, waiting for transfers between devices, on_device(): lax.ppermute(right, 'azim', [(i, (i + 1) % around) for i in range(around)])  6.98 us
    ppermute x1, waiting for transfers between devices, on_device(): lax.ppermute(left, 'azim', [(i, (i - 1) % around) for i in range(around)])  4.48 us
    all_to_all x1, starting transfers between devices, on_device(): lax.all_to_all(parts, 'axial', split_axis=0, concat_axis=0, tiled=True)  4.13 us
    pallas_call x1, Pallas kernels, on_device(): call(body(pack_azimuth), [strip, strip, (sz.ext // 2 * NR, CZ)], n_in=8)  3.7 us
    all_to_all x1, waiting for transfers between devices, on_device(): lax.all_to_all(parts, 'axial', split_axis=0, concat_axis=0, tiled=True)  2.53 us
  transfers between devices with their start and end apart: 5, of which 3 were waited for; matrix products, arithmetic and copies ran while one was open for 3% of the time, Pallas kernels for 0%

commit v1 on v0

v1 whole, which is shorter than its diff:
```python
import math

import jax
import jax.numpy as jnp
from jax import lax
from jax.experimental import pallas as pl
from jax.experimental.pallas import tpu as pltpu
from jax.sharding import PartitionSpec as P

DILATION = 0.25
DT = 0.2
CA, NR, CZ = 16, 12, 128
REACH = 3
SLOT = 16
PAIR = 2 * NR
PAD = 16
PER = CZ // SLOT
UNROLL = 3
NFIELD = 7
NEXACT = lax.Precision.HIGHEST
F32 = jnp.float32


def offset_table():
    table = []
    for da in range(REACH + 1):
        for dz in range(-REACH, REACH + 1):
            if da * da + dz * dz <= REACH * REACH and (da > 0 or dz > 0):
                table.append((da, 0, dz))
    table.append((0, 1, 0))
    return table


OFFSETS = offset_table()
NBOND = len(OFFSETS)
NUMBER = {o: i for i, o in enumerate(OFFSETS)}


def scales(o):
    return sum(x * x for x in o), math.gcd(math.gcd(o[0], o[1]), abs(o[2]))


def roll(x, shift, axis=1):
    shift %= x.shape[axis]
    return pltpu.roll(x, shift, axis) if shift else x


def lanes_of(shape=(NR, CZ)):
    return lax.broadcasted_iota(jnp.int32, shape, 1)


def dot_nt(a, b):
    return lax.dot_general(a, b, (((1,), (1,)), ((), ())), preferred_element_type=F32)


class Sizes:
    def __init__(self, sections):
        self.sections = sections
        self.halo = REACH * sections
        self.ext = CA + 2 * self.halo
        self.code_rows = 4 * sections
        self.edge_at = {}
        at = PAD
        for f in range(NFIELD):
            for e in range(self.halo):
                if not self.moving(f) or e < self.halo - REACH:
                    self.edge_at[f, e] = at
                    at += NR
        self.tab_at = -(-at // 8) * 8
        self.edge_rows = self.tab_at + PAD
        self.own_tiles = CA // PER
        self.side_rows = PAD + NFIELD * self.own_tiles * NR + PAD
        self.side_rows = -(-self.side_rows // 8) * 8
        self.far_tiles = 2 * self.halo // PER
        self.far_pad = 2 * self.code_rows
        self.heat_tiles = -(-self.ext // 2 // PER)
        self.far_rows = self.far_pad + (NFIELD * self.far_tiles + self.heat_tiles) * NR + PAD
        self.far_rows = -(-self.far_rows // 8) * 8
        self.temp_rows = PAD + self.ext // 2 * NR + PAD

    def moving(self, f):
        return 3 <= f < 6

    def edge_row(self, f, p):
        e = p if p < self.halo else p - self.halo - CA
        if self.moving(f) and p < self.halo:
            e -= REACH
        return self.edge_at.get((f, e))

    def source(self, p):
        if p < self.halo:
            return 0, CA - self.halo + p
        if p < self.halo + CA:
            return 1, p - self.halo
        return 2, p - self.halo - CA

    def side_row(self, f, t):
        return PAD + (f * self.own_tiles + t) * NR

    def far_row(self, f, t):
        return self.far_pad + (f * self.far_tiles + t) * NR


def own_plane(refs, f, a):
    disp, velo, stiff = refs
    ref, g = (disp, f) if f < 3 else (velo, f - 3) if f < 6 else (stiff, 0)
    return ref[pl.ds(g * CA * NR + a, NR, stride=CA), :]


def is_top():
    return lax.broadcasted_iota(jnp.int32, (PAIR, CZ), 0) < NR


def twice(upper, lower, at):
    return jnp.where(is_top(), upper[pl.ds(at, PAIR), :], lower[pl.ds(at - NR, PAIR), :])


def wanted_rows(table, count):
    rows = lax.broadcasted_iota(jnp.int32, (count, table.shape[1]), 0)
    return (rows == table).astype(F32)


def layers_of():
    shape = (CA // 2 * NR, CA // 2 * NR // 2)
    i = lax.broadcasted_iota(jnp.int32, shape, 0)
    j = lax.broadcasted_iota(jnp.int32, shape, 1)
    return (i // 2 == j).astype(F32)


def exact_dot(a, b, dims=((1,), (0,))):
    return lax.dot_general(a, b, (dims, ((), ())), precision=NEXACT, preferred_element_type=F32)


def pack_tiles(sz, planes, left, right, row):
    lane = lanes_of()
    to_left = to_right = None
    for s, x in enumerate(planes):
        if x is None:
            continue
        x = roll(x, SLOT * (s + 1))
        if to_left is None:
            to_left = to_right = x
            continue
        to_right = jnp.where(lane >= SLOT * s, x, to_right)
        n = (s + 1) % PER
        to_left = jnp.where((lane >= SLOT * n) & (lane < SLOT * (n + 1)), x, to_left)
    left[pl.ds(row, NR), :] = to_left
    right[pl.ds(row, NR), :] = to_right


def pack_first(sz, held, disp, velo, stiff, codes, owner, row_of, up, down, left, right, code_f):
    refs = (disp, velo, stiff)
    for f in range(NFIELD):
        for p in range(sz.halo):
            at = sz.edge_row(f, p)
            if at is not None:
                up[pl.ds(at, NR), :] = own_plane(refs, f, CA - sz.halo + p)
            at = sz.edge_row(f, p + sz.halo + CA)
            if at is not None:
                down[pl.ds(at, NR), :] = own_plane(refs, f, p)
        for t in range(sz.own_tiles):
            planes = [own_plane(refs, f, t * PER + s) for s in range(PER)]
            pack_tiles(sz, planes, left, right, sz.side_row(f, t))
    c = codes[...].astype(F32)
    code_f[...] = c
    table = (owner[...] * held + row_of[...]).astype(F32)
    blank = jnp.zeros((PAD, CZ), F32)
    for out in (up, down, left, right):
        out[pl.ds(out.shape[0] - PAD, PAD), :] = blank
        out[pl.ds(0, sz.code_rows), :] = c
    for out in (up, down):
        out[pl.ds(sz.tab_at, 1), pl.ds(0, table.shape[1])] = table


def pack_second(sz, held, low, high, thermal, owner, row_of, left, right, temp):
    n = owner.shape[1]
    rows = thermal.shape[0]
    heat = thermal[...]
    expand = layers_of()
    blank = jnp.zeros((PAD, CZ), F32)
    temp[pl.ds(0, PAD), :] = blank
    temp[pl.ds(sz.temp_rows - PAD, PAD), :] = blank
    at = PAD
    for which in range(3):
        if which == 1:
            table = owner[...] * held + row_of[...]
        else:
            src = low if which == 0 else high
            table = src[pl.ds(sz.tab_at, 1), :][:, 0:n].astype(jnp.int32)
        got = exact_dot(wanted_rows(table, rows), heat, ((0,), (0,)))
        got = exact_dot(expand, got)
        first = (CA - sz.halo) // 2 * NR if which == 0 else 0
        count = (CA if which == 1 else sz.halo) // 2 * NR
        temp[pl.ds(at, count), :] = got[first : first + count]
        at += count
    far = list(range(sz.halo)) + list(range(sz.halo + CA, sz.ext))
    for f in range(NFIELD):
        for t in range(sz.far_tiles):
            planes = []
            for p in far[t * PER : (t + 1) * PER]:
                at = sz.edge_row(f, p)
                src = low if p < sz.halo else high
                planes.append(None if at is None else src[pl.ds(at, NR), :])
            pack_tiles(sz, planes, left, right, sz.far_row(f, t))
    pairs = sz.ext // 2
    for t in range(sz.heat_tiles):
        planes = [temp[pl.ds(PAD + b * NR, NR), :] for b in range(t * PER, min(pairs, (t + 1) * PER))]
        pack_tiles(sz, planes, left, right, sz.far_row(NFIELD, t))
    for out in (left, right):
        out[pl.ds(sz.far_rows - PAD, PAD), :] = blank
        out[pl.ds(0, sz.code_rows), :] = low[pl.ds(0, sz.code_rows), :]
        out[pl.ds(sz.code_rows, sz.code_rows), :] = high[pl.ds(0, sz.code_rows), :]


def decode(codes):
    hi = jnp.floor(codes * (1.0 / CZ))
    z = codes - hi * CZ
    k = jnp.floor((hi + 0.5) * (1.0 / (CA * NR)))
    rest = hi - k * (CA * NR)
    a = jnp.floor((rest + 0.5) * (1.0 / NR))
    return k, a, rest - a * NR, z


def spread(ref, index, rows, chunk, lane_at=0, weigh=False):
    for first in range(0, rows, chunk):
        size = min(chunk, rows - first)
        near = jnp.clip(index - first, -1.0, 256.0)
        at = lax.broadcasted_iota(jnp.int32, (size, CZ), 0).astype(F32).astype(jnp.bfloat16)
        for i in range(index.shape[0]):
            w = jnp.full((size, CZ), 2.0 ** (-12 * (i // 4)) if weigh else 1.0, jnp.bfloat16)
            here = jnp.broadcast_to(near[i : i + 1, :], (size, CZ)).astype(jnp.bfloat16)
            ref[pl.ds(first, size), pl.ds(lane_at + i * CZ, CZ)] = jnp.where(
                at == here, w, jnp.zeros_like(w)
            )


def read_breaks(sz, codes, parts, out, rows_ref, cols_ref, acc):
    at = 0
    for src, lo_group, groups, planes in parts:
        k, a, r, z = decode(src)
        group = jnp.floor(a * 0.25)
        per_k = groups * NR
        rows = -(-NBOND * per_k // 16) * 16
        inside = (group >= lo_group) & (group < lo_group + groups)
        index = jnp.where(inside, k * per_k + (group - lo_group) * NR + r, -1.0)
        spread(rows_ref, index, rows, 240)
        spread(cols_ref, (a - 4 * group) * CZ + z, 4 * CZ, CZ * 2, weigh=True)
        acc[pl.ds(PAD, rows), :] = dot_nt(rows_ref[pl.ds(0, rows), :], cols_ref[...])
        for b in range(NBOND):
            for i, plane in enumerate(planes):
                row = PAD + b * per_k + (plane // 4 - lo_group) * NR
                lanes = pl.ds(plane % 4 * CZ, CZ)
                out[b, at + i] = jnp.where(
                    is_top(), acc[pl.ds(row, PAIR), lanes], acc[pl.ds(row - NR, PAIR), lanes]
                )
        at += len(planes)


def breaks_own(sz, codes, out, rows_ref, cols_ref, acc):
    acc[pl.ds(0, PAD), :] = jnp.zeros((PAD, 4 * CZ), F32)
    parts = [(codes[...], 0, CA // 4, list(range(CA)))]
    read_breaks(sz, None, parts, out, rows_ref, cols_ref, acc)


def breaks_far(sz, low, high, out, rows_ref, cols_ref, acc):
    acc[pl.ds(0, PAD), :] = jnp.zeros((PAD, 4 * CZ), F32)
    n = sz.code_rows
    parts = [
        (low[pl.ds(0, n), :], (CA - sz.halo) // 4, sz.halo // 4, list(range(CA - sz.halo, CA))),
        (high[pl.ds(0, n), :], 0, sz.halo // 4, list(range(sz.halo))),
    ]
    read_breaks(sz, None, parts, out, rows_ref, cols_ref, acc)


def side_breaks(sz, sources, broken, rows_ref, cols_ref, acc, edge):
    n = sz.code_rows * CZ
    rows = -(-NBOND * PAIR // 16) * 16
    for which, (left, right) in enumerate(sources):
        k, a, r, z = decode(left)
        spread(rows_ref, k * PAIR + r, rows, 240)
        spread(cols_ref, jnp.where(z >= CZ - SLOT, a * SLOT + z - (CZ - SLOT), -1.0), CA * SLOT, 256, weigh=True)
        k, a, r, z = decode(right)
        spread(rows_ref, k * PAIR + NR + r, rows, 240, lane_at=n)
        tile = jnp.floor(a * (1.0 / PER))
        slot = a - tile * PER + 1
        slot = jnp.where(slot == PER, 0.0, slot)
        spread(cols_ref, jnp.where(z < SLOT, tile * CZ + slot * SLOT + z, -1.0), CA * SLOT, 256, n, weigh=True)
        acc[...] = dot_nt(rows_ref[...], cols_ref[...])
        for p in range(sz.ext):
            if sz.source(p)[0] != which:
                continue
            a = sz.source(p)[1]
            for b in range(NBOND):
                x = acc[pl.ds(b * PAIR, PAIR), pl.ds(a // PER * CZ, CZ)]
                broken[b, p] = jnp.where(edge, roll(x, SLOT * (PER - 1 - a % PER)), broken[b, p])


def march(
    sz, total, held, first, disp, velo, stiff, low, high, temp, side_l, side_r, far_l, far_r, codes, owner, row_of,
    w_own, w_far, out_d, out_v, out_e, fld, stiffk, heatk, broken, fa, fz, energy, pooled, rows_ref, cols_ref, acc, sems,
):
    refs = (disp, velo, stiff)
    halo = sz.halo
    moves = [
        pltpu.make_async_copy(w_own, broken.at[:, pl.ds(halo, CA)], sems.at[0]),
        pltpu.make_async_copy(w_far.at[:, pl.ds(0, halo)], broken.at[:, pl.ds(0, halo)], sems.at[1]),
        pltpu.make_async_copy(w_far.at[:, pl.ds(halo, halo)], broken.at[:, pl.ds(halo + CA, halo)], sems.at[2]),
    ]
    for m in moves:
        m.start()
    lane = lanes_of()
    wide = lanes_of((PAIR, CZ))
    top = is_top()
    edge = (top & (wide >= CZ - SLOT)) | (~top & (wide < SLOT))
    n = sz.code_rows
    for f in range(NFIELD + 1):
        for p in range(sz.ext):
            which, a = sz.source(p)
            if f == NFIELD:
                x = twice(temp, temp, PAD + p // 2 * NR)
                s = p // 2
                t, s = s // PER, s % PER
                y = twice(far_l, far_r, sz.far_row(NFIELD, t))
            elif which == 1:
                x = own_plane(refs, f, a)
                x = jnp.concatenate([x, x], axis=0)
                t, s = a // PER, a % PER
                y = twice(side_l, side_r, sz.side_row(f, t))
            else:
                at = sz.edge_row(f, p)
                if at is None:
                    continue
                src = low if which == 0 else high
                x = twice(src, src, at)
                q = p if which == 0 else p - CA
                t, s = q // PER, q % PER
                y = twice(far_l, far_r, sz.far_row(f, t))
            fld[f, p] = jnp.where(edge, roll(y, SLOT * (PER - 1 - s)), x)

    row = lax.broadcasted_iota(jnp.int32, (PAIR, CZ), 0)
    not_top = jnp.where((row == NR - 1) | (row == PAIR - 1), 0.0, 1.0)
    start = first[0]

    def prepare(p):
        at = start + p
        live = [
            jnp.where((at >= 0) & (at + da < total), 1.0, 0.0).astype(F32) for da in range(REACH + 1)
        ]
        for k, (da, dr, dz) in enumerate(OFFSETS):
            n2, d = scales((da, dr, dz))
            c = fld[6, p]
            h = fld[7, p]
            if dr:
                c2, h2 = roll(c, -1, 0), roll(h, -1, 0)
            else:
                c2, h2 = roll(fld[6, p + da], -dz), roll(fld[7, p + da], -dz)
            m = (c + c2) * (live[da] * (0.5 * d * d / (n2 * n2)))
            stiffk[k, p] = m * not_top if dr else m
            heatk[k, p] = (h + h2) * (DILATION * 0.5 * n2 / d)

    def several(body, count):
        def run(first_plane, times):
            def one(i, c):
                for j in range(count):
                    body(first_plane + i * count + j)
                return c

            lax.fori_loop(0, times, one, 0)

        return run

    several(prepare, UNROLL)(0, (sz.ext - 1) // UNROLL)
    for m in moves:
        m.wait()
    side_breaks(
        sz,
        [
            (far_l[pl.ds(0, n), :], far_r[pl.ds(0, n), :]),
            (side_l[pl.ds(0, n), :], side_r[pl.ds(0, n), :]),
            (far_l[pl.ds(n, n), :], far_r[pl.ds(n, n), :]),
        ],
        broken, rows_ref, cols_ref, acc, edge,
    )
    energy[...] = jnp.zeros_like(energy)

    def advance(p, limit, with_energy):
        ua, ur, uz = fld[0, p], fld[1, p], fld[2, p]
        sums = {}

        def bond(o, elongation):
            k = NUMBER[o]
            q = elongation - heatk[k, p]
            g = jnp.where(broken[k, p] >= limit, 0.0, stiffk[k, p]) * q
            if with_energy:
                n2 = scales(o)[0]
                sums[n2] = sums[n2] + g * q if n2 in sums else g * q
            return g

        force_a = fa[p]
        force_z = fz[p]
        for dz in (1, 2, 3):
            g = bond((0, 0, dz), roll(uz, -dz) - uz)
            force_z = force_z + (g - roll(g, dz))
        g = bond((0, 1, 0), roll(ur, -1, 0) - ur)
        force_r = g - roll(g, 1, 0)
        for da in (1, 2):
            ua2, uz2 = fld[0, p + da], fld[2, p + da]
            g = bond((da, 0, 0), ua2 - ua)
            force_a = force_a + g
            push_a = g
            push_z = None
            for dz in (1, 2):
                gs = []
                for sign in (1, -1):
                    dua = roll(ua2, -sign * dz) - ua
                    duz = roll(uz2, -sign * dz) - uz
                    if da == dz:
                        e = dua + duz if sign > 0 else dua - duz
                    elif dz == 2:
                        e = dua + (2.0 * sign) * duz
                    else:
                        e = 2.0 * dua + duz if sign > 0 else 2.0 * dua - duz
                    gs.append(bond((da, 0, sign * dz), e))
                ma = 1.0 if da == dz else float(da)
                mz = 1.0 if da == dz else float(dz)
                own_s, own_d = gs[0] + gs[1], gs[0] - gs[1]
                plus, minus = roll(gs[0], dz), roll(gs[1], -dz)
                far_s, far_d = plus + minus, plus - minus
                if ma != 1.0:
                    own_s, far_s = ma * own_s, ma * far_s
                if mz != 1.0:
                    own_d, far_d = mz * own_d, mz * far_d
                force_a = force_a + own_s
                force_z = force_z + own_d
                push_a = push_a + far_s
                push_z = far_d if push_z is None else push_z + far_d
            fa[p + da] = fa[p + da] - push_a
            fz[p + da] = fz[p + da] - push_z
        g = bond((3, 0, 0), fld[0, p + 3] - ua)
        force_a = force_a + g
        fa[p + 3] = -g
        fz[p + 3] = jnp.zeros_like(g)
        for f, u, force in ((0, ua, force_a), (1, ur, force_r), (2, uz, force_z)):
            v = fld[3 + f, p] + DT * force
            fld[3 + f, p] = v
            fld[f, p] = u + DT * v
        if with_energy:
            e = None
            for n2, x in sums.items():
                y = x * (0.5 / math.sqrt(n2))
                e = y if e is None else e + y
            energy[p - sz.halo] = energy[p - sz.halo] + e

    counted = -(-CA // UNROLL)

    def step(s, limit):
        quiet = several(lambda p: advance(p, limit, False), UNROLL)
        quiet(REACH * s, sz.sections - s)
        several(lambda p: advance(p, limit, True), UNROLL)(halo, counted)
        quiet(halo + counted * UNROLL, sz.sections - 1 - s)
        return limit * (2.0**-12)

    fa[...] = jnp.zeros_like(fa)
    fz[...] = jnp.zeros_like(fz)
    lax.fori_loop(0, sz.sections, step, jnp.float32(1.0))

    half = lane < CZ // 2
    for c in range(3):
        for a in range(CA):
            at = pl.ds(c * CA * NR + a, NR, stride=CA)
            p = halo + a
            out_d[at, :] = jnp.where(half, fld[c, p, pl.ds(0, NR), :], fld[c, p, pl.ds(NR, NR), :])
            out_v[at, :] = jnp.where(half, fld[3 + c, p, pl.ds(0, NR), :], fld[3 + c, p, pl.ds(NR, NR), :])
    for b in range(CA // 2):
        up = energy[2 * b, pl.ds(0, NR), :] + energy[2 * b + 1, pl.ds(0, NR), :]
        dn = energy[2 * b, pl.ds(NR, NR), :] + energy[2 * b + 1, pl.ds(NR, NR), :]
        pooled[pl.ds(b * NR, NR), :] = jnp.where(half, up, dn) * (0.25 / sz.sections)
    mean = exact_dot(layers_of(), pooled[...], ((0,), (0,)))
    table = owner[...] * held + row_of[...]
    out_e[...] = exact_dot(wanted_rows(table, out_e.shape[0]), mean)


def call(body, ins, outs, scratch=(), name=None):
    arrays = [i[0] if isinstance(i, tuple) else i for i in ins]
    spaces = [i[1] if isinstance(i, tuple) else pltpu.VMEM for i in ins]
    scratch = list(scratch)
    size = sum(math.prod(s.shape) * s.dtype.itemsize for s in scratch if hasattr(s, "shape") and s.dtype in (F32, jnp.bfloat16))
    size += sum(4 * math.prod(s) for s in outs)
    size += sum(4 * math.prod(a.shape) for a, m in zip(arrays, spaces) if m is pltpu.VMEM)
    return pl.pallas_call(
        body,
        name=name,
        out_shape=[jax.ShapeDtypeStruct(s, F32) for s in outs],
        in_specs=[pl.BlockSpec(memory_space=m) for m in spaces],
        out_specs=[pl.BlockSpec(memory_space=pltpu.VMEM)] * len(outs),
        scratch_shapes=scratch,
        compiler_params=pltpu.CompilerParams(vmem_limit_bytes=min(60 << 20, size + (6 << 20))),
    )(*arrays)


def on_device(displace, velocity, stiff, thermal, owner_of, row_of, breaks):
    sz = Sizes(breaks.shape[0])
    groups = lax.axis_size("axial")
    around = lax.axis_size("azim")
    held = thermal.shape[0]
    nreq = row_of.shape[-1]
    codes = breaks.reshape(sz.code_rows, CZ)
    owner = owner_of.reshape(1, nreq)
    local = row_of.reshape(1, nreq)
    disp = displace.transpose(0, 2, 1, 3).reshape(3 * NR * CA, CZ)
    velo = velocity.transpose(0, 2, 1, 3).reshape(3 * NR * CA, CZ)
    stif = stiff.transpose(1, 0, 2).reshape(NR * CA, CZ)

    edge, side, far = (sz.edge_rows, CZ), (sz.side_rows, CZ), (sz.far_rows, CZ)
    up, down, left, right, code_f = call(
        lambda *refs: pack_first(sz, held, *refs),
        [disp, velo, stif, codes, owner, local],
        [edge, edge, side, side, (sz.code_rows, CZ)],
        name="pack_first",
    )
    to_left = [(i, (i - 1) % around) for i in range(around)]
    to_right = [(i, (i + 1) % around) for i in range(around)]
    low = lax.ppermute(up, "axial", [(i, i + 1) for i in range(groups - 1)])
    high = lax.ppermute(down, "axial", [(i + 1, i) for i in range(groups - 1)])
    side_r = lax.ppermute(left, "azim", to_left)
    side_l = lax.ppermute(right, "azim", to_right)
    spread_heat = jnp.broadcast_to(thermal[None], (groups,) + thermal.shape)
    everyone = lax.all_to_all(spread_heat, "axial", split_axis=0, concat_axis=0, tiled=True)
    everyone = everyone.reshape(groups * held, CZ)

    plane = (PAIR, CZ)
    n = sz.code_rows * CZ
    tall = NBOND * CA // 4 * NR
    work = [
        pltpu.VMEM((tall, n), jnp.bfloat16),
        pltpu.VMEM((4 * CZ, n), jnp.bfloat16),
        pltpu.VMEM((tall + 2 * PAD, 4 * CZ), F32),
    ]
    (w_own,) = call(
        lambda *refs: breaks_own(sz, *refs), [code_f], [(NBOND, CA) + plane], work, name="breaks_own"
    )
    left, right, temp = call(
        lambda *refs: pack_second(sz, held, *refs),
        [low, high, everyone, owner, local],
        [far, far, (sz.temp_rows, CZ)],
        name="pack_second",
    )
    far_r = lax.ppermute(left, "azim", to_left)
    far_l = lax.ppermute(right, "azim", to_right)
    (w_far,) = call(
        lambda *refs: breaks_far(sz, *refs), [low, high], [(NBOND, 2 * sz.halo) + plane], work, name="breaks_far"
    )
    first = (lax.axis_index("axial") * CA - sz.halo).astype(jnp.int32).reshape(1)
    planes = sz.ext + 2
    strip = -(-NBOND * PAIR // 16) * 16
    scratch = [
        pltpu.VMEM((NFIELD + 1, planes) + plane, F32),
        pltpu.VMEM((NBOND, sz.ext) + plane, F32),
        pltpu.VMEM((NBOND, sz.ext) + plane, F32),
        pltpu.VMEM((NBOND, sz.ext) + plane, F32),
        pltpu.VMEM((planes,) + plane, F32),
        pltpu.VMEM((planes,) + plane, F32),
        pltpu.VMEM((-(-CA // UNROLL) * UNROLL,) + plane, F32),
        pltpu.VMEM((CA // 2 * NR, CZ), F32),
        pltpu.VMEM((strip, 2 * n), jnp.bfloat16),
        pltpu.VMEM((CA * SLOT, 2 * n), jnp.bfloat16),
        pltpu.VMEM((strip, CA * SLOT), F32),
        pltpu.SemaphoreType.DMA((3,)),
    ]
    total = groups * CA
    out_d, out_v, out_e = call(
        lambda *refs: march(sz, total, held, *refs),
        [
            (first, pltpu.SMEM), disp, velo, stif, low, high, temp, side_l, side_r, far_l, far_r, code_f, owner, local,
            (w_own, pl.ANY), (w_far, pl.ANY),
        ],
        [disp.shape, velo.shape, (groups * held, CZ)],
        scratch,
        name="march",
    )
    parts = out_e.reshape(groups, held, CZ)
    arrived = lax.all_to_all(parts, "axial", split_axis=0, concat_axis=0, tiled=True)
    shape = (3, NR, CA, CZ)
    return (
        out_d.reshape(shape).transpose(0, 2, 1, 3),
        out_v.reshape(shape).transpose(0, 2, 1, 3),
        jnp.sum(arrived, axis=0),
    )


def solution(mesh):
    return jax.shard_map(
        on_device,
        mesh=mesh,
        in_specs=(
            P(None, "axial", None, "azim"),
            P(None, "axial", None, "azim"),
            P("axial", None, "azim"),
            P("axial", "azim"),
            P("axial", "azim", None, None),
            P("axial", "azim", None),
            P(None, "axial", "azim", None),
        ),
        out_specs=(
            P(None, "axial", None, "azim"),
            P(None, "axial", None, "azim"),
            P("axial", "azim"),
        ),
        check_vma=False,
    )
```

time: 117 us -> 112 us (0.957)
  waiting for transfers between devices: 14 us -> 1.21 us
  Pallas kernels: 57.6 us -> 65.9 us
  blocking collectives: 19.3 us -> 22.4 us
  other arithmetic: 2.65 us -> 0.61 us
  local copies, waits for them, and re-layouts: 10.5 us -> 9.33 us
    all_to_all x0 -> x2, blocking collectives: none -> 22.4 us  [the longest x1 14.1 us: on_device(): lax.all_to_all(spread_heat, 'axial', split_axis=0, concat_axis=0, tiled=T...]
    all_gather x1 -> x0, blocking collectives: 19.3 us -> none  [on_device(): everyone = lax.all_gather(thermal, 'axial', tiled=True)]
    ppermute x2 -> x4, waiting for transfers between devices: 11.5 us -> 1.21 us  [the longest x1 0.83 us: on_device(): side_l = lax.ppermute(right, 'azim', to_right)]
    pallas_call x3 -> x5, Pallas kernels: 57.6 us -> 65.9 us  [call(): pl.pallas_call(body, name=name, out_shape=[jax.ShapeDtypeStruct(s, F32) f...]
    all_to_all x1 -> x0, starting transfers between devices: 4.13 us -> none  [on_device(): lax.all_to_all(parts, 'axial', split_axis=0, concat_axis=0, tiled=True)]
    ppermute x2 -> x4, starting transfers between devices: 3.82 us -> 7.65 us  [the longest x1 3.82 us: on_device(): side_r = lax.ppermute(left, 'azim', to_left)]
    all_to_all x1 -> x0, waiting for transfers between devices: 2.53 us -> none  [on_device(): lax.all_to_all(parts, 'axial', split_axis=0, concat_axis=0, tiled=True)]
    unnamed x1 -> x0, other arithmetic: 1.32 us -> none
  transfers between devices with their start and end apart: 5 -> 6, of which waited for: 3 -> 2; matrix products, arithmetic and copies ran while one was open for 3% -> 1% of each run, Pallas kernels for 0% -> 5%
where the time goes in v1:
time: 112 us; the launch traced here: 111 us
  Pallas kernels  65.9 us (59%)
  blocking collectives  22.4 us (20%)
  starting transfers between devices  11.3 us (10%)
  local copies, waits for them, and re-layouts  9.33 us (8%)
  waiting for transfers between devices  1.21 us (1%)
    pallas_call x5, Pallas kernels, call(): pl.pallas_call(body, name=name, out_shape=[jax.ShapeDtypeStruct(s, F32) f...  65.9 us
    all_to_all x1, blocking collectives, on_device(): lax.all_to_all(spread_heat, 'axial', split_axis=0, concat_axis=0, tiled=T...  14.1 us
    unnamed x36, local copies, waits for them, and re-layouts  8.61 us
    all_to_all x1, blocking collectives, on_device(): lax.all_to_all(parts, 'axial', split_axis=0, concat_axis=0, tiled=True)  8.34 us
    ppermute x1, starting transfers between devices, on_device(): side_r = lax.ppermute(left, 'azim', to_left)  3.82 us
    ppermute x1, starting transfers between devices, on_device(): low = lax.ppermute(up, 'axial', [(i, i + 1) for i in range(groups - 1)])  2.37 us
    ppermute x1, starting transfers between devices, on_device(): far_r = lax.ppermute(left, 'azim', to_left)  2.25 us
  transfers between devices with their start and end apart: 6, of which 2 were waited for; matrix products, arithmetic and copies ran while one was open for 1% of the time, Pallas kernels for 5%

profile of v1, /device:TPU:0, one launch (start us, length us, event | category | flops | bytes accessed | tf_op | source)
XLA Modules:
  0.0 111.5 jit_solution(11186711727205646515)
XLA Ops:
  0.6 0.0 copy-start.3
  0.6 1.0 copy-done.3
  1.6 1.0 copy-done.5
  2.6 0.9 copy-done.7
  3.5 0.7 copy-done.11
  4.1 0.7 copy-done.12
  4.8 0.7 copy-done.15
  5.5 1.1 %pack_first.1 = (f32[936,128]{1,0:T(8,128)S(1)}, f32[936,128]{1,0:T(8,128)S(1)}, f32[200,128]{1,0:T(8,128)}, f32[200,128]{1,0:T(8,128)}, f32[16,128]{1,0:T(8,128)S(1)}) custom-call(f32[576,128]{1,0:T(8,128)S(1)} %bitcast.21, f32[576,128]{1,0:T(8,128)S(1)} %bitcast.23, f32[192,128]{1,0:T(8,128)S(1)} %bitcast.25, s32[16,128]{1,0:T(8,128)S(1)} %bitcast.29, ...), custom_call_target="tpu_custom_call" | custom-call | tf_op jit(solution)/shard_map/pack_first/pallas_call | solution.py:490
  6.6 2.4 %collective-permute-start = (f32[936,128]{1,0:T(8,128)S(1)}, f32[936,128]{1,0:T(8,128)S(1)}, u32[]{:S(2)}, u32[]{:S(2)}) collective-permute-start(f32[936,128]{1,0:T(8,128)S(1)} %get-tuple-element.14), channel_id=1, source_target_pairs={{0,4},{4,8},{8,12},{12,16},{16,20},{20,24},{24,28},{1,5},{5,9},{9,... | collective-permute-start | bytes 1437704 | tf_op jit(solution)/shard_map/ppermute | solution.py:523
  9.0 1.3 %collective-permute-start.1 = (f32[936,128]{1,0:T(8,128)S(1)}, f32[936,128]{1,0:T(8,128)S(1)}, u32[]{:S(2)}, u32[]{:S(2)}) collective-permute-start(f32[936,128]{1,0:T(8,128)S(1)} %get-tuple-element.15), channel_id=1, source_target_pairs={{4,0},{8,4},{12,8},{16,12},{20,16},{24,20},{28,24},{5,1},{9,5},{13... | collective-permute-start | bytes 1437704 | tf_op jit(solution)/shard_map/ppermute | solution.py:524
  10.3 0.7 broadcast_in_dim.2
  11.0 14.1 %all_to_all.10 = f32[8,24,128]{2,1,0:T(8,128)S(1)} all-to-all(f32[8,24,128]{2,1,0:T(8,128)S(1)} %broadcast_in_dim.2), channel_id=1, replica_groups=mesh['axial'=8,'azim'=4] {'axial'}, dimensions={0} | all-to-all | bytes 196608 | tf_op jit(solution)/shard_map/all_to_all | solution.py:528
  25.0 0.0 collective-permute-done.refs_0_.refs_4_
  25.0 0.0 collective-permute-done.1.refs_1_.refs_5_
  25.1 0.7 copy-done.13
  25.7 0.7 copy-done.16
  26.4 1.8 %pack_second.1 = (f32[336,128]{1,0:T(8,128)}, f32[336,128]{1,0:T(8,128)}, f32[272,128]{1,0:T(8,128)S(1)}) custom-call(f32[936,128]{1,0:T(8,128)S(1)} %collective-permute-done.refs_0_.refs_4_, f32[936,128]{1,0:T(8,128)S(1)} %collective-permute-done.1.refs_1_.refs_5_, f32[192,128]{1,0:T(8,128)S(1)} %bitcast.27, s32[1,48]{1,0:T(1,128)S(1)} %bitcast.31, ...), custom_call_target="tpu_custom_call" | custom-call | tf_op jit(solution)/shard_map/pack_second/pallas_call | solution.py:490
  28.2 0.8 copy-done
  29.0 0.6 copy-done.9
  29.6 1.6 %collective-permute-start.4 = (f32[336,128]{1,0:T(8,128)}, f32[336,128]{1,0:T(8,128)}, u32[]{:S(2)}, u32[]{:S(2)}) collective-permute-start(f32[336,128]{1,0:T(8,128)} %get-tuple-element.19), channel_id=1, source_target_pairs={{0,1},{1,2},{2,3},{3,0},{4,5},{5,6},{6,7},{7,4},{8,9},{9,10},{10,1... | collective-permute-start | bytes 516104 | tf_op jit(solution)/shard_map/ppermute | solution.py:549
  31.2 2.2 %collective-permute-start.5 = (f32[336,128]{1,0:T(8,128)}, f32[336,128]{1,0:T(8,128)}, u32[]{:S(2)}, u32[]{:S(2)}) collective-permute-start(f32[336,128]{1,0:T(8,128)} %get-tuple-element.20), channel_id=1, source_target_pairs={{0,3},{1,0},{2,1},{3,2},{4,7},{5,4},{6,5},{7,6},{8,11},{9,8},{10,9... | collective-permute-start | bytes 516104 | tf_op jit(solution)/shard_map/ppermute | solution.py:548
  33.5 0.0 collective-permute-start.2
  33.5 3.8 %collective-permute-start.3 = (f32[200,128]{1,0:T(8,128)}, f32[200,128]{1,0:T(8,128)}, u32[]{:S(2)}, u32[]{:S(2)}) collective-permute-start(f32[200,128]{1,0:T(8,128)} %get-tuple-element.18), channel_id=1, source_target_pairs={{0,3},{1,0},{2,1},{3,2},{4,7},{5,4},{6,5},{7,6},{8,11},{9,8},{10,9... | collective-permute-start | bytes 307208 | tf_op jit(solution)/shard_map/ppermute | solution.py:525
  37.3 2.1 %breaks_own.1.refs_14_ = f32[15,16,24,128]{3,2,1,0:T(8,128)S(1)} custom-call(f32[16,128]{1,0:T(8,128)S(1)} %get-tuple-element.21.refs_0_.refs_11_), custom_call_target="tpu_custom_call" | custom-call | tf_op jit(solution)/shard_map/breaks_own/pallas_call | solution.py:490
  39.4 1.0 copy-done.1
  40.4 3.6 %breaks_far.1.refs_15_ = f32[15,24,24,128]{3,2,1,0:T(8,128)S(1)} custom-call(f32[936,128]{1,0:T(8,128)S(1)} %collective-permute-done.refs_0_.refs_4_, f32[936,128]{1,0:T(8,128)S(1)} %copy-done.1), custom_call_target="tpu_custom_call" | custom-call | tf_op jit(solution)/shard_map/breaks_far/pallas_call | solution.py:490
  44.0 0.8 collective-permute-done.2.refs_7_
  44.8 0.4 collective-permute-done.3.refs_8_
  45.2 0.0 collective-permute-done.5.refs_10_
  45.2 57.3 %march.1 = (f32[576,128]{1,0:T(8,128)}, f32[576,128]{1,0:T(8,128)}, f32[192,128]{1,0:T(8,128)S(1)}) custom-call(s32[1]{0:T(128)} %bitcast.refs_0_, f32[576,128]{1,0:T(8,128)S(1)} %bitcast.22, f32[576,128]{1,0:T(8,128)S(1)} %bitcast.24, f32[192,128]{1,0:T(8,128)S(1)} %bitcast.26, f32[936,128]{1,0:T(8,128)S(1)} %collective-permute-done.refs_0_.refs_4_, ...), custom_call_target="tpu_custom_call" | custom-call | tf_op jit(solution)/shard_map/march/pallas_call | solution.py:490
  102.5 8.3 %all_to_all.11 = f32[8,24,128]{2,1,0:T(8,128)S(1)} all-to-all(f32[8,24,128]{2,1,0:T(8,128)S(1)} %bitcast.28), channel_id=1, replica_groups=mesh['axial'=8,'azim'=4] {'axial'}, dimensions={0} | all-to-all | bytes 196608 | tf_op jit(solution)/shard_map/all_to_all | solution.py:582
  110.9 0.6 reduce_sum.9
  (25 shorter events, 0.0 us)
Async XLA Ops:
  0.6 1.0 copy-start.3
  1.6 1.0 copy-start.5
  2.6 0.9 copy-start.7
  3.5 0.7 copy-start.11
  4.1 0.7 copy-start.12
  4.8 0.7 copy-start.15
  6.6 18.5 %collective-permute-start = (f32[936,128]{1,0:T(8,128)S(1)}, f32[936,128]{1,0:T(8,128)S(1)}, u32[]{:S(2)}, u32[]{:S(2)}) collective-permute-start(f32[936,128]{1,0:T(8,128)S(1)} %get-tuple-element.14), channel_id=1, source_target_pairs={{0,4},{4,8},{8,12},{12,16},{16,20},{20,24},{24,28},{1,5},{5,9},{9,... | collective-permute-start | bytes 1437704 | tf_op jit(solution)/shard_map/ppermute | solution.py:523
  9.0 16.1 %collective-permute-start.1 = (f32[936,128]{1,0:T(8,128)S(1)}, f32[936,128]{1,0:T(8,128)S(1)}, u32[]{:S(2)}, u32[]{:S(2)}) collective-permute-start(f32[936,128]{1,0:T(8,128)S(1)} %get-tuple-element.15), channel_id=1, source_target_pairs={{4,0},{8,4},{12,8},{16,12},{20,16},{24,20},{28,24},{5,1},{9,5},{13... | collective-permute-start | bytes 1437704 | tf_op jit(solution)/shard_map/ppermute | solution.py:524
  25.0 0.7 copy-start.13
  25.7 0.7 copy-start.16
  28.2 0.8 copy-start
  29.0 0.6 copy-start.9
  29.6 15.5 %copy-start.8 = (f32[16,12,128]{2,0,1:T(8,128)S(1)}, f32[16,12,128]{2,0,1:T(8,128)}, u32[]{:S(2)}) copy-start(f32[16,12,128]{2,0,1:T(8,128)} %param.9) | copy-start | bytes 294916
  29.6 15.5 %copy-start.14 = (s32[1,1,48,1]{2,3,1,0:T(1,128)S(1)}, s32[1,1,48,1]{2,3,1,0:T(1,128)}, u32[]{:S(2)}) copy-start(s32[1,1,48,1]{2,3,1,0:T(1,128)} %param.11) | copy-start | bytes 580
  29.6 15.6 %copy-start.17 = (s32[1,1,48]{2,1,0:T(1,128)S(1)}, s32[1,1,48]{2,1,0:T(1,128)}, u32[]{:S(2)}) copy-start(s32[1,1,48]{2,1,0:T(1,128)} %param.12) | copy-start | bytes 580
  29.6 15.5 %collective-permute-start.4 = (f32[336,128]{1,0:T(8,128)}, f32[336,128]{1,0:T(8,128)}, u32[]{:S(2)}, u32[]{:S(2)}) collective-permute-start(f32[336,128]{1,0:T(8,128)} %get-tuple-element.19), channel_id=1, source_target_pairs={{0,1},{1,2},{2,3},{3,0},{4,5},{5,6},{6,7},{7,4},{8,9},{9,10},{10,1... | collective-permute-start | bytes 516104 | tf_op jit(solution)/shard_map/ppermute | solution.py:549
  31.2 14.0 %collective-permute-start.5 = (f32[336,128]{1,0:T(8,128)}, f32[336,128]{1,0:T(8,128)}, u32[]{:S(2)}, u32[]{:S(2)}) collective-permute-start(f32[336,128]{1,0:T(8,128)} %get-tuple-element.20), channel_id=1, source_target_pairs={{0,3},{1,0},{2,1},{3,2},{4,7},{5,4},{6,5},{7,6},{8,11},{9,8},{10,9... | collective-permute-start | bytes 516104 | tf_op jit(solution)/shard_map/ppermute | solution.py:548
  33.5 11.3 %collective-permute-start.2 = (f32[200,128]{1,0:T(8,128)}, f32[200,128]{1,0:T(8,128)}, u32[]{:S(2)}, u32[]{:S(2)}) collective-permute-start(f32[200,128]{1,0:T(8,128)} %get-tuple-element.17), channel_id=1, source_target_pairs={{0,1},{1,2},{2,3},{3,0},{4,5},{5,6},{6,7},{7,4},{8,9},{9,10},{10,1... | collective-permute-start | bytes 307208 | tf_op jit(solution)/shard_map/ppermute | solution.py:526
  33.5 11.7 %collective-permute-start.3 = (f32[200,128]{1,0:T(8,128)}, f32[200,128]{1,0:T(8,128)}, u32[]{:S(2)}, u32[]{:S(2)}) collective-permute-start(f32[200,128]{1,0:T(8,128)} %get-tuple-element.18), channel_id=1, source_target_pairs={{0,3},{1,0},{2,1},{3,2},{4,7},{5,4},{6,5},{7,6},{8,11},{9,8},{10,9... | collective-permute-start | bytes 307208 | tf_op jit(solution)/shard_map/ppermute | solution.py:525
  39.4 1.0 copy-start.1
  40.4 4.8 %copy-start.2 = (f32[936,128]{1,0:T(8,128)S(1)}, f32[936,128]{1,0:T(8,128)}, u32[]{:S(2)}) copy-start(f32[936,128]{1,0:T(8,128)} %copy-done) | copy-start | bytes 1437700
  40.4 4.8 %copy-start.4 = (f32[3,16,12,128]{3,1,2,0:T(8,128)S(1)}, f32[3,16,12,128]{3,1,2,0:T(8,128)}, u32[]{:S(2)}) copy-start(f32[3,16,12,128]{3,1,2,0:T(8,128)} %param.7) | copy-start | bytes 884740
  40.4 4.8 %copy-start.6 = (f32[3,16,12,128]{3,1,2,0:T(8,128)S(1)}, f32[3,16,12,128]{3,1,2,0:T(8,128)}, u32[]{:S(2)}) copy-start(f32[3,16,12,128]{3,1,2,0:T(8,128)} %param.8) | copy-start | bytes 884740
  40.4 4.8 %copy-start.10 = (f32[272,128]{1,0:T(8,128)S(1)}, f32[272,128]{1,0:T(8,128)}, u32[]{:S(2)}) copy-start(f32[272,128]{1,0:T(8,128)} %copy-done.9) | copy-start | bytes 417796

commit v2 on v1

--- a/solution.py
+++ b/solution.py
@@ -72,7 +72,7 @@
         self.side_rows = PAD + NFIELD * self.own_tiles * NR + PAD
         self.side_rows = -(-self.side_rows // 8) * 8
         self.far_tiles = 2 * self.halo // PER
-        self.far_pad = 2 * self.code_rows
+        self.far_pad = PAD
         self.heat_tiles = -(-self.ext // 2 // PER)
         self.far_rows = self.far_pad + (NFIELD * self.far_tiles + self.heat_tiles) * NR + PAD
         self.far_rows = -(-self.far_rows // 8) * 8
@@ -148,7 +148,7 @@
     right[pl.ds(row, NR), :] = to_right
 
 
-def pack_first(sz, held, disp, velo, stiff, codes, owner, row_of, up, down, left, right, code_f):
+def pack_first(sz, share, disp, velo, stiff, codes, owner, row_of, up, down, left, right, code_f):
     refs = (disp, velo, stiff)
     for f in range(NFIELD):
         for p in range(sz.halo):
@@ -163,7 +163,7 @@
             pack_tiles(sz, planes, left, right, sz.side_row(f, t))
     c = codes[...].astype(F32)
     code_f[...] = c
-    table = (owner[...] * held + row_of[...]).astype(F32)
+    table = (owner[...] * share + row_of[...]).astype(F32)
     blank = jnp.zeros((PAD, CZ), F32)
     for out in (up, down, left, right):
         out[pl.ds(out.shape[0] - PAD, PAD), :] = blank
@@ -172,7 +172,7 @@
         out[pl.ds(sz.tab_at, 1), pl.ds(0, table.shape[1])] = table
 
 
-def pack_second(sz, held, low, high, thermal, owner, row_of, left, right, temp):
+def pack_second(sz, held, share, low, high, thermal, owner, row_of, left, right, temp):
     n = owner.shape[1]
     rows = thermal.shape[0]
     heat = thermal[...]
@@ -183,7 +183,7 @@
     at = PAD
     for which in range(3):
         if which == 1:
-            table = owner[...] * held + row_of[...]
+            table = owner[...] * share + row_of[...]
         else:
             src = low if which == 0 else high
             table = src[pl.ds(sz.tab_at, 1), :][:, 0:n].astype(jnp.int32)
@@ -208,8 +208,17 @@
         pack_tiles(sz, planes, left, right, sz.far_row(NFIELD, t))
     for out in (left, right):
         out[pl.ds(sz.far_rows - PAD, PAD), :] = blank
-        out[pl.ds(0, sz.code_rows), :] = low[pl.ds(0, sz.code_rows), :]
-        out[pl.ds(sz.code_rows, sz.code_rows), :] = high[pl.ds(0, sz.code_rows), :]
+        out[pl.ds(0, PAD), :] = blank
+
+
+def relay(groups, thermal, side_l, side_r, box):
+    rows = thermal.shape[0]
+    n = side_l.shape[0]
+    for g in range(groups):
+        at = g * (rows + 2 * n)
+        box[pl.ds(at, rows), :] = thermal[...]
+        box[pl.ds(at + rows, n), :] = side_l[...]
+        box[pl.ds(at + rows + n, n), :] = side_r[...]
 
 
 def decode(codes):
@@ -234,9 +243,8 @@
             )
 
 
-def read_breaks(sz, codes, parts, out, rows_ref, cols_ref, acc):
-    at = 0
-    for src, lo_group, groups, planes in parts:
+def read_breaks(sz, parts, out, rows_ref, cols_ref, acc):
+    for src, lo_group, groups, first, count, at in parts:
         k, a, r, z = decode(src)
         group = jnp.floor(a * 0.25)
         per_k = groups * NR
@@ -247,32 +255,41 @@
         spread(cols_ref, (a - 4 * group) * CZ + z, 4 * CZ, CZ * 2, weigh=True)
         acc[pl.ds(PAD, rows), :] = dot_nt(rows_ref[pl.ds(0, rows), :], cols_ref[...])
         for b in range(NBOND):
-            for i, plane in enumerate(planes):
+            for i in range(count):
+                plane = first + i
                 row = PAD + b * per_k + (plane // 4 - lo_group) * NR
                 lanes = pl.ds(plane % 4 * CZ, CZ)
                 out[b, at + i] = jnp.where(
                     is_top(), acc[pl.ds(row, PAIR), lanes], acc[pl.ds(row - NR, PAIR), lanes]
                 )
-        at += len(planes)
 
 
 def breaks_own(sz, codes, out, rows_ref, cols_ref, acc):
     acc[pl.ds(0, PAD), :] = jnp.zeros((PAD, 4 * CZ), F32)
-    parts = [(codes[...], 0, CA // 4, list(range(CA)))]
-    read_breaks(sz, None, parts, out, rows_ref, cols_ref, acc)
-
-
-def breaks_far(sz, low, high, out, rows_ref, cols_ref, acc):
+    read_breaks(sz, [(codes[...], 0, CA // 4, 0, CA, 0)], out, rows_ref, cols_ref, acc)
+
+
+def breaks_all(
+    sz, at_lo, at_hi, own, low, high, side_l, side_r, box, out, rows_ref, cols_ref, acc, rows_s, cols_s, acc_s
+):
+    n, halo = sz.code_rows, sz.halo
     acc[pl.ds(0, PAD), :] = jnp.zeros((PAD, 4 * CZ), F32)
-    n = sz.code_rows
     parts = [
-        (low[pl.ds(0, n), :], (CA - sz.halo) // 4, sz.halo // 4, list(range(CA - sz.halo, CA))),
-        (high[pl.ds(0, n), :], 0, sz.halo // 4, list(range(sz.halo))),
+        (low[...], (CA - halo) // 4, halo // 4, CA - halo, halo, 0),
+        (high[...], 0, halo // 4, 0, halo, halo + CA),
     ]
-    read_breaks(sz, None, parts, out, rows_ref, cols_ref, acc)
-
-
-def side_breaks(sz, sources, broken, rows_ref, cols_ref, acc, edge):
+    read_breaks(sz, parts, out, rows_ref, cols_ref, acc)
+    wide = lanes_of((PAIR, CZ))
+    edge = (is_top() & (wide >= CZ - SLOT)) | (~is_top() & (wide < SLOT))
+    sources = [
+        (box[pl.ds(at_lo, n), :], box[pl.ds(at_lo + n, n), :]),
+        (side_l[...], side_r[...]),
+        (box[pl.ds(at_hi, n), :], box[pl.ds(at_hi + n, n), :]),
+    ]
+    side_breaks(sz, sources, own, out, rows_s, cols_s, acc_s, edge)
+
+
+def side_breaks(sz, sources, own, out, rows_ref, cols_ref, acc, edge):
     n = sz.code_rows * CZ
     rows = -(-NBOND * PAIR // 16) * 16
     for which, (left, right) in enumerate(sources):
@@ -292,27 +309,20 @@
             a = sz.source(p)[1]
             for b in range(NBOND):
                 x = acc[pl.ds(b * PAIR, PAIR), pl.ds(a // PER * CZ, CZ)]
-                broken[b, p] = jnp.where(edge, roll(x, SLOT * (PER - 1 - a % PER)), broken[b, p])
+                old = own[b, a] if which == 1 else out[b, p]
+                out[b, p] = jnp.where(edge, roll(x, SLOT * (PER - 1 - a % PER)), old)
 
 
 def march(
-    sz, total, held, first, disp, velo, stiff, low, high, temp, side_l, side_r, far_l, far_r, codes, owner, row_of,
-    w_own, w_far, out_d, out_v, out_e, fld, stiffk, heatk, broken, fa, fz, energy, pooled, rows_ref, cols_ref, acc, sems,
+    sz, total, held, place, disp, velo, stiff, low, high, temp, side_l, side_r, far_l, far_r, owner, row_of,
+    broken, out_d, out_v, out_e, fld, stiffk, heatk, bonds, forces, wait_a, wait_b, energy, pooled,
 ):
     refs = (disp, velo, stiff)
     halo = sz.halo
-    moves = [
-        pltpu.make_async_copy(w_own, broken.at[:, pl.ds(halo, CA)], sems.at[0]),
-        pltpu.make_async_copy(w_far.at[:, pl.ds(0, halo)], broken.at[:, pl.ds(0, halo)], sems.at[1]),
-        pltpu.make_async_copy(w_far.at[:, pl.ds(halo, halo)], broken.at[:, pl.ds(halo + CA, halo)], sems.at[2]),
-    ]
-    for m in moves:
-        m.start()
     lane = lanes_of()
     wide = lanes_of((PAIR, CZ))
     top = is_top()
     edge = (top & (wide >= CZ - SLOT)) | (~top & (wide < SLOT))
-    n = sz.code_rows
     for f in range(NFIELD + 1):
         for p in range(sz.ext):
             which, a = sz.source(p)
@@ -339,129 +349,168 @@
 
     row = lax.broadcasted_iota(jnp.int32, (PAIR, CZ), 0)
     not_top = jnp.where((row == NR - 1) | (row == PAIR - 1), 0.0, 1.0)
-    start = first[0]
+    start = place[0] * CA - halo
+
+    def turned(cache, f, p, i, dz):
+        key = f, i, dz
+        if key not in cache:
+            x = turned(cache, f, p, i, 0) if dz else fld[f, p + i]
+            cache[key] = roll(x, -dz)
+        return cache[key]
 
     def prepare(p):
-        at = start + p
-        live = [
-            jnp.where((at >= 0) & (at + da < total), 1.0, 0.0).astype(F32) for da in range(REACH + 1)
-        ]
-        for k, (da, dr, dz) in enumerate(OFFSETS):
-            n2, d = scales((da, dr, dz))
-            c = fld[6, p]
-            h = fld[7, p]
-            if dr:
-                c2, h2 = roll(c, -1, 0), roll(h, -1, 0)
-            else:
-                c2, h2 = roll(fld[6, p + da], -dz), roll(fld[7, p + da], -dz)
-            m = (c + c2) * (live[da] * (0.5 * d * d / (n2 * n2)))
-            stiffk[k, p] = m * not_top if dr else m
-            heatk[k, p] = (h + h2) * (DILATION * 0.5 * n2 / d)
-
-    def several(body, count):
-        def run(first_plane, times):
-            def one(i, c):
-                for j in range(count):
-                    body(first_plane + i * count + j)
-                return c
-
-            lax.fori_loop(0, times, one, 0)
+        cache = {}
+        get = lambda f, i, dz=0: turned(cache, f, p, i, dz)
+        for i in range(UNROLL):
+            at = start + p + i
+            live = [
+                jnp.where((at >= 0) & (at + da < total), 1.0, 0.0).astype(F32) for da in range(REACH + 1)
+            ]
+            c, h = get(6, i), get(7, i)
+            for k, (da, dr, dz) in enumerate(OFFSETS):
+                n2, d = scales((da, dr, dz))
+                if dr:
+                    c2, h2 = roll(c, -1, 0), roll(h, -1, 0)
+                else:
+                    c2, h2 = get(6, i + da, dz), get(7, i + da, dz)
+                m = (c + c2) * (live[da] * (0.5 * d * d / (n2 * n2)))
+                stiffk[k, p + i] = m * not_top if dr else m
+                heatk[k, p + i] = (h + h2) * (DILATION * 0.5 * n2 / d)
+
+    def several(body, first_plane, times):
+        def one(i, c):
+            body(first_plane + i * UNROLL)
+            return c
+
+        lax.fori_loop(0, times, one, 0)
+
+    several(prepare, 0, (sz.ext - 1) // UNROLL)
+    energy[...] = jnp.zeros_like(energy)
+
+    span = range(UNROLL)
+
+    def pull(p, limit, with_energy):
+        cache = {}
+        get = lambda f, i, dz=0: turned(cache, f, p, i, dz)
+        fa_at = {i: wait_a[i] for i in range(REACH)}
+        fz_at = {}
+        sums = [{} for _ in span]
+        keep = []
+
+        def add(to, i, x):
+            to[i] = to[i] + x if i in to else x
+
+        def bond(i, o, elongation):
+            k = NUMBER[o]
+            q = elongation - heatk[k, p + i]
+            g = jnp.where(broken[k, p + i] >= limit, 0.0, stiffk[k, p + i]) * q
+            if with_energy:
+                add(sums[i], scales(o)[0], g * q)
+            if o[2]:
+                keep.append((bonds, (k, i), g))
+            return g
+
+        for i in span:
+            ua, ur, uz = get(0, i), get(1, i), get(2, i)
+            for dz in (1, 2, 3):
+                add(fz_at, i, bond(i, (0, 0, dz), get(2, i, dz) - uz))
+            g = bond(i, (0, 1, 0), roll(ur, -1, 0) - ur)
+            keep.append((forces, (1, i), g - roll(g, 1, 0)))
+            for da in (1, 2):
+                j = i + da
+                g = bond(i, (da, 0, 0), get(0, j) - ua)
+                add(fa_at, i, g)
+                add(fa_at, j, -g)
+                for dz in (1, 2):
+                    gs = []
+                    for sign in (1, -1):
+                        dua = get(0, j, sign * dz) - ua
+                        duz = get(2, j, sign * dz) - uz
+                        if da == dz:
+                            e = dua + duz if sign > 0 else dua - duz
+                        elif dz == 2:
+                            e = dua + (2.0 * sign) * duz
+                        else:
+                            e = 2.0 * dua + duz if sign > 0 else 2.0 * dua - duz
+                        gs.append(bond(i, (da, 0, sign * dz), e))
+                    own_s, own_d = gs[0] + gs[1], gs[0] - gs[1]
+                    add(fa_at, i, own_s if da in (1, dz) else float(da) * own_s)
+                    add(fz_at, i, own_d if dz in (1, da) else float(dz) * own_d)
+            g = bond(i, (3, 0, 0), get(0, i + 3) - ua)
+            add(fa_at, i, g)
+            add(fa_at, i + 3, -g)
+            keep.append((forces, (0, i), fa_at[i]))
+            keep.append((forces, (2, i), fz_at[i]))
+        keep += [(wait_a, (i,), fa_at[i + UNROLL]) for i in range(REACH)]
+        if with_energy:
+            for i in span:
+                e = None
+                for n2, x in sums[i].items():
+                    y = x * (0.5 / math.sqrt(n2))
+                    e = y if e is None else e + y
+                keep.append((energy, (p + i - halo,), energy[p + i - halo] + e))
+        return keep
+
+    def push(p):
+        fa_at = {i: wait_b[0, i] for i in range(REACH - 1)}
+        fz_at = {i: wait_b[1, i] for i in range(REACH - 1)}
+        keep = []
+
+        def add(to, i, x):
+            to[i] = to[i] + x if i in to else x
+
+        for i in span:
+            for da in (0, 1, 2):
+                j = i + da
+                for dz in (1, 2) if da else (1, 2, 3):
+                    plus = roll(bonds[NUMBER[da, 0, dz], i], dz)
+                    if da == 0:
+                        add(fz_at, j, plus)
+                        continue
+                    minus = roll(bonds[NUMBER[da, 0, -dz], i], -dz)
+                    both, gap = plus + minus, plus - minus
+                    add(fa_at, j, both if da in (1, dz) else float(da) * both)
+                    add(fz_at, j, gap if dz in (1, da) else float(dz) * gap)
+            for f, force in (
+                (0, forces[0, i] - fa_at[i]),
+                (1, forces[1, i]),
+                (2, forces[2, i] - fz_at[i]),
+            ):
+                v = fld[3 + f, p + i] + DT * force
+                keep.append((fld, (3 + f, p + i), v))
+                keep.append((fld, (f, p + i), fld[f, p + i] + DT * v))
+        for i in range(REACH - 1):
+            keep.append((wait_b, (0, i), fa_at[UNROLL + i]))
+            keep.append((wait_b, (1, i), fz_at[UNROLL + i]))
+        return keep
+
+    def store(keep):
+        for ref, index, value in keep:
+            ref[index] = value
+
+    def both_halves(limit, with_energy):
+        def run(p):
+            late = push(p - UNROLL)
+            fresh = pull(p, limit, with_energy)
+            store(fresh)
+            store(late)
 
         return run
 
-    several(prepare, UNROLL)(0, (sz.ext - 1) // UNROLL)
-    for m in moves:
-        m.wait()
-    side_breaks(
-        sz,
-        [
-            (far_l[pl.ds(0, n), :], far_r[pl.ds(0, n), :]),
-            (side_l[pl.ds(0, n), :], side_r[pl.ds(0, n), :]),
-            (far_l[pl.ds(n, n), :], far_r[pl.ds(n, n), :]),
-        ],
-        broken, rows_ref, cols_ref, acc, edge,
-    )
-    energy[...] = jnp.zeros_like(energy)
-
-    def advance(p, limit, with_energy):
-        ua, ur, uz = fld[0, p], fld[1, p], fld[2, p]
-        sums = {}
-
-        def bond(o, elongation):
-            k = NUMBER[o]
-            q = elongation - heatk[k, p]
-            g = jnp.where(broken[k, p] >= limit, 0.0, stiffk[k, p]) * q
-            if with_energy:
-                n2 = scales(o)[0]
-                sums[n2] = sums[n2] + g * q if n2 in sums else g * q
-            return g
-
-        force_a = fa[p]
-        force_z = fz[p]
-        for dz in (1, 2, 3):
-            g = bond((0, 0, dz), roll(uz, -dz) - uz)
-            force_z = force_z + (g - roll(g, dz))
-        g = bond((0, 1, 0), roll(ur, -1, 0) - ur)
-        force_r = g - roll(g, 1, 0)
-        for da in (1, 2):
-            ua2, uz2 = fld[0, p + da], fld[2, p + da]
-            g = bond((da, 0, 0), ua2 - ua)
-            force_a = force_a + g
-            push_a = g
-            push_z = None
-            for dz in (1, 2):
-                gs = []
-                for sign in (1, -1):
-                    dua = roll(ua2, -sign * dz) - ua
-                    duz = roll(uz2, -sign * dz) - uz
-                    if da == dz:
-                        e = dua + duz if sign > 0 else dua - duz
-                    elif dz == 2:
-                        e = dua + (2.0 * sign) * duz
-                    else:
-                        e = 2.0 * dua + duz if sign > 0 else 2.0 * dua - duz
-                    gs.append(bond((da, 0, sign * dz), e))
-                ma = 1.0 if da == dz else float(da)
-                mz = 1.0 if da == dz else float(dz)
-                own_s, own_d = gs[0] + gs[1], gs[0] - gs[1]
-                plus, minus = roll(gs[0], dz), roll(gs[1], -dz)
-                far_s, far_d = plus + minus, plus - minus
-                if ma != 1.0:
-                    own_s, far_s = ma * own_s, ma * far_s
-                if mz != 1.0:
-                    own_d, far_d = mz * own_d, mz * far_d
-                force_a = force_a + own_s
-                force_z = force_z + own_d
-                push_a = push_a + far_s
-                push_z = far_d if push_z is None else push_z + far_d
-            fa[p + da] = fa[p + da] - push_a
-            fz[p + da] = fz[p + da] - push_z
-        g = bond((3, 0, 0), fld[0, p + 3] - ua)
-        force_a = force_a + g
-        fa[p + 3] = -g
-        fz[p + 3] = jnp.zeros_like(g)
-        for f, u, force in ((0, ua, force_a), (1, ur, force_r), (2, uz, force_z)):
-            v = fld[3 + f, p] + DT * force
-            fld[3 + f, p] = v
-            fld[f, p] = u + DT * v
-        if with_energy:
-            e = None
-            for n2, x in sums.items():
-                y = x * (0.5 / math.sqrt(n2))
-                e = y if e is None else e + y
-            energy[p - sz.halo] = energy[p - sz.halo] + e
-
     counted = -(-CA // UNROLL)
 
     def step(s, limit):
-        quiet = several(lambda p: advance(p, limit, False), UNROLL)
-        quiet(REACH * s, sz.sections - s)
-        several(lambda p: advance(p, limit, True), UNROLL)(halo, counted)
-        quiet(halo + counted * UNROLL, sz.sections - 1 - s)
+        first_plane = REACH * s
+        store(pull(first_plane, limit, False))
+        quiet = both_halves(limit, False)
+        several(quiet, first_plane + UNROLL, sz.sections - 1 - s)
+        several(both_halves(limit, True), halo, counted)
+        several(quiet, halo + counted * UNROLL, sz.sections - 1 - s)
+        store(push(halo + (counted + sz.sections - 2 - s) * UNROLL))
         return limit * (2.0**-12)
 
-    fa[...] = jnp.zeros_like(fa)
-    fz[...] = jnp.zeros_like(fz)
+    for ref in (wait_a, wait_b):
+        ref[...] = jnp.zeros_like(ref)
     lax.fori_loop(0, sz.sections, step, jnp.float32(1.0))
 
     half = lane < CZ // 2
@@ -481,19 +530,44 @@
 
 
 def call(body, ins, outs, scratch=(), name=None):
-    arrays = [i[0] if isinstance(i, tuple) else i for i in ins]
-    spaces = [i[1] if isinstance(i, tuple) else pltpu.VMEM for i in ins]
-    scratch = list(scratch)
-    size = sum(math.prod(s.shape) * s.dtype.itemsize for s in scratch if hasattr(s, "shape") and s.dtype in (F32, jnp.bfloat16))
+    arrays, spaces, parts = [], [], []
+    for i in ins:
+        x, how = i if isinstance(i, tuple) else (i, i.shape[0])
+        staged = isinstance(how, int)
+        arrays.append(pltpu.with_memory_space_constraint(x, pltpu.HBM) if staged else x)
+        spaces.append(pltpu.HBM if staged else how)
+        parts.append(how if staged else None)
+    staged = [i for i, m in enumerate(parts) if m is not None]
+    buffers = [pltpu.VMEM((parts[i],) + arrays[i].shape[1:], arrays[i].dtype) for i in staged]
+
+    def kernel(*refs):
+        refs = list(refs)
+        sems = refs.pop()
+        held = refs[len(refs) - len(staged) :]
+        refs = refs[: len(refs) - len(staged)]
+        copies = [
+            pltpu.make_async_copy(refs[i].at[pl.ds(0, parts[i])], held[j], sems.at[j])
+            for j, i in enumerate(staged)
+        ]
+        for c in copies:
+            c.start()
+        for j, i in enumerate(staged):
+            refs[i] = held[j]
+        for c in copies:
+            c.wait()
+        body(*refs)
+
+    every = list(scratch) + buffers
+    size = sum(math.prod(b.shape) * jnp.dtype(b.dtype).itemsize for b in every)
     size += sum(4 * math.prod(s) for s in outs)
     size += sum(4 * math.prod(a.shape) for a, m in zip(arrays, spaces) if m is pltpu.VMEM)
     return pl.pallas_call(
-        body,
+        kernel,
         name=name,
         out_shape=[jax.ShapeDtypeStruct(s, F32) for s in outs],
         in_specs=[pl.BlockSpec(memory_space=m) for m in spaces],
         out_specs=[pl.BlockSpec(memory_space=pltpu.VMEM)] * len(outs),
-        scratch_shapes=scratch,
+        scratch_shapes=every + [pltpu.SemaphoreType.DMA((max(1, len(staged)),))],
         compiler_params=pltpu.CompilerParams(vmem_limit_bytes=min(60 << 20, size + (6 << 20))),
     )(*arrays)
 
@@ -513,66 +587,91 @@
 
     edge, side, far = (sz.edge_rows, CZ), (sz.side_rows, CZ), (sz.far_rows, CZ)
     up, down, left, right, code_f = call(
-        lambda *refs: pack_first(sz, held, *refs),
+        lambda *refs: pack_first(sz, held + 2 * sz.code_rows, *refs),
         [disp, velo, stif, codes, owner, local],
         [edge, edge, side, side, (sz.code_rows, CZ)],
         name="pack_first",
     )
     to_left = [(i, (i - 1) % around) for i in range(around)]
     to_right = [(i, (i + 1) % around) for i in range(around)]
-    low = lax.ppermute(up, "axial", [(i, i + 1) for i in range(groups - 1)])
-    high = lax.ppermute(down, "axial", [(i + 1, i) for i in range(groups - 1)])
+    upward = [(i, i + 1) for i in range(groups - 1)]
+    downward = [(i + 1, i) for i in range(groups - 1)]
+    low = lax.ppermute(up, "axial", upward)
+    high = lax.ppermute(down, "axial", downward)
     side_r = lax.ppermute(left, "azim", to_left)
     side_l = lax.ppermute(right, "azim", to_right)
-    spread_heat = jnp.broadcast_to(thermal[None], (groups,) + thermal.shape)
-    everyone = lax.all_to_all(spread_heat, "axial", split_axis=0, concat_axis=0, tiled=True)
-    everyone = everyone.reshape(groups * held, CZ)
+    n = sz.code_rows
+    share = held + 2 * n
+    (out_box,) = call(
+        lambda *refs: relay(groups, *refs),
+        [thermal, (side_l, n), (side_r, n)],
+        [(groups * share, CZ)],
+        name="relay",
+    )
+    box = lax.all_to_all(out_box.reshape(groups, share, CZ), "axial", split_axis=0, concat_axis=0, tiled=True)
 
     plane = (PAIR, CZ)
-    n = sz.code_rows * CZ
+    lanes = sz.code_rows * CZ
     tall = NBOND * CA // 4 * NR
     work = [
-        pltpu.VMEM((tall, n), jnp.bfloat16),
-        pltpu.VMEM((4 * CZ, n), jnp.bfloat16),
+        pltpu.VMEM((tall, lanes), jnp.bfloat16),
+        pltpu.VMEM((4 * CZ, lanes), jnp.bfloat16),
         pltpu.VMEM((tall + 2 * PAD, 4 * CZ), F32),
     ]
     (w_own,) = call(
         lambda *refs: breaks_own(sz, *refs), [code_f], [(NBOND, CA) + plane], work, name="breaks_own"
     )
+    low, high, side_l, side_r, box, w_own = lax.optimization_barrier(
+        (low, high, side_l, side_r, box, w_own)
+    )
     left, right, temp = call(
-        lambda *refs: pack_second(sz, held, *refs),
-        [low, high, everyone, owner, local],
+        lambda *refs: pack_second(sz, held, share, *refs),
+        [low, high, box.reshape(groups * share, CZ), owner, local],
         [far, far, (sz.temp_rows, CZ)],
         name="pack_second",
     )
     far_r = lax.ppermute(left, "azim", to_left)
     far_l = lax.ppermute(right, "azim", to_right)
-    (w_far,) = call(
-        lambda *refs: breaks_far(sz, *refs), [low, high], [(NBOND, 2 * sz.halo) + plane], work, name="breaks_far"
-    )
-    first = (lax.axis_index("axial") * CA - sz.halo).astype(jnp.int32).reshape(1)
+    strip = -(-NBOND * PAIR // 16) * 16
+    place = lax.axis_index("axial").astype(jnp.int32).reshape(1)
+
+    def all_breaks(place, *refs):
+        x = place[0]
+        rows = [
+            pl.multiple_of(jnp.clip(x + d, 0, groups - 1) * share + held, 8) for d in (-1, 1)
+        ]
+        breaks_all(sz, *rows, *refs)
+
+    (broken,) = call(
+        all_breaks,
+        [(place, pltpu.SMEM), (w_own, pltpu.VMEM), (low, n), (high, n), (side_l, n), (side_r, n), box.reshape(groups * share, CZ)],
+        [(NBOND, sz.ext) + plane],
+        work
+        + [
+            pltpu.VMEM((strip, 2 * lanes), jnp.bfloat16),
+            pltpu.VMEM((CA * SLOT, 2 * lanes), jnp.bfloat16),
+            pltpu.VMEM((strip, CA * SLOT), F32),
+        ],
+        name="breaks_all",
+    )
     planes = sz.ext + 2
-    strip = -(-NBOND * PAIR // 16) * 16
     scratch = [
         pltpu.VMEM((NFIELD + 1, planes) + plane, F32),
         pltpu.VMEM((NBOND, sz.ext) + plane, F32),
         pltpu.VMEM((NBOND, sz.ext) + plane, F32),
-        pltpu.VMEM((NBOND, sz.ext) + plane, F32),
-        pltpu.VMEM((planes,) + plane, F32),
-        pltpu.VMEM((planes,) + plane, F32),
+        pltpu.VMEM((NBOND, UNROLL) + plane, F32),
+        pltpu.VMEM((3, UNROLL) + plane, F32),
+        pltpu.VMEM((REACH,) + plane, F32),
+        pltpu.VMEM((2, REACH - 1) + plane, F32),
         pltpu.VMEM((-(-CA // UNROLL) * UNROLL,) + plane, F32),
         pltpu.VMEM((CA // 2 * NR, CZ), F32),
-        pltpu.VMEM((strip, 2 * n), jnp.bfloat16),
-        pltpu.VMEM((CA * SLOT, 2 * n), jnp.bfloat16),
-        pltpu.VMEM((strip, CA * SLOT), F32),
-        pltpu.SemaphoreType.DMA((3,)),
     ]
     total = groups * CA
     out_d, out_v, out_e = call(
         lambda *refs: march(sz, total, held, *refs),
         [
-            (first, pltpu.SMEM), disp, velo, stif, low, high, temp, side_l, side_r, far_l, far_r, code_f, owner, local,
-            (w_own, pl.ANY), (w_far, pl.ANY),
+            (place, pltpu.SMEM), disp, velo, stif, low, high, temp, side_l, side_r, far_l, far_r, owner, local,
+            (broken, pltpu.VMEM),
         ],
         [disp.shape, velo.shape, (groups * held, CZ)],
         scratch,

time: 112 us -> 78.7 us (0.70)
  Pallas kernels: 65.9 us -> 40 us
  blocking collectives: 22.4 us -> 7.58 us
  waiting for transfers between devices: 1.21 us -> 9.66 us
  local copies, waits for them, and re-layouts: 9.33 us -> 2.52 us
  starting transfers between devices: 11.3 us -> 17 us
    pallas_call x5 -> x6, Pallas kernels: 65.9 us -> 40 us  [call(): pl.pallas_call(kernel, name=name, out_shape=[jax.ShapeDtypeStruct(s, F32)...]
    all_to_all x1 -> x0, blocking collectives: 14.1 us -> none  [on_device(): lax.all_to_all(spread_heat, 'axial', split_axis=0, concat_axis=0, tiled=T...]
    unnamed x36 -> x10, local copies, waits for them, and re-layouts: 8.61 us -> 2.52 us
    all_to_all x0 -> x1, starting transfers between devices: none -> 4.23 us  [on_device(): lax.all_to_all(out_box.reshape(groups, share, CZ), 'axial', split_axis=0,...]
    all_to_all x0 -> x1, waiting for transfers between devices: none -> 3.9 us  [on_device(): lax.all_to_all(out_box.reshape(groups, share, CZ), 'axial', split_axis=0,...]
    ppermute x1, waiting for transfers between devices: 0.37 us -> 2.84 us  [on_device(): side_r = lax.ppermute(left, 'azim', to_left)]
    ppermute x1, starting transfers between devices: 0.01 us -> 2.46 us  [on_device(): side_l = lax.ppermute(right, 'azim', to_right)]
    ppermute x1, waiting for transfers between devices: 0.83 us -> 2.91 us  [on_device(): side_l = lax.ppermute(right, 'azim', to_right)]
  transfers between devices with their start and end apart: 6 -> 7, of which waited for: 2 -> 3; matrix products, arithmetic and copies ran while one was open for 1% -> 0% of each run, Pallas kernels for 5% -> 17%
where the time goes in v2:
time: 78.7 us; the launch traced here: 78.2 us
  Pallas kernels  40 us (51%)
  starting transfers between devices  17 us (22%)
  waiting for transfers between devices  9.66 us (12%)
  blocking collectives  7.58 us (10%)
  local copies, waits for them, and re-layouts  2.52 us (3%)
    pallas_call x6, Pallas kernels, call(): pl.pallas_call(kernel, name=name, out_shape=[jax.ShapeDtypeStruct(s, F32)...  40 us
    all_to_all x1, blocking collectives, on_device(): lax.all_to_all(parts, 'axial', split_axis=0, concat_axis=0, tiled=True)  7.58 us
    all_to_all x1, starting transfers between devices, on_device(): lax.all_to_all(out_box.reshape(groups, share, CZ), 'axial', split_axis=0,...  4.23 us
    all_to_all x1, waiting for transfers between devices, on_device(): lax.all_to_all(out_box.reshape(groups, share, CZ), 'axial', split_axis=0,...  3.9 us
    ppermute x1, starting transfers between devices, on_device(): low = lax.ppermute(up, 'axial', upward)  3.13 us
    ppermute x1, starting transfers between devices, on_device(): far_r = lax.ppermute(left, 'azim', to_left)  3.08 us
    ppermute x1, waiting for transfers between devices, on_device(): side_l = lax.ppermute(right, 'azim', to_right)  2.91 us
    ppermute x1, waiting for transfers between devices, on_device(): side_r = lax.ppermute(left, 'azim', to_left)  2.84 us
  transfers between devices with their start and end apart: 7, of which 3 were waited for; matrix products, arithmetic and copies ran while one was open for 0% of the time, Pallas kernels for 17%

profile of v2, /device:TPU:0, one launch (start us, length us, event | category | flops | bytes accessed | tf_op | source)
XLA Modules:
  0.0 78.2 jit_solution(6135137957131777499)
XLA Ops:
  0.6 2.4 %pack_first.1 = (f32[936,128]{1,0:T(8,128)}, f32[936,128]{1,0:T(8,128)S(1)}, f32[200,128]{1,0:T(8,128)S(1)}, f32[200,128]{1,0:T(8,128)S(1)}, f32[16,128]{1,0:T(8,128)S(1)}) custom-call(f32[576,128]{1,0:T(8,128)} %bitcast.23, f32[576,128]{1,0:T(8,128)} %bitcast.25, f32[192,128]{1,0:T(8,128)} %bitcast.27, s32[16,128]{1,0:T(8,128)} %bitcast.29, ...), custom_call_target="tpu_custom_call" | custom-call | tf_op jit(solution)/shard_map/pack_first/pallas_call | solution.py:564
  3.0 0.0 copy-start.1
  3.1 0.6 copy-done.1
  3.6 3.1 %collective-permute-start = (f32[936,128]{1,0:T(8,128)}, f32[936,128]{1,0:T(8,128)}, u32[]{:S(2)}, u32[]{:S(2)}) collective-permute-start(f32[936,128]{1,0:T(8,128)} %get-tuple-element.20), channel_id=1, source_target_pairs={{0,4},{4,8},{8,12},{12,16},{16,20},{20,24},{24,28},{1,5},{5,9},{9,... | collective-permute-start | bytes 1437704 | tf_op jit(solution)/shard_map/ppermute | solution.py:599
  6.8 1.3 %collective-permute-start.1 = (f32[936,128]{1,0:T(8,128)S(1)}, f32[936,128]{1,0:T(8,128)}, u32[]{:S(2)}, u32[]{:S(2)}) collective-permute-start(f32[936,128]{1,0:T(8,128)S(1)} %get-tuple-element.21), channel_id=1, source_target_pairs={{4,0},{8,4},{12,8},{16,12},{20,16},{24,20},{28,24},{5,1},{9,5},{13... | collective-permute-start | bytes 1437704 | tf_op jit(solution)/shard_map/ppermute | solution.py:600
  8.1 2.5 %collective-permute-start.2 = (f32[200,128]{1,0:T(8,128)S(1)}, f32[200,128]{1,0:T(8,128)S(1)}, u32[]{:S(2)}, u32[]{:S(2)}) collective-permute-start(f32[200,128]{1,0:T(8,128)S(1)} %get-tuple-element.22), channel_id=1, source_target_pairs={{0,1},{1,2},{2,3},{3,0},{4,5},{5,6},{6,7},{7,4},{8,9},{9,10},{10,1... | collective-permute-start | bytes 307208 | tf_op jit(solution)/shard_map/ppermute | solution.py:602
  10.5 2.1 %collective-permute-start.3 = (f32[200,128]{1,0:T(8,128)S(1)}, f32[200,128]{1,0:T(8,128)S(1)}, u32[]{:S(2)}, u32[]{:S(2)}) collective-permute-start(f32[200,128]{1,0:T(8,128)S(1)} %get-tuple-element.23), channel_id=1, source_target_pairs={{0,3},{1,0},{2,1},{3,2},{4,7},{5,4},{6,5},{7,6},{8,11},{9,8},{10,9... | collective-permute-start | bytes 307208 | tf_op jit(solution)/shard_map/ppermute | solution.py:601
  12.6 2.9 %collective-permute-done.2.refs_1_.refs_4_.refs_7_ = f32[200,128]{1,0:T(8,128)S(1)} collective-permute-done((f32[200,128]{1,0:T(8,128)S(1)}, f32[200,128]{1,0:T(8,128)S(1)}, u32[]{:S(2)}, u32[]{:S(2)}) %collective-permute-start.2) | collective-permute-done | bytes 102432 | tf_op jit(solution)/shard_map/ppermute | solution.py:602
  15.5 0.0 copy-start.2
  15.5 2.8 %collective-permute-done.3.refs_2_.refs_5_.refs_8_ = f32[200,128]{1,0:T(8,128)S(1)} collective-permute-done((f32[200,128]{1,0:T(8,128)S(1)}, f32[200,128]{1,0:T(8,128)S(1)}, u32[]{:S(2)}, u32[]{:S(2)}) %collective-permute-start.3) | collective-permute-done | bytes 102432 | tf_op jit(solution)/shard_map/ppermute | solution.py:601
  18.4 0.0 copy-done.2
  18.4 0.0 copy-start.3
  18.4 0.6 copy-done.3
  19.0 1.5 %relay.1 = f32[448,128]{1,0:T(8,128)} custom-call(f32[24,128]{1,0:T(8,128)} %refs_0_.1, f32[200,128]{1,0:T(8,128)} %copy-done.2, f32[200,128]{1,0:T(8,128)} %copy-done.3), custom_call_target="tpu_custom_call" | custom-call | tf_op jit(solution)/shard_map/relay/pallas_call | solution.py:564
  20.5 4.2 %all-to-all-start = ((f32[8,56,128]{2,1,0:T(8,128)}), f32[8,56,128]{2,1,0:T(8,128)}, u32[]{:S(2)}, u32[]{:S(2)}) async-start(f32[8,56,128]{2,1,0:T(8,128)} %bitcast.13), calls=%async_computation | async-start | bytes 458752 | tf_op jit(solution)/shard_map/all_to_all | solution.py:611
  24.7 2.8 %breaks_own.1.refs_1_ = f32[15,16,24,128]{3,2,1,0:T(8,128)S(1)} custom-call(f32[16,128]{1,0:T(8,128)} %copy-done.1), custom_call_target="tpu_custom_call" | custom-call | tf_op jit(solution)/shard_map/breaks_own/pallas_call | solution.py:564
  27.5 3.9 %all-to-all-done = f32[8,56,128]{2,1,0:T(8,128)} async-done(((f32[8,56,128]{2,1,0:T(8,128)}), f32[8,56,128]{2,1,0:T(8,128)}, u32[]{:S(2)}, u32[]{:S(2)}) %all-to-all-start) | async-done | bytes 229408 | tf_op jit(solution)/shard_map/all_to_all | solution.py:611
  31.4 0.0 collective-permute-done.refs_0_.refs_2_.refs_4_
  31.4 0.0 collective-permute-done.1.refs_1_.refs_3_.refs_5_
  31.4 2.8 %pack_second.1 = (f32[320,128]{1,0:T(8,128)S(1)}, f32[320,128]{1,0:T(8,128)S(1)}, f32[272,128]{1,0:T(8,128)S(1)}) custom-call(f32[936,128]{1,0:T(8,128)} %collective-permute-done.refs_0_.refs_2_.refs_4_, f32[936,128]{1,0:T(8,128)} %collective-permute-done.1.refs_1_.refs_3_.refs_5_, f32[448,128]{1,0:T(8,128)} %bitcast.14.refs_2_.refs_6_, s32[1,48]{1,0:T(1,128)} %bitcast.31, ...), custom_call_target="tpu_custom_call" | custom-call | tf_op jit(solution)/shard_map/pack_second/pallas_call | solution.py:564
  34.2 0.0 copy-start
  34.2 0.6 copy-done
  34.9 0.7 collective-permute-start.4
  35.6 3.1 %collective-permute-start.5 = (f32[320,128]{1,0:T(8,128)S(1)}, f32[320,128]{1,0:T(8,128)}, u32[]{:S(2)}, u32[]{:S(2)}) collective-permute-start(f32[320,128]{1,0:T(8,128)S(1)} %get-tuple-element.32), channel_id=1, source_target_pairs={{0,3},{1,0},{2,1},{3,2},{4,7},{5,4},{6,5},{7,6},{8,11},{9,8},{10,9... | collective-permute-start | bytes 491528 | tf_op jit(solution)/shard_map/ppermute | solution.py:633
  38.7 9.4 %breaks_all.1.refs_13_ = f32[15,40,24,128]{3,2,1,0:T(8,128)S(1)} custom-call(s32[1]{0:T(128)} %bitcast.refs_0_, f32[15,16,24,128]{3,2,1,0:T(8,128)S(1)} %breaks_own.1.refs_1_, f32[936,128]{1,0:T(8,128)} %collective-permute-done.refs_0_.refs_2_.refs_4_, f32[936,128]{1,0:T(8,128)} %collective-permute-done.1.refs_1_.refs_3_.refs_5_, f32[200,128]{1,0:T(8,128)} %copy-done.2, ...), custom_call_target="tpu_custom_call" | custom-call | tf_op jit(solution)/shard_map/breaks_all/pallas_call | solution.py:564
  48.1 0.0 collective-permute-done.4.refs_9_
  48.1 0.0 copy-start.4
  48.1 0.0 collective-permute-done.5.refs_10_
  48.1 0.7 copy-done.4
  48.7 21.2 %march.1 = (f32[576,128]{1,0:T(8,128)}, f32[576,128]{1,0:T(8,128)}, f32[192,128]{1,0:T(8,128)S(1)}) custom-call(s32[1]{0:T(128)} %bitcast.refs_0_, f32[576,128]{1,0:T(8,128)} %bitcast.24, f32[576,128]{1,0:T(8,128)} %bitcast.26, f32[192,128]{1,0:T(8,128)} %bitcast.28, f32[936,128]{1,0:T(8,128)} %collective-permute-done.refs_0_.refs_2_.refs_4_, ...), custom_call_target="tpu_custom_call" | custom-call | tf_op jit(solution)/shard_map/march/pallas_call | solution.py:564
  70.0 7.6 %all_to_all.10 = f32[8,24,128]{2,1,0:T(8,128)S(1)} all-to-all(f32[8,24,128]{2,1,0:T(8,128)S(1)} %bitcast.22), channel_id=1, replica_groups=mesh['axial'=8,'azim'=4] {'axial'}, dimensions={0} | all-to-all | bytes 196608 | tf_op jit(solution)/shard_map/all_to_all | solution.py:681
  77.5 0.6 reduce_sum.9
Async XLA Ops:
  3.0 0.6 copy-start.1
  3.6 27.8 %collective-permute-start = (f32[936,128]{1,0:T(8,128)}, f32[936,128]{1,0:T(8,128)}, u32[]{:S(2)}, u32[]{:S(2)}) collective-permute-start(f32[936,128]{1,0:T(8,128)} %get-tuple-element.20), channel_id=1, source_target_pairs={{0,4},{4,8},{8,12},{12,16},{16,20},{20,24},{24,28},{1,5},{5,9},{9,... | collective-permute-start | bytes 1437704 | tf_op jit(solution)/shard_map/ppermute | solution.py:599
  6.8 24.6 %collective-permute-start.1 = (f32[936,128]{1,0:T(8,128)S(1)}, f32[936,128]{1,0:T(8,128)}, u32[]{:S(2)}, u32[]{:S(2)}) collective-permute-start(f32[936,128]{1,0:T(8,128)S(1)} %get-tuple-element.21), channel_id=1, source_target_pairs={{4,0},{8,4},{12,8},{16,12},{20,16},{24,20},{28,24},{5,1},{9,5},{13... | collective-permute-start | bytes 1437704 | tf_op jit(solution)/shard_map/ppermute | solution.py:600
  8.1 7.5 %collective-permute-start.2 = (f32[200,128]{1,0:T(8,128)S(1)}, f32[200,128]{1,0:T(8,128)S(1)}, u32[]{:S(2)}, u32[]{:S(2)}) collective-permute-start(f32[200,128]{1,0:T(8,128)S(1)} %get-tuple-element.22), channel_id=1, source_target_pairs={{0,1},{1,2},{2,3},{3,0},{4,5},{5,6},{6,7},{7,4},{8,9},{9,10},{10,1... | collective-permute-start | bytes 307208 | tf_op jit(solution)/shard_map/ppermute | solution.py:602
  10.5 7.8 %collective-permute-start.3 = (f32[200,128]{1,0:T(8,128)S(1)}, f32[200,128]{1,0:T(8,128)S(1)}, u32[]{:S(2)}, u32[]{:S(2)}) collective-permute-start(f32[200,128]{1,0:T(8,128)S(1)} %get-tuple-element.23), channel_id=1, source_target_pairs={{0,3},{1,0},{2,1},{3,2},{4,7},{5,4},{6,5},{7,6},{8,11},{9,8},{10,9... | collective-permute-start | bytes 307208 | tf_op jit(solution)/shard_map/ppermute | solution.py:601
  15.5 2.8 %copy-start.2 = (f32[200,128]{1,0:T(8,128)}, f32[200,128]{1,0:T(8,128)S(1)}, u32[]{:S(2)}) copy-start(f32[200,128]{1,0:T(8,128)S(1)} %collective-permute-done.2.refs_1_.refs_4_.refs_7_) | copy-start | bytes 307204
  18.4 0.6 copy-start.3
  20.5 10.9 %all-to-all-start = ((f32[8,56,128]{2,1,0:T(8,128)}), f32[8,56,128]{2,1,0:T(8,128)}, u32[]{:S(2)}, u32[]{:S(2)}) async-start(f32[8,56,128]{2,1,0:T(8,128)} %bitcast.13), calls=%async_computation | async-start | bytes 458752 | tf_op jit(solution)/shard_map/all_to_all | solution.py:611
  34.2 0.6 copy-start
  34.9 13.2 %collective-permute-start.4 = (f32[320,128]{1,0:T(8,128)S(1)}, f32[320,128]{1,0:T(8,128)S(1)}, u32[]{:S(2)}, u32[]{:S(2)}) collective-permute-start(f32[320,128]{1,0:T(8,128)S(1)} %get-tuple-element.31), channel_id=1, source_target_pairs={{0,1},{1,2},{2,3},{3,0},{4,5},{5,6},{6,7},{7,4},{8,9},{9,10},{10,1... | collective-permute-start | bytes 491528 | tf_op jit(solution)/shard_map/ppermute | solution.py:634
  35.6 12.5 %collective-permute-start.5 = (f32[320,128]{1,0:T(8,128)S(1)}, f32[320,128]{1,0:T(8,128)}, u32[]{:S(2)}, u32[]{:S(2)}) collective-permute-start(f32[320,128]{1,0:T(8,128)S(1)} %get-tuple-element.32), channel_id=1, source_target_pairs={{0,3},{1,0},{2,1},{3,2},{4,7},{5,4},{6,5},{7,6},{8,11},{9,8},{10,9... | collective-permute-start | bytes 491528 | tf_op jit(solution)/shard_map/ppermute | solution.py:633
  48.1 0.7 copy-start.4

commit v3 on v2

--- a/solution.py
+++ b/solution.py
@@ -16,6 +16,7 @@
 PAD = 16
 PER = CZ // SLOT
 UNROLL = 3
+PREPARE = 13
 NFIELD = 7
 NEXACT = lax.Precision.HIGHEST
 F32 = jnp.float32
@@ -54,7 +55,7 @@
 
 
 class Sizes:
-    def __init__(self, sections):
+    def __init__(self, sections, rows):
         self.sections = sections
         self.halo = REACH * sections
         self.ext = CA + 2 * self.halo
@@ -69,14 +70,10 @@
         self.tab_at = -(-at // 8) * 8
         self.edge_rows = self.tab_at + PAD
         self.own_tiles = CA // PER
-        self.side_rows = PAD + NFIELD * self.own_tiles * NR + PAD
-        self.side_rows = -(-self.side_rows // 8) * 8
-        self.far_tiles = 2 * self.halo // PER
-        self.far_pad = PAD
-        self.heat_tiles = -(-self.ext // 2 // PER)
-        self.far_rows = self.far_pad + (NFIELD * self.far_tiles + self.heat_tiles) * NR + PAD
-        self.far_rows = -(-self.far_rows // 8) * 8
-        self.temp_rows = PAD + self.ext // 2 * NR + PAD
+        self.side_heat = -(-(PAD + NFIELD * self.own_tiles * NR + NR) // 8) * 8
+        self.side_tab = self.side_heat + rows
+        self.side_rows = self.side_tab + 8
+        self.table = CA // 2 * NR
 
     def moving(self, f):
         return 3 <= f < 6
@@ -97,9 +94,6 @@
     def side_row(self, f, t):
         return PAD + (f * self.own_tiles + t) * NR
 
-    def far_row(self, f, t):
-        return self.far_pad + (f * self.far_tiles + t) * NR
-
 
 def own_plane(refs, f, a):
     disp, velo, stiff = refs
@@ -111,8 +105,9 @@
     return lax.broadcasted_iota(jnp.int32, (PAIR, CZ), 0) < NR
 
 
-def twice(upper, lower, at):
-    return jnp.where(is_top(), upper[pl.ds(at, PAIR), :], lower[pl.ds(at - NR, PAIR), :])
+def twice(upper, lower, at, low_at=None):
+    low_at = at if low_at is None else low_at
+    return jnp.where(is_top(), upper[pl.ds(at, PAIR), :], lower[pl.ds(low_at - NR, PAIR), :])
 
 
 def wanted_rows(table, count):
@@ -148,7 +143,7 @@
     right[pl.ds(row, NR), :] = to_right
 
 
-def pack_first(sz, share, disp, velo, stiff, codes, owner, row_of, up, down, left, right, code_f):
+def pack_first(sz, share, disp, velo, stiff, codes, owner, row_of, thermal, up, down, left, right, code_f):
     refs = (disp, velo, stiff)
     for f in range(NFIELD):
         for p in range(sz.halo):
@@ -163,62 +158,30 @@
             pack_tiles(sz, planes, left, right, sz.side_row(f, t))
     c = codes[...].astype(F32)
     code_f[...] = c
-    table = (owner[...] * share + row_of[...]).astype(F32)
-    blank = jnp.zeros((PAD, CZ), F32)
+    wanted = (owner[...] * share + row_of[...]).astype(F32)
+    wanted = jnp.broadcast_to(wanted, (8, wanted.shape[1]))
+    table = exact_dot(wanted, layers_of(), ((1,), (1,)))
     for out in (up, down, left, right):
-        out[pl.ds(out.shape[0] - PAD, PAD), :] = blank
         out[pl.ds(0, sz.code_rows), :] = c
-    for out in (up, down):
-        out[pl.ds(sz.tab_at, 1), pl.ds(0, table.shape[1])] = table
-
-
-def pack_second(sz, held, share, low, high, thermal, owner, row_of, left, right, temp):
-    n = owner.shape[1]
+    for out, at in ((up, sz.tab_at), (down, sz.tab_at), (left, sz.side_tab), (right, sz.side_tab)):
+        out[pl.ds(at, 8), pl.ds(0, sz.table)] = table
+    for out in (left, right):
+        out[pl.ds(sz.side_heat, thermal.shape[0]), :] = thermal[...]
+
+
+def relay(sz, groups, thermal, side_l, side_r, box, ring):
     rows = thermal.shape[0]
-    heat = thermal[...]
-    expand = layers_of()
-    blank = jnp.zeros((PAD, CZ), F32)
-    temp[pl.ds(0, PAD), :] = blank
-    temp[pl.ds(sz.temp_rows - PAD, PAD), :] = blank
-    at = PAD
-    for which in range(3):
-        if which == 1:
-            table = owner[...] * share + row_of[...]
-        else:
-            src = low if which == 0 else high
-            table = src[pl.ds(sz.tab_at, 1), :][:, 0:n].astype(jnp.int32)
-        got = exact_dot(wanted_rows(table, rows), heat, ((0,), (0,)))
-        got = exact_dot(expand, got)
-        first = (CA - sz.halo) // 2 * NR if which == 0 else 0
-        count = (CA if which == 1 else sz.halo) // 2 * NR
-        temp[pl.ds(at, count), :] = got[first : first + count]
-        at += count
-    far = list(range(sz.halo)) + list(range(sz.halo + CA, sz.ext))
-    for f in range(NFIELD):
-        for t in range(sz.far_tiles):
-            planes = []
-            for p in far[t * PER : (t + 1) * PER]:
-                at = sz.edge_row(f, p)
-                src = low if p < sz.halo else high
-                planes.append(None if at is None else src[pl.ds(at, NR), :])
-            pack_tiles(sz, planes, left, right, sz.far_row(f, t))
-    pairs = sz.ext // 2
-    for t in range(sz.heat_tiles):
-        planes = [temp[pl.ds(PAD + b * NR, NR), :] for b in range(t * PER, min(pairs, (t + 1) * PER))]
-        pack_tiles(sz, planes, left, right, sz.far_row(NFIELD, t))
-    for out in (left, right):
-        out[pl.ds(sz.far_rows - PAD, PAD), :] = blank
-        out[pl.ds(0, PAD), :] = blank
-
-
-def relay(groups, thermal, side_l, side_r, box):
-    rows = thermal.shape[0]
-    n = side_l.shape[0]
+    n = sz.code_rows
+    heat = pl.ds(sz.side_heat, rows)
+    beside = jnp.where(lanes_of((rows, CZ)) < CZ // 2, side_r[heat, :], side_l[heat, :])
     for g in range(groups):
-        at = g * (rows + 2 * n)
+        at = g * (2 * rows + 2 * n)
         box[pl.ds(at, rows), :] = thermal[...]
-        box[pl.ds(at + rows, n), :] = side_l[...]
-        box[pl.ds(at + rows + n, n), :] = side_r[...]
+        box[pl.ds(at + rows, rows), :] = beside
+        box[pl.ds(at + 2 * rows, n), :] = side_l[pl.ds(0, n), :]
+        box[pl.ds(at + 2 * rows + n, n), :] = side_r[pl.ds(0, n), :]
+    ring[pl.ds(0, sz.side_rows), :] = side_l[...]
+    ring[pl.ds(sz.side_rows, sz.side_rows), :] = side_r[...]
 
 
 def decode(codes):
@@ -270,7 +233,7 @@
 
 
 def breaks_all(
-    sz, at_lo, at_hi, own, low, high, side_l, side_r, box, out, rows_ref, cols_ref, acc, rows_s, cols_s, acc_s
+    sz, at_lo, at_hi, own, low, high, side_l, side_r, box, out, rows_ref, cols_ref, acc, rows_s, cols_s, acc_l, acc_r
 ):
     n, halo = sz.code_rows, sz.halo
     acc[pl.ds(0, PAD), :] = jnp.zeros((PAD, 4 * CZ), F32)
@@ -283,39 +246,46 @@
     edge = (is_top() & (wide >= CZ - SLOT)) | (~is_top() & (wide < SLOT))
     sources = [
         (box[pl.ds(at_lo, n), :], box[pl.ds(at_lo + n, n), :]),
-        (side_l[...], side_r[...]),
+        (side_l[pl.ds(0, n), :], side_r[pl.ds(0, n), :]),
         (box[pl.ds(at_hi, n), :], box[pl.ds(at_hi + n, n), :]),
     ]
-    side_breaks(sz, sources, own, out, rows_s, cols_s, acc_s, edge)
-
-
-def side_breaks(sz, sources, own, out, rows_ref, cols_ref, acc, edge):
-    n = sz.code_rows * CZ
-    rows = -(-NBOND * PAIR // 16) * 16
+    side_breaks(sz, sources, own, out, rows_s, cols_s, acc_l, acc_r, edge)
+
+
+def side_breaks(sz, sources, own, out, rows_ref, cols_ref, acc_l, acc_r, edge):
+    rows = -(-NBOND * NR // 16) * 16
     for which, (left, right) in enumerate(sources):
-        k, a, r, z = decode(left)
-        spread(rows_ref, k * PAIR + r, rows, 240)
-        spread(cols_ref, jnp.where(z >= CZ - SLOT, a * SLOT + z - (CZ - SLOT), -1.0), CA * SLOT, 256, weigh=True)
-        k, a, r, z = decode(right)
-        spread(rows_ref, k * PAIR + NR + r, rows, 240, lane_at=n)
-        tile = jnp.floor(a * (1.0 / PER))
-        slot = a - tile * PER + 1
-        slot = jnp.where(slot == PER, 0.0, slot)
-        spread(cols_ref, jnp.where(z < SLOT, tile * CZ + slot * SLOT + z, -1.0), CA * SLOT, 256, n, weigh=True)
-        acc[...] = dot_nt(rows_ref[...], cols_ref[...])
-        for p in range(sz.ext):
-            if sz.source(p)[0] != which:
-                continue
-            a = sz.source(p)[1]
-            for b in range(NBOND):
-                x = acc[pl.ds(b * PAIR, PAIR), pl.ds(a // PER * CZ, CZ)]
-                old = own[b, a] if which == 1 else out[b, p]
-                out[b, p] = jnp.where(edge, roll(x, SLOT * (PER - 1 - a % PER)), old)
+        first = CA - sz.halo if which == 0 else 0
+        count = CA if which == 1 else sz.halo
+        cols = -(-count // PER) * CZ
+        for side, codes in enumerate((left, right)):
+            k, a, r, z = decode(codes)
+            spread(rows_ref, k * NR + r, rows, 192)
+            a = a - first
+            tile = jnp.floor(a * (1.0 / PER))
+            slot = a - tile * PER + side
+            slot = jnp.where(slot == PER, 0.0, slot)
+            lane = z if side else z - (CZ - SLOT)
+            near = (lane >= 0) & (lane < SLOT) & (a >= 0) & (a < count)
+            spread(cols_ref, jnp.where(near, tile * CZ + slot * SLOT + lane, -1.0), cols, 256, weigh=True)
+            acc = acc_r if side else acc_l
+            acc[pl.ds(PAD, rows), pl.ds(0, cols)] = dot_nt(rows_ref[...], cols_ref[pl.ds(0, cols), :])
+        for b in range(NBOND):
+            for t in range(cols // CZ):
+                lanes = pl.ds(t * CZ, CZ)
+                x = jnp.where(
+                    is_top(), acc_l[pl.ds(PAD + b * NR, PAIR), lanes], acc_r[pl.ds(PAD + b * NR - NR, PAIR), lanes]
+                )
+                for s in range(min(PER, count - t * PER)):
+                    i = t * PER + s
+                    p = i + (0, sz.halo, sz.halo + CA)[which]
+                    old = own[b, i] if which == 1 else out[b, p]
+                    out[b, p] = jnp.where(edge, roll(x, SLOT * (PER - 1 - s)), old)
 
 
 def march(
-    sz, total, held, place, disp, velo, stiff, low, high, temp, side_l, side_r, far_l, far_r, owner, row_of,
-    broken, out_d, out_v, out_e, fld, stiffk, heatk, bonds, forces, wait_a, wait_b, energy, pooled,
+    sz, total, held, place, disp, velo, stiff, low, high, side_l, side_r, ring_lo, ring_hi, owner, row_of,
+    box, broken, out_d, out_v, out_e, fld, stiffk, heatk, bonds, forces, wait_a, wait_b, energy, pooled, temp, tables,
 ):
     refs = (disp, velo, stiff)
     halo = sz.halo
@@ -323,29 +293,57 @@
     wide = lanes_of((PAIR, CZ))
     top = is_top()
     edge = (top & (wide >= CZ - SLOT)) | (~top & (wide < SLOT))
-    for f in range(NFIELD + 1):
-        for p in range(sz.ext):
-            which, a = sz.source(p)
-            if f == NFIELD:
-                x = twice(temp, temp, PAD + p // 2 * NR)
-                s = p // 2
-                t, s = s // PER, s % PER
-                y = twice(far_l, far_r, sz.far_row(NFIELD, t))
-            elif which == 1:
+    share = 2 * (held + sz.code_rows)
+    heat = box[...]
+    wanted = (owner[...] * share + row_of[...]).astype(F32)
+    wanted = exact_dot(jnp.broadcast_to(wanted, (8, wanted.shape[1])), layers_of(), ((1,), (1,)))
+    lists = {
+        (0, 1): low[pl.ds(sz.tab_at, 8), pl.ds(0, sz.table)],
+        (1, 1): wanted,
+        (2, 1): high[pl.ds(sz.tab_at, 8), pl.ds(0, sz.table)],
+    }
+    for which, ref, at in (
+        (0, ring_lo, 0), (0, ring_lo, sz.side_rows), (1, side_l, 0), (1, side_r, 0), (2, ring_hi, 0), (2, ring_hi, sz.side_rows)
+    ):
+        side = 2 if at or ref is side_r else 0
+        lists[which, side] = ref[pl.ds(at + sz.side_tab, 8), pl.ds(0, sz.table)] + held
+    parts, rest = [], heat
+    for _ in range(3):
+        part = rest.astype(jnp.bfloat16)
+        parts.append(part)
+        rest = rest - part.astype(F32)
+    heat3 = jnp.concatenate(parts, axis=1)
+    for j, (key, table) in enumerate(lists.items()):
+        tables[pl.ds(j, 1), pl.ds(0, sz.table)] = table[0:1]
+    columns = tables[...].T
+    row_id = lax.broadcasted_iota(jnp.int32, (sz.table, heat.shape[0]), 1).astype(F32)
+    for j, (which, side) in enumerate(lists):
+        hot = jnp.where(columns[0 : sz.table, j : j + 1] == row_id, 1.0, 0.0).astype(jnp.bfloat16)
+        got = jnp.dot(hot, heat3, preferred_element_type=F32)
+        temp[3 * which + side, pl.ds(PAD, sz.table), :] = (
+            got[:, 0:CZ] + got[:, CZ : 2 * CZ] + got[:, 2 * CZ :]
+        )
+    for p in range(sz.ext):
+        which, a = sz.source(p)
+        for f in range(NFIELD):
+            if which == 1:
                 x = own_plane(refs, f, a)
                 x = jnp.concatenate([x, x], axis=0)
-                t, s = a // PER, a % PER
-                y = twice(side_l, side_r, sz.side_row(f, t))
+                y = twice(side_l, side_r, sz.side_row(f, a // PER))
             else:
                 at = sz.edge_row(f, p)
                 if at is None:
                     continue
                 src = low if which == 0 else high
                 x = twice(src, src, at)
-                q = p if which == 0 else p - CA
-                t, s = q // PER, q % PER
-                y = twice(far_l, far_r, sz.far_row(f, t))
-            fld[f, p] = jnp.where(edge, roll(y, SLOT * (PER - 1 - s)), x)
+                ring = ring_lo if which == 0 else ring_hi
+                at = sz.side_row(f, a // PER)
+                y = twice(ring, ring, at, at + sz.side_rows)
+            fld[f, p] = jnp.where(edge, roll(y, SLOT * (PER - 1 - a % PER)), x)
+        at = PAD + a // 2 * NR
+        x = twice(temp.at[3 * which + 1], temp.at[3 * which + 1], at)
+        y = twice(temp.at[3 * which], temp.at[3 * which + 2], at)
+        fld[NFIELD, p] = jnp.where(edge, y, x)
 
     row = lax.broadcasted_iota(jnp.int32, (PAIR, CZ), 0)
     not_top = jnp.where((row == NR - 1) | (row == PAIR - 1), 0.0, 1.0)
@@ -361,7 +359,7 @@
     def prepare(p):
         cache = {}
         get = lambda f, i, dz=0: turned(cache, f, p, i, dz)
-        for i in range(UNROLL):
+        for i in range(PREPARE):
             at = start + p + i
             live = [
                 jnp.where((at >= 0) & (at + da < total), 1.0, 0.0).astype(F32) for da in range(REACH + 1)
@@ -377,14 +375,14 @@
                 stiffk[k, p + i] = m * not_top if dr else m
                 heatk[k, p + i] = (h + h2) * (DILATION * 0.5 * n2 / d)
 
-    def several(body, first_plane, times):
+    def several(body, first_plane, times, group=UNROLL):
         def one(i, c):
-            body(first_plane + i * UNROLL)
+            body(first_plane + i * group)
             return c
 
         lax.fori_loop(0, times, one, 0)
 
-    several(prepare, 0, (sz.ext - 1) // UNROLL)
+    several(prepare, 0, (sz.ext - 1) // PREPARE, PREPARE)
     energy[...] = jnp.zeros_like(energy)
 
     span = range(UNROLL)
@@ -558,7 +556,7 @@
         body(*refs)
 
     every = list(scratch) + buffers
-    size = sum(math.prod(b.shape) * jnp.dtype(b.dtype).itemsize for b in every)
+    size = sum(math.prod(b.shape) * 4 for b in every)
     size += sum(4 * math.prod(s) for s in outs)
     size += sum(4 * math.prod(a.shape) for a, m in zip(arrays, spaces) if m is pltpu.VMEM)
     return pl.pallas_call(
@@ -573,7 +571,7 @@
 
 
 def on_device(displace, velocity, stiff, thermal, owner_of, row_of, breaks):
-    sz = Sizes(breaks.shape[0])
+    sz = Sizes(breaks.shape[0], thermal.shape[0])
     groups = lax.axis_size("axial")
     around = lax.axis_size("azim")
     held = thermal.shape[0]
@@ -585,11 +583,13 @@
     velo = velocity.transpose(0, 2, 1, 3).reshape(3 * NR * CA, CZ)
     stif = stiff.transpose(1, 0, 2).reshape(NR * CA, CZ)
 
-    edge, side, far = (sz.edge_rows, CZ), (sz.side_rows, CZ), (sz.far_rows, CZ)
+    edge, side = (sz.edge_rows, CZ), (sz.side_rows, CZ)
+    n = sz.code_rows
+    share = 2 * (held + n)
     up, down, left, right, code_f = call(
-        lambda *refs: pack_first(sz, held + 2 * sz.code_rows, *refs),
-        [disp, velo, stif, codes, owner, local],
-        [edge, edge, side, side, (sz.code_rows, CZ)],
+        lambda *refs: pack_first(sz, share, *refs),
+        [disp, velo, stif, codes, owner, local, thermal],
+        [edge, edge, side, side, (n, CZ)],
         name="pack_first",
     )
     to_left = [(i, (i - 1) % around) for i in range(around)]
@@ -600,18 +600,8 @@
     high = lax.ppermute(down, "axial", downward)
     side_r = lax.ppermute(left, "azim", to_left)
     side_l = lax.ppermute(right, "azim", to_right)
-    n = sz.code_rows
-    share = held + 2 * n
-    (out_box,) = call(
-        lambda *refs: relay(groups, *refs),
-        [thermal, (side_l, n), (side_r, n)],
-        [(groups * share, CZ)],
-        name="relay",
-    )
-    box = lax.all_to_all(out_box.reshape(groups, share, CZ), "axial", split_axis=0, concat_axis=0, tiled=True)
-
     plane = (PAIR, CZ)
-    lanes = sz.code_rows * CZ
+    lanes = n * CZ
     tall = NBOND * CA // 4 * NR
     work = [
         pltpu.VMEM((tall, lanes), jnp.bfloat16),
@@ -619,38 +609,43 @@
         pltpu.VMEM((tall + 2 * PAD, 4 * CZ), F32),
     ]
     (w_own,) = call(
-        lambda *refs: breaks_own(sz, *refs), [code_f], [(NBOND, CA) + plane], work, name="breaks_own"
+        lambda *refs: breaks_own(sz, *refs),
+        [(code_f, pltpu.VMEM)],
+        [(NBOND, CA) + plane],
+        work,
+        name="breaks_own",
     )
-    low, high, side_l, side_r, box, w_own = lax.optimization_barrier(
-        (low, high, side_l, side_r, box, w_own)
+    side_l, side_r, w_own = lax.optimization_barrier((side_l, side_r, w_own))
+    out_box, ring = call(
+        lambda *refs: relay(sz, groups, *refs),
+        [thermal, (side_l, pltpu.VMEM), (side_r, pltpu.VMEM)],
+        [(groups * share, CZ), (2 * sz.side_rows, CZ)],
+        name="relay",
     )
-    left, right, temp = call(
-        lambda *refs: pack_second(sz, held, share, *refs),
-        [low, high, box.reshape(groups * share, CZ), owner, local],
-        [far, far, (sz.temp_rows, CZ)],
-        name="pack_second",
-    )
-    far_r = lax.ppermute(left, "azim", to_left)
-    far_l = lax.ppermute(right, "azim", to_right)
-    strip = -(-NBOND * PAIR // 16) * 16
+    ring_lo = lax.ppermute(ring, "axial", upward)
+    ring_hi = lax.ppermute(ring, "axial", downward)
+    box = lax.all_to_all(out_box.reshape(groups, share, CZ), "axial", split_axis=0, concat_axis=0, tiled=True)
+    box = box.reshape(groups * share, CZ)
+    strip = -(-NBOND * NR // 16) * 16
     place = lax.axis_index("axial").astype(jnp.int32).reshape(1)
 
     def all_breaks(place, *refs):
         x = place[0]
         rows = [
-            pl.multiple_of(jnp.clip(x + d, 0, groups - 1) * share + held, 8) for d in (-1, 1)
+            pl.multiple_of(jnp.clip(x + d, 0, groups - 1) * share + 2 * held, 8) for d in (-1, 1)
         ]
         breaks_all(sz, *rows, *refs)
 
     (broken,) = call(
         all_breaks,
-        [(place, pltpu.SMEM), (w_own, pltpu.VMEM), (low, n), (high, n), (side_l, n), (side_r, n), box.reshape(groups * share, CZ)],
+        [(place, pltpu.SMEM), (w_own, pltpu.VMEM), (low, n), (high, n), (side_l, pltpu.VMEM), (side_r, pltpu.VMEM), (box, pltpu.VMEM)],
         [(NBOND, sz.ext) + plane],
         work
         + [
-            pltpu.VMEM((strip, 2 * lanes), jnp.bfloat16),
-            pltpu.VMEM((CA * SLOT, 2 * lanes), jnp.bfloat16),
-            pltpu.VMEM((strip, CA * SLOT), F32),
+            pltpu.VMEM((strip, lanes), jnp.bfloat16),
+            pltpu.VMEM((CA * SLOT, lanes), jnp.bfloat16),
+            pltpu.VMEM((strip + 2 * PAD, CA * SLOT), F32),
+            pltpu.VMEM((strip + 2 * PAD, CA * SLOT), F32),
         ],
         name="breaks_all",
     )
@@ -665,13 +660,15 @@
         pltpu.VMEM((2, REACH - 1) + plane, F32),
         pltpu.VMEM((-(-CA // UNROLL) * UNROLL,) + plane, F32),
         pltpu.VMEM((CA // 2 * NR, CZ), F32),
+        pltpu.VMEM((9, PAD + sz.table + PAD, CZ), F32),
+        pltpu.VMEM((CZ, CZ), F32),
     ]
     total = groups * CA
     out_d, out_v, out_e = call(
         lambda *refs: march(sz, total, held, *refs),
         [
-            (place, pltpu.SMEM), disp, velo, stif, low, high, temp, side_l, side_r, far_l, far_r, owner, local,
-            (broken, pltpu.VMEM),
+            (place, pltpu.SMEM), disp, velo, stif, low, high, (side_l, pltpu.VMEM), (side_r, pltpu.VMEM), ring_lo, ring_hi, owner, local,
+            (box, pltpu.VMEM), (broken, pltpu.VMEM),
         ],
         [disp.shape, velo.shape, (groups * held, CZ)],
         scratch,

time: 78.7 us -> 69.8 us (0.89)
  Pallas kernels: 40 us -> 34.2 us
  waiting for transfers between devices: 9.66 us -> 7.45 us
  local copies, waits for them, and re-layouts: 2.52 us -> 1.42 us
    pallas_call x6 -> x5, Pallas kernels: 40 us -> 34.2 us  [call(): pl.pallas_call(kernel, name=name, out_shape=[jax.ShapeDtypeStruct(s, F32)...]
    ppermute x1, waiting for transfers between devices: 2.91 us -> 1.21 us  [on_device(): side_l = lax.ppermute(right, 'azim', to_right)]
    unnamed x10 -> x4, local copies, waits for them, and re-layouts: 2.52 us -> 1.42 us
    all_to_all x1, waiting for transfers between devices: 3.9 us -> 3.07 us  [on_device(): lax.all_to_all(out_box.reshape(groups, share, CZ), 'axial', split_axis=0,...]
  transfers between devices with their start and end apart: 7 -> 7, of which waited for: 3 -> 3; matrix products, arithmetic and copies ran while one was open for 0% -> 0% of each run, Pallas kernels for 17% -> 16%
where the time goes in v3:
time: 69.8 us; the launch traced here: 69.3 us
  Pallas kernels  34.2 us (49%)
  starting transfers between devices  17.4 us (25%)
  blocking collectives  7.58 us (11%)
  waiting for transfers between devices  7.45 us (11%)
  local copies, waits for them, and re-layouts  1.42 us (2%)
  between operations  0.72 us (1%)
    pallas_call x5, Pallas kernels, call(): pl.pallas_call(kernel, name=name, out_shape=[jax.ShapeDtypeStruct(s, F32)...  34.2 us
    all_to_all x1, blocking collectives, on_device(): lax.all_to_all(parts, 'axial', split_axis=0, concat_axis=0, tiled=True)  7.58 us
    all_to_all x1, starting transfers between devices, on_device(): lax.all_to_all(out_box.reshape(groups, share, CZ), 'axial', split_axis=0,...  3.82 us
    ppermute x1, waiting for transfers between devices, on_device(): side_r = lax.ppermute(left, 'azim', to_left)  3.16 us
    ppermute x1, starting transfers between devices, on_device(): low = lax.ppermute(up, 'axial', upward)  3.16 us
    ppermute x1, starting transfers between devices, on_device(): ring_lo = lax.ppermute(ring, 'axial', upward)  3.1 us
    all_to_all x1, waiting for transfers between devices, on_device(): lax.all_to_all(out_box.reshape(groups, share, CZ), 'axial', split_axis=0,...  3.07 us
    ppermute x1, starting transfers between devices, on_device(): side_l = lax.ppermute(right, 'azim', to_right)  2.46 us
  transfers between devices with their start and end apart: 7, of which 3 were waited for; matrix products, arithmetic and copies ran while one was open for 0% of the time, Pallas kernels for 16%

profile of v3, /device:TPU:0, one launch (start us, length us, event | category | flops | bytes accessed | tf_op | source)
XLA Modules:
  0.0 69.3 jit_solution(499219746095524553)
XLA Ops:
  0.6 2.4 %pack_first.1 = (f32[936,128]{1,0:T(8,128)}, f32[936,128]{1,0:T(8,128)}, f32[232,128]{1,0:T(8,128)S(1)}, f32[232,128]{1,0:T(8,128)S(1)}, f32[16,128]{1,0:T(8,128)S(1)}) custom-call(f32[576,128]{1,0:T(8,128)} %bitcast.26, f32[576,128]{1,0:T(8,128)} %bitcast.28, f32[192,128]{1,0:T(8,128)} %bitcast.30, s32[16,128]{1,0:T(8,128)} %bitcast.32, s32[1,48]{1,0:T(1,128)} %bitcast.33, ...), custom_call_target="tpu_custom_call" | custom-call | tf_op jit(solution)/shard_map/pack_first/pallas_call | solution.py:562
  3.1 3.2 %collective-permute-start = (f32[936,128]{1,0:T(8,128)}, f32[936,128]{1,0:T(8,128)}, u32[]{:S(2)}, u32[]{:S(2)}) collective-permute-start(f32[936,128]{1,0:T(8,128)} %get-tuple-element.16), channel_id=1, source_target_pairs={{0,4},{4,8},{8,12},{12,16},{16,20},{20,24},{24,28},{1,5},{5,9},{9,... | collective-permute-start | bytes 1437704 | tf_op jit(solution)/shard_map/ppermute | solution.py:599
  6.2 1.3 %collective-permute-start.1 = (f32[936,128]{1,0:T(8,128)}, f32[936,128]{1,0:T(8,128)}, u32[]{:S(2)}, u32[]{:S(2)}) collective-permute-start(f32[936,128]{1,0:T(8,128)} %get-tuple-element.17), channel_id=1, source_target_pairs={{4,0},{8,4},{12,8},{16,12},{20,16},{24,20},{28,24},{5,1},{9,5},{13... | collective-permute-start | bytes 1437704 | tf_op jit(solution)/shard_map/ppermute | solution.py:600
  7.5 2.5 %collective-permute-start.2 = (f32[232,128]{1,0:T(8,128)S(1)}, f32[232,128]{1,0:T(8,128)S(1)}, u32[]{:S(2)}, u32[]{:S(2)}) collective-permute-start(f32[232,128]{1,0:T(8,128)S(1)} %get-tuple-element.18), channel_id=1, source_target_pairs={{0,1},{1,2},{2,3},{3,0},{4,5},{5,6},{6,7},{7,4},{8,9},{9,10},{10,1... | collective-permute-start | bytes 356360 | tf_op jit(solution)/shard_map/ppermute | solution.py:602
  10.0 2.1 %collective-permute-start.3 = (f32[232,128]{1,0:T(8,128)S(1)}, f32[232,128]{1,0:T(8,128)S(1)}, u32[]{:S(2)}, u32[]{:S(2)}) collective-permute-start(f32[232,128]{1,0:T(8,128)S(1)} %get-tuple-element.19), channel_id=1, source_target_pairs={{0,3},{1,0},{2,1},{3,2},{4,7},{5,4},{6,5},{7,6},{8,11},{9,8},{10,9... | collective-permute-start | bytes 356360 | tf_op jit(solution)/shard_map/ppermute | solution.py:601
  12.1 2.1 %breaks_own.1.refs_1_ = f32[15,16,24,128]{3,2,1,0:T(8,128)S(1)} custom-call(f32[16,128]{1,0:T(8,128)S(1)} %get-tuple-element.20.refs_0_), custom_call_target="tpu_custom_call" | custom-call | tf_op jit(solution)/shard_map/breaks_own/pallas_call | solution.py:562
  14.2 1.2 %collective-permute-done.2.refs_1_.refs_4_.refs_6_ = f32[232,128]{1,0:T(8,128)S(1)} collective-permute-done((f32[232,128]{1,0:T(8,128)S(1)}, f32[232,128]{1,0:T(8,128)S(1)}, u32[]{:S(2)}, u32[]{:S(2)}) %collective-permute-start.2) | collective-permute-done | bytes 118816 | tf_op jit(solution)/shard_map/ppermute | solution.py:602
  15.4 3.2 %collective-permute-done.3.refs_2_.refs_5_.refs_7_ = f32[232,128]{1,0:T(8,128)S(1)} collective-permute-done((f32[232,128]{1,0:T(8,128)S(1)}, f32[232,128]{1,0:T(8,128)S(1)}, u32[]{:S(2)}, u32[]{:S(2)}) %collective-permute-start.3) | collective-permute-done | bytes 118816 | tf_op jit(solution)/shard_map/ppermute | solution.py:601
  18.5 0.8 %relay.1 = (f32[640,128]{1,0:T(8,128)S(1)}, f32[464,128]{1,0:T(8,128)S(1)}) custom-call(f32[24,128]{1,0:T(8,128)} %refs_0_.1, f32[232,128]{1,0:T(8,128)S(1)} %collective-permute-done.2.refs_1_.refs_4_.refs_6_, f32[232,128]{1,0:T(8,128)S(1)} %collective-permute-done.3.refs_2_.refs_5_.refs_7_), custom_call_target="tpu_custom_call" | custom-call | tf_op jit(solution)/shard_map/relay/pallas_call | solution.py:562
  19.3 0.0 copy-start.1
  19.3 0.7 copy-done.1
  20.0 0.0 copy-start
  20.0 0.7 %copy-done = f32[640,128]{1,0:T(8,128)} copy-done((f32[640,128]{1,0:T(8,128)}, f32[640,128]{1,0:T(8,128)S(1)}, u32[]{:S(2)}) %copy-start) | copy-done | bytes 327704
  20.7 3.8 %all-to-all-start = ((f32[8,80,128]{2,1,0:T(8,128)}), f32[8,80,128]{2,1,0:T(8,128)S(1)}, u32[]{:S(2)}, u32[]{:S(2)}) async-start(f32[8,80,128]{2,1,0:T(8,128)} %bitcast.24), calls=%async_computation | async-start | bytes 655360 | tf_op jit(solution)/shard_map/all_to_all | solution.py:627
  24.6 3.1 %collective-permute-start.4 = (f32[464,128]{1,0:T(8,128)}, f32[464,128]{1,0:T(8,128)}, u32[]{:S(2)}, u32[]{:S(2)}) collective-permute-start(f32[464,128]{1,0:T(8,128)} %copy-done.1), channel_id=1, source_target_pairs={{0,4},{4,8},{8,12},{12,16},{16,20},{20,24},{24,28},{1,5},{5,9},{9,... | collective-permute-start | bytes 712712 | tf_op jit(solution)/shard_map/ppermute | solution.py:625
  27.7 1.5 %collective-permute-start.5 = (f32[464,128]{1,0:T(8,128)}, f32[464,128]{1,0:T(8,128)}, u32[]{:S(2)}, u32[]{:S(2)}) collective-permute-start(f32[464,128]{1,0:T(8,128)} %copy-done.1), channel_id=1, source_target_pairs={{4,0},{8,4},{12,8},{16,12},{20,16},{24,20},{28,24},{5,1},{9,5},{13... | collective-permute-start | bytes 712712 | tf_op jit(solution)/shard_map/ppermute | solution.py:626
  29.1 3.1 %all-to-all-done = f32[8,80,128]{2,1,0:T(8,128)S(1)} async-done(((f32[8,80,128]{2,1,0:T(8,128)}), f32[8,80,128]{2,1,0:T(8,128)S(1)}, u32[]{:S(2)}, u32[]{:S(2)}) %all-to-all-start) | async-done | bytes 327712 | tf_op jit(solution)/shard_map/all_to_all | solution.py:627
  32.2 0.0 collective-permute-done.refs_2_.refs_4_
  32.2 0.0 collective-permute-done.1.refs_3_.refs_5_
  32.2 8.1 %breaks_all.1.refs_13_ = f32[15,40,24,128]{3,2,1,0:T(8,128)S(1)} custom-call(s32[1]{0:T(128)} %bitcast.refs_0_, f32[15,16,24,128]{3,2,1,0:T(8,128)S(1)} %breaks_own.1.refs_1_, f32[936,128]{1,0:T(8,128)} %collective-permute-done.refs_2_.refs_4_, f32[936,128]{1,0:T(8,128)} %collective-permute-done.1.refs_3_.refs_5_, ...), custom_call_target="tpu_custom_call" | custom-call | tf_op jit(solution)/shard_map/breaks_all/pallas_call | solution.py:562
  40.4 0.0 collective-permute-done.4.refs_8_
  40.4 0.0 collective-permute-done.5.refs_9_
  40.4 20.7 %march.1 = (f32[576,128]{1,0:T(8,128)}, f32[576,128]{1,0:T(8,128)}, f32[192,128]{1,0:T(8,128)S(1)}) custom-call(s32[1]{0:T(128)} %bitcast.refs_0_, f32[576,128]{1,0:T(8,128)} %bitcast.27, f32[576,128]{1,0:T(8,128)} %bitcast.29, f32[192,128]{1,0:T(8,128)} %bitcast.31, f32[936,128]{1,0:T(8,128)} %collective-permute-done.refs_2_.refs_4_, ...), custom_call_target="tpu_custom_call" | custom-call | tf_op jit(solution)/shard_map/march/pallas_call | solution.py:562
  61.1 7.6 %all_to_all.10 = f32[8,24,128]{2,1,0:T(8,128)S(1)} all-to-all(f32[8,24,128]{2,1,0:T(8,128)S(1)} %bitcast.25), channel_id=1, replica_groups=mesh['axial'=8,'azim'=4] {'axial'}, dimensions={0} | all-to-all | bytes 196608 | tf_op jit(solution)/shard_map/all_to_all | solution.py:678
  68.7 0.6 reduce_sum.9
Async XLA Ops:
  3.1 29.1 %collective-permute-start = (f32[936,128]{1,0:T(8,128)}, f32[936,128]{1,0:T(8,128)}, u32[]{:S(2)}, u32[]{:S(2)}) collective-permute-start(f32[936,128]{1,0:T(8,128)} %get-tuple-element.16), channel_id=1, source_target_pairs={{0,4},{4,8},{8,12},{12,16},{16,20},{20,24},{24,28},{1,5},{5,9},{9,... | collective-permute-start | bytes 1437704 | tf_op jit(solution)/shard_map/ppermute | solution.py:599
  6.2 26.0 %collective-permute-start.1 = (f32[936,128]{1,0:T(8,128)}, f32[936,128]{1,0:T(8,128)}, u32[]{:S(2)}, u32[]{:S(2)}) collective-permute-start(f32[936,128]{1,0:T(8,128)} %get-tuple-element.17), channel_id=1, source_target_pairs={{4,0},{8,4},{12,8},{16,12},{20,16},{24,20},{28,24},{5,1},{9,5},{13... | collective-permute-start | bytes 1437704 | tf_op jit(solution)/shard_map/ppermute | solution.py:600
  7.5 7.8 %collective-permute-start.2 = (f32[232,128]{1,0:T(8,128)S(1)}, f32[232,128]{1,0:T(8,128)S(1)}, u32[]{:S(2)}, u32[]{:S(2)}) collective-permute-start(f32[232,128]{1,0:T(8,128)S(1)} %get-tuple-element.18), channel_id=1, source_target_pairs={{0,1},{1,2},{2,3},{3,0},{4,5},{5,6},{6,7},{7,4},{8,9},{9,10},{10,1... | collective-permute-start | bytes 356360 | tf_op jit(solution)/shard_map/ppermute | solution.py:602
  10.0 8.6 %collective-permute-start.3 = (f32[232,128]{1,0:T(8,128)S(1)}, f32[232,128]{1,0:T(8,128)S(1)}, u32[]{:S(2)}, u32[]{:S(2)}) collective-permute-start(f32[232,128]{1,0:T(8,128)S(1)} %get-tuple-element.19), channel_id=1, source_target_pairs={{0,3},{1,0},{2,1},{3,2},{4,7},{5,4},{6,5},{7,6},{8,11},{9,8},{10,9... | collective-permute-start | bytes 356360 | tf_op jit(solution)/shard_map/ppermute | solution.py:601
  19.3 0.7 %copy-start.1 = (f32[464,128]{1,0:T(8,128)}, f32[464,128]{1,0:T(8,128)S(1)}, u32[]{:S(2)}) copy-start(f32[464,128]{1,0:T(8,128)S(1)} %get-tuple-element.23) | copy-start | bytes 712708
  20.0 0.7 %copy-start = (f32[640,128]{1,0:T(8,128)}, f32[640,128]{1,0:T(8,128)S(1)}, u32[]{:S(2)}) copy-start(f32[640,128]{1,0:T(8,128)S(1)} %get-tuple-element.24) | copy-start | bytes 983044
  20.7 11.5 %all-to-all-start = ((f32[8,80,128]{2,1,0:T(8,128)}), f32[8,80,128]{2,1,0:T(8,128)S(1)}, u32[]{:S(2)}, u32[]{:S(2)}) async-start(f32[8,80,128]{2,1,0:T(8,128)} %bitcast.24), calls=%async_computation | async-start | bytes 655360 | tf_op jit(solution)/shard_map/all_to_all | solution.py:627
  24.6 15.8 %collective-permute-start.4 = (f32[464,128]{1,0:T(8,128)}, f32[464,128]{1,0:T(8,128)}, u32[]{:S(2)}, u32[]{:S(2)}) collective-permute-start(f32[464,128]{1,0:T(8,128)} %copy-done.1), channel_id=1, source_target_pairs={{0,4},{4,8},{8,12},{12,16},{16,20},{20,24},{24,28},{1,5},{5,9},{9,... | collective-permute-start | bytes 712712 | tf_op jit(solution)/shard_map/ppermute | solution.py:625
  27.7 12.7 %collective-permute-start.5 = (f32[464,128]{1,0:T(8,128)}, f32[464,128]{1,0:T(8,128)}, u32[]{:S(2)}, u32[]{:S(2)}) collective-permute-start(f32[464,128]{1,0:T(8,128)} %copy-done.1), channel_id=1, source_target_pairs={{4,0},{8,4},{12,8},{16,12},{20,16},{24,20},{28,24},{5,1},{9,5},{13... | collective-permute-start | bytes 712712 | tf_op jit(solution)/shard_map/ppermute | solution.py:626

commit v4 on v3

--- a/solution.py
+++ b/solution.py
@@ -169,19 +169,30 @@
         out[pl.ds(sz.side_heat, thermal.shape[0]), :] = thermal[...]
 
 
-def relay(sz, groups, thermal, side_l, side_r, box, ring):
+def relay(sz, groups, thermal, side_l, side_r, ring, box, share, sems, ring_sems):
     rows = thermal.shape[0]
     n = sz.code_rows
+    copies = [
+        pltpu.make_async_copy(side, ring.at[pl.ds(i * sz.side_rows, sz.side_rows)], ring_sems.at[i])
+        for i, side in enumerate((side_l, side_r))
+    ]
+    for c in copies:
+        c.start()
     heat = pl.ds(sz.side_heat, rows)
-    beside = jnp.where(lanes_of((rows, CZ)) < CZ // 2, side_r[heat, :], side_l[heat, :])
-    for g in range(groups):
-        at = g * (2 * rows + 2 * n)
-        box[pl.ds(at, rows), :] = thermal[...]
-        box[pl.ds(at + rows, rows), :] = beside
-        box[pl.ds(at + 2 * rows, n), :] = side_l[pl.ds(0, n), :]
-        box[pl.ds(at + 2 * rows + n, n), :] = side_r[pl.ds(0, n), :]
-    ring[pl.ds(0, sz.side_rows), :] = side_l[...]
-    ring[pl.ds(sz.side_rows, sz.side_rows), :] = side_r[...]
+    share[pl.ds(0, rows), :] = thermal[...]
+    share[pl.ds(rows, rows), :] = jnp.where(
+        lanes_of((rows, CZ)) < CZ // 2, side_r[heat, :], side_l[heat, :]
+    )
+    share[pl.ds(2 * rows, n), :] = side_l[pl.ds(0, n), :]
+    share[pl.ds(2 * rows + n, n), :] = side_r[pl.ds(0, n), :]
+    size = share.shape[0]
+    more = [
+        pltpu.make_async_copy(share, box.at[pl.ds(g * size, size)], sems.at[g]) for g in range(groups)
+    ]
+    for c in more:
+        c.start()
+    for c in copies + more:
+        c.wait()
 
 
 def decode(codes):
@@ -233,7 +244,7 @@
 
 
 def breaks_all(
-    sz, at_lo, at_hi, own, low, high, side_l, side_r, box, out, rows_ref, cols_ref, acc, rows_s, cols_s, acc_l, acc_r
+    sz, at_lo, at_hi, side_l, side_r, own, low, high, box, out, rows_ref, cols_ref, acc, rows_s, cols_s, acc_l, acc_r
 ):
     n, halo = sz.code_rows, sz.halo
     acc[pl.ds(0, PAD), :] = jnp.zeros((PAD, 4 * CZ), F32)
@@ -284,8 +295,8 @@
 
 
 def march(
-    sz, total, held, place, disp, velo, stiff, low, high, side_l, side_r, ring_lo, ring_hi, owner, row_of,
-    box, broken, out_d, out_v, out_e, fld, stiffk, heatk, bonds, forces, wait_a, wait_b, energy, pooled, temp, tables,
+    sz, total, held, place, side_l, side_r, disp, velo, stiff, low, high, ring_lo, ring_hi, owner, row_of,
+    box, broken, out_d, out_v, out_e, fld, stiffk, heatk, bonds, forces, wait_a, wait_b, energy, pooled, temp, tables, heat3,
 ):
     refs = (disp, velo, stiff)
     halo = sz.halo
@@ -312,14 +323,15 @@
         part = rest.astype(jnp.bfloat16)
         parts.append(part)
         rest = rest - part.astype(F32)
-    heat3 = jnp.concatenate(parts, axis=1)
+    for i, part in enumerate(parts):
+        heat3[:, pl.ds(i * CZ, CZ)] = part
     for j, (key, table) in enumerate(lists.items()):
         tables[pl.ds(j, 1), pl.ds(0, sz.table)] = table[0:1]
     columns = tables[...].T
     row_id = lax.broadcasted_iota(jnp.int32, (sz.table, heat.shape[0]), 1).astype(F32)
     for j, (which, side) in enumerate(lists):
         hot = jnp.where(columns[0 : sz.table, j : j + 1] == row_id, 1.0, 0.0).astype(jnp.bfloat16)
-        got = jnp.dot(hot, heat3, preferred_element_type=F32)
+        got = jnp.dot(hot, heat3[...], preferred_element_type=F32)
         temp[3 * which + side, pl.ds(PAD, sz.table), :] = (
             got[:, 0:CZ] + got[:, CZ : 2 * CZ] + got[:, 2 * CZ :]
         )
@@ -527,7 +539,7 @@
     out_e[...] = exact_dot(wanted_rows(table, out_e.shape[0]), mean)
 
 
-def call(body, ins, outs, scratch=(), name=None):
+def call(body, ins, outs, scratch=(), name=None, in_hbm=0):
     arrays, spaces, parts = [], [], []
     for i in ins:
         x, how = i if isinstance(i, tuple) else (i, i.shape[0])
@@ -562,9 +574,13 @@
     return pl.pallas_call(
         kernel,
         name=name,
-        out_shape=[jax.ShapeDtypeStruct(s, F32) for s in outs],
+        out_shape=[
+            pltpu.HBM(s, F32) if i >= len(outs) - in_hbm else jax.ShapeDtypeStruct(s, F32)
+            for i, s in enumerate(outs)
+        ],
         in_specs=[pl.BlockSpec(memory_space=m) for m in spaces],
-        out_specs=[pl.BlockSpec(memory_space=pltpu.VMEM)] * len(outs),
+        out_specs=[pl.BlockSpec(memory_space=pltpu.VMEM)] * (len(outs) - in_hbm)
+        + [pl.BlockSpec(memory_space=pltpu.HBM)] * in_hbm,
         scratch_shapes=every + [pltpu.SemaphoreType.DMA((max(1, len(staged)),))],
         compiler_params=pltpu.CompilerParams(vmem_limit_bytes=min(60 << 20, size + (6 << 20))),
     )(*arrays)
@@ -596,10 +612,10 @@
     to_right = [(i, (i + 1) % around) for i in range(around)]
     upward = [(i, i + 1) for i in range(groups - 1)]
     downward = [(i + 1, i) for i in range(groups - 1)]
+    side_r = lax.ppermute(left, "azim", to_left)
+    side_l = lax.ppermute(right, "azim", to_right)
     low = lax.ppermute(up, "axial", upward)
     high = lax.ppermute(down, "axial", downward)
-    side_r = lax.ppermute(left, "azim", to_left)
-    side_l = lax.ppermute(right, "azim", to_right)
     plane = (PAIR, CZ)
     lanes = n * CZ
     tall = NBOND * CA // 4 * NR
@@ -616,11 +632,13 @@
         name="breaks_own",
     )
     side_l, side_r, w_own = lax.optimization_barrier((side_l, side_r, w_own))
-    out_box, ring = call(
+    ring, out_box = call(
         lambda *refs: relay(sz, groups, *refs),
         [thermal, (side_l, pltpu.VMEM), (side_r, pltpu.VMEM)],
-        [(groups * share, CZ), (2 * sz.side_rows, CZ)],
+        [(2 * sz.side_rows, CZ), (groups * share, CZ)],
+        [pltpu.VMEM((share, CZ), F32), pltpu.SemaphoreType.DMA((groups,)), pltpu.SemaphoreType.DMA((2,))],
         name="relay",
+        in_hbm=2,
     )
     ring_lo = lax.ppermute(ring, "axial", upward)
     ring_hi = lax.ppermute(ring, "axial", downward)
@@ -638,7 +656,7 @@
 
     (broken,) = call(
         all_breaks,
-        [(place, pltpu.SMEM), (w_own, pltpu.VMEM), (low, n), (high, n), (side_l, pltpu.VMEM), (side_r, pltpu.VMEM), (box, pltpu.VMEM)],
+        [(place, pltpu.SMEM), (side_l, pltpu.VMEM), (side_r, pltpu.VMEM), (w_own, pltpu.VMEM), (low, n), (high, n), (box, pltpu.VMEM)],
         [(NBOND, sz.ext) + plane],
         work
         + [
@@ -662,12 +680,13 @@
         pltpu.VMEM((CA // 2 * NR, CZ), F32),
         pltpu.VMEM((9, PAD + sz.table + PAD, CZ), F32),
         pltpu.VMEM((CZ, CZ), F32),
+        pltpu.VMEM((groups * share, 3 * CZ), jnp.bfloat16),
     ]
     total = groups * CA
     out_d, out_v, out_e = call(
         lambda *refs: march(sz, total, held, *refs),
         [
-            (place, pltpu.SMEM), disp, velo, stif, low, high, (side_l, pltpu.VMEM), (side_r, pltpu.VMEM), ring_lo, ring_hi, owner, local,
+            (place, pltpu.SMEM), (side_l, pltpu.VMEM), (side_r, pltpu.VMEM), disp, velo, stif, low, high, ring_lo, ring_hi, owner, local,
             (box, pltpu.VMEM), (broken, pltpu.VMEM),
         ],
         [disp.shape, velo.shape, (groups * held, CZ)],

time: 69.8 us -> 69.2 us (level)
  local copies, waits for them, and re-layouts: 1.42 us -> 0 us
  Pallas kernels: 34.2 us -> 35 us
    unnamed x4 -> x0, local copies, waits for them, and re-layouts: 1.42 us -> none
    pallas_call x5, Pallas kernels: 34.2 us -> 35 us  [call(): pl.pallas_call(kernel, name=name, out_shape=[pltpu.HBM(s, F32) if i >= le...]
  transfers between devices with their start and end apart: 7 -> 7, of which waited for: 3 -> 3; matrix products, arithmetic and copies ran while one was open for 0% -> 0% of each run, Pallas kernels for 16% -> 17%
where the time goes in v4:
time: 69.2 us; the launch traced here: 68.8 us
  Pallas kernels  35 us (51%)
  starting transfers between devices  17.4 us (25%)
  blocking collectives  7.58 us (11%)
  waiting for transfers between devices  7.46 us (11%)
  between operations  0.71 us (1%)
    pallas_call x5, Pallas kernels, call(): pl.pallas_call(kernel, name=name, out_shape=[pltpu.HBM(s, F32) if i >= le...  35 us
    all_to_all x1, blocking collectives, on_device(): lax.all_to_all(parts, 'axial', split_axis=0, concat_axis=0, tiled=True)  7.58 us
    all_to_all x1, starting transfers between devices, on_device(): lax.all_to_all(out_box.reshape(groups, share, CZ), 'axial', split_axis=0,...  3.87 us
    ppermute x1, waiting for transfers between devices, on_device(): side_r = lax.ppermute(left, 'azim', to_left)  3.17 us
    ppermute x1, starting transfers between devices, on_device(): low = lax.ppermute(up, 'axial', upward)  3.15 us
    ppermute x1, starting transfers between devices, on_device(): ring_lo = lax.ppermute(ring, 'axial', upward)  3.09 us
    all_to_all x1, waiting for transfers between devices, on_device(): lax.all_to_all(out_box.reshape(groups, share, CZ), 'axial', split_axis=0,...  3.08 us
    ppermute x1, starting transfers between devices, on_device(): side_l = lax.ppermute(right, 'azim', to_right)  2.46 us
  transfers between devices with their start and end apart: 7, of which 3 were waited for; matrix products, arithmetic and copies ran while one was open for 0% of the time, Pallas kernels for 17%

profile of v4, /device:TPU:0, one launch (start us, length us, event | category | flops | bytes accessed | tf_op | source)
XLA Modules:
  0.0 68.8 jit_solution(7946665478582739634)
XLA Ops:
  0.6 2.4 %pack_first.1 = (f32[936,128]{1,0:T(8,128)}, f32[936,128]{1,0:T(8,128)}, f32[232,128]{1,0:T(8,128)S(1)}, f32[232,128]{1,0:T(8,128)S(1)}, f32[16,128]{1,0:T(8,128)S(1)}) custom-call(f32[576,128]{1,0:T(8,128)} %bitcast.25, f32[576,128]{1,0:T(8,128)} %bitcast.27, f32[192,128]{1,0:T(8,128)} %bitcast.29, s32[16,128]{1,0:T(8,128)} %bitcast.32, s32[1,48]{1,0:T(1,128)} %bitcast.33, ...), custom_call_target="tpu_custom_call" | custom-call | tf_op jit(solution)/shard_map/pack_first/pallas_call | solution.py:574
  3.1 3.2 %collective-permute-start.2 = (f32[936,128]{1,0:T(8,128)}, f32[936,128]{1,0:T(8,128)}, u32[]{:S(2)}, u32[]{:S(2)}) collective-permute-start(f32[936,128]{1,0:T(8,128)} %get-tuple-element.21), channel_id=1, source_target_pairs={{0,4},{4,8},{8,12},{12,16},{16,20},{20,24},{24,28},{1,5},{5,9},{9,... | collective-permute-start | bytes 1437704 | tf_op jit(solution)/shard_map/ppermute | solution.py:617
  6.2 1.3 %collective-permute-start.3 = (f32[936,128]{1,0:T(8,128)}, f32[936,128]{1,0:T(8,128)}, u32[]{:S(2)}, u32[]{:S(2)}) collective-permute-start(f32[936,128]{1,0:T(8,128)} %get-tuple-element.22), channel_id=1, source_target_pairs={{4,0},{8,4},{12,8},{16,12},{20,16},{24,20},{28,24},{5,1},{9,5},{13... | collective-permute-start | bytes 1437704 | tf_op jit(solution)/shard_map/ppermute | solution.py:618
  7.5 2.5 %collective-permute-start = (f32[232,128]{1,0:T(8,128)S(1)}, f32[232,128]{1,0:T(8,128)S(1)}, u32[]{:S(2)}, u32[]{:S(2)}) collective-permute-start(f32[232,128]{1,0:T(8,128)S(1)} %get-tuple-element.16), channel_id=1, source_target_pairs={{0,1},{1,2},{2,3},{3,0},{4,5},{5,6},{6,7},{7,4},{8,9},{9,10},{10,1... | collective-permute-start | bytes 356360 | tf_op jit(solution)/shard_map/ppermute | solution.py:616
  10.0 2.1 %collective-permute-start.1 = (f32[232,128]{1,0:T(8,128)S(1)}, f32[232,128]{1,0:T(8,128)S(1)}, u32[]{:S(2)}, u32[]{:S(2)}) collective-permute-start(f32[232,128]{1,0:T(8,128)S(1)} %get-tuple-element.17), channel_id=1, source_target_pairs={{0,3},{1,0},{2,1},{3,2},{4,7},{5,4},{6,5},{7,6},{8,11},{9,8},{10,9... | collective-permute-start | bytes 356360 | tf_op jit(solution)/shard_map/ppermute | solution.py:615
  12.1 2.1 %breaks_own.1.refs_3_ = f32[15,16,24,128]{3,2,1,0:T(8,128)S(1)} custom-call(f32[16,128]{1,0:T(8,128)S(1)} %get-tuple-element.18.refs_0_), custom_call_target="tpu_custom_call" | custom-call | tf_op jit(solution)/shard_map/breaks_own/pallas_call | solution.py:574
  14.2 1.2 %collective-permute-done.refs_1_ = f32[232,128]{1,0:T(8,128)S(1)} collective-permute-done((f32[232,128]{1,0:T(8,128)S(1)}, f32[232,128]{1,0:T(8,128)S(1)}, u32[]{:S(2)}, u32[]{:S(2)}) %collective-permute-start) | collective-permute-done | bytes 118816 | tf_op jit(solution)/shard_map/ppermute | solution.py:616
  15.4 3.2 %collective-permute-done.1.refs_2_ = f32[232,128]{1,0:T(8,128)S(1)} collective-permute-done((f32[232,128]{1,0:T(8,128)S(1)}, f32[232,128]{1,0:T(8,128)S(1)}, u32[]{:S(2)}, u32[]{:S(2)}) %collective-permute-start.1) | collective-permute-done | bytes 118816 | tf_op jit(solution)/shard_map/ppermute | solution.py:615
  18.5 1.6 %relay.1 = (f32[464,128]{1,0:T(8,128)}, f32[640,128]{1,0:T(8,128)}) custom-call(f32[24,128]{1,0:T(8,128)} %refs_0_.1, f32[232,128]{1,0:T(8,128)S(1)} %collective-permute-done.refs_1_, f32[232,128]{1,0:T(8,128)S(1)} %collective-permute-done.1.refs_2_), custom_call_target="tpu_custom_call" | custom-call | tf_op jit(solution)/shard_map/relay/pallas_call | solution.py:574
  20.1 3.9 %all-to-all-start = ((f32[8,80,128]{2,1,0:T(8,128)}), f32[8,80,128]{2,1,0:T(8,128)S(1)}, u32[]{:S(2)}, u32[]{:S(2)}) async-start(f32[8,80,128]{2,1,0:T(8,128)} %bitcast.31), calls=%async_computation | async-start | bytes 655360 | tf_op jit(solution)/shard_map/all_to_all | solution.py:645
  24.0 3.1 %collective-permute-start.4 = (f32[464,128]{1,0:T(8,128)}, f32[464,128]{1,0:T(8,128)}, u32[]{:S(2)}, u32[]{:S(2)}) collective-permute-start(f32[464,128]{1,0:T(8,128)} %get-tuple-element.23), channel_id=1, source_target_pairs={{0,4},{4,8},{8,12},{12,16},{16,20},{20,24},{24,28},{1,5},{5,9},{9,... | collective-permute-start | bytes 712712 | tf_op jit(solution)/shard_map/ppermute | solution.py:643
  27.1 1.5 %collective-permute-start.5 = (f32[464,128]{1,0:T(8,128)}, f32[464,128]{1,0:T(8,128)}, u32[]{:S(2)}, u32[]{:S(2)}) collective-permute-start(f32[464,128]{1,0:T(8,128)} %get-tuple-element.23), channel_id=1, source_target_pairs={{4,0},{8,4},{12,8},{16,12},{20,16},{24,20},{28,24},{5,1},{9,5},{13... | collective-permute-start | bytes 712712 | tf_op jit(solution)/shard_map/ppermute | solution.py:644
  28.5 3.1 %all-to-all-done = f32[8,80,128]{2,1,0:T(8,128)S(1)} async-done(((f32[8,80,128]{2,1,0:T(8,128)}), f32[8,80,128]{2,1,0:T(8,128)S(1)}, u32[]{:S(2)}, u32[]{:S(2)}) %all-to-all-start) | async-done | bytes 327712 | tf_op jit(solution)/shard_map/all_to_all | solution.py:645
  31.6 0.0 collective-permute-done.2.refs_4_.refs_6_
  31.6 0.0 collective-permute-done.3.refs_5_.refs_7_
  31.6 8.1 %breaks_all.1.refs_13_ = f32[15,40,24,128]{3,2,1,0:T(8,128)S(1)} custom-call(s32[1]{0:T(128)} %bitcast.refs_0_, f32[232,128]{1,0:T(8,128)S(1)} %collective-permute-done.refs_1_, f32[232,128]{1,0:T(8,128)S(1)} %collective-permute-done.1.refs_2_, f32[15,16,24,128]{3,2,1,0:T(8,128)S(1)} %breaks_own.1.refs_3_, ...), custom_call_target="tpu_custom_call" | custom-call | tf_op jit(solution)/shard_map/breaks_all/pallas_call | solution.py:574
  39.8 0.0 collective-permute-done.4.refs_8_
  39.8 0.0 collective-permute-done.5.refs_9_
  39.8 20.8 %march.1 = (f32[576,128]{1,0:T(8,128)}, f32[576,128]{1,0:T(8,128)}, f32[192,128]{1,0:T(8,128)S(1)}) custom-call(s32[1]{0:T(128)} %bitcast.refs_0_, f32[232,128]{1,0:T(8,128)S(1)} %collective-permute-done.refs_1_, f32[232,128]{1,0:T(8,128)S(1)} %collective-permute-done.1.refs_2_, f32[576,128]{1,0:T(8,128)} %bitcast.26, f32[576,128]{1,0:T(8,128)} %bitcast.28, ...), custom_call_target="tpu_custom_call" | custom-call | tf_op jit(solution)/shard_map/march/pallas_call | solution.py:574
  60.6 7.6 %all_to_all.10 = f32[8,24,128]{2,1,0:T(8,128)S(1)} all-to-all(f32[8,24,128]{2,1,0:T(8,128)S(1)} %bitcast.24), channel_id=1, replica_groups=mesh['axial'=8,'azim'=4] {'axial'}, dimensions={0} | all-to-all | bytes 196608 | tf_op jit(solution)/shard_map/all_to_all | solution.py:697
  68.2 0.6 reduce_sum.9
Async XLA Ops:
  3.1 28.5 %collective-permute-start.2 = (f32[936,128]{1,0:T(8,128)}, f32[936,128]{1,0:T(8,128)}, u32[]{:S(2)}, u32[]{:S(2)}) collective-permute-start(f32[936,128]{1,0:T(8,128)} %get-tuple-element.21), channel_id=1, source_target_pairs={{0,4},{4,8},{8,12},{12,16},{16,20},{20,24},{24,28},{1,5},{5,9},{9,... | collective-permute-start | bytes 1437704 | tf_op jit(solution)/shard_map/ppermute | solution.py:617
  6.2 25.4 %collective-permute-start.3 = (f32[936,128]{1,0:T(8,128)}, f32[936,128]{1,0:T(8,128)}, u32[]{:S(2)}, u32[]{:S(2)}) collective-permute-start(f32[936,128]{1,0:T(8,128)} %get-tuple-element.22), channel_id=1, source_target_pairs={{4,0},{8,4},{12,8},{16,12},{20,16},{24,20},{28,24},{5,1},{9,5},{13... | collective-permute-start | bytes 1437704 | tf_op jit(solution)/shard_map/ppermute | solution.py:618
  7.5 7.8 %collective-permute-start = (f32[232,128]{1,0:T(8,128)S(1)}, f32[232,128]{1,0:T(8,128)S(1)}, u32[]{:S(2)}, u32[]{:S(2)}) collective-permute-start(f32[232,128]{1,0:T(8,128)S(1)} %get-tuple-element.16), channel_id=1, source_target_pairs={{0,1},{1,2},{2,3},{3,0},{4,5},{5,6},{6,7},{7,4},{8,9},{9,10},{10,1... | collective-permute-start | bytes 356360 | tf_op jit(solution)/shard_map/ppermute | solution.py:616
  10.0 8.6 %collective-permute-start.1 = (f32[232,128]{1,0:T(8,128)S(1)}, f32[232,128]{1,0:T(8,128)S(1)}, u32[]{:S(2)}, u32[]{:S(2)}) collective-permute-start(f32[232,128]{1,0:T(8,128)S(1)} %get-tuple-element.17), channel_id=1, source_target_pairs={{0,3},{1,0},{2,1},{3,2},{4,7},{5,4},{6,5},{7,6},{8,11},{9,8},{10,9... | collective-permute-start | bytes 356360 | tf_op jit(solution)/shard_map/ppermute | solution.py:615
  20.1 11.5 %all-to-all-start = ((f32[8,80,128]{2,1,0:T(8,128)}), f32[8,80,128]{2,1,0:T(8,128)S(1)}, u32[]{:S(2)}, u32[]{:S(2)}) async-start(f32[8,80,128]{2,1,0:T(8,128)} %bitcast.31), calls=%async_computation | async-start | bytes 655360 | tf_op jit(solution)/shard_map/all_to_all | solution.py:645
  24.0 15.8 %collective-permute-start.4 = (f32[464,128]{1,0:T(8,128)}, f32[464,128]{1,0:T(8,128)}, u32[]{:S(2)}, u32[]{:S(2)}) collective-permute-start(f32[464,128]{1,0:T(8,128)} %get-tuple-element.23), channel_id=1, source_target_pairs={{0,4},{4,8},{8,12},{12,16},{16,20},{20,24},{24,28},{1,5},{5,9},{9,... | collective-permute-start | bytes 712712 | tf_op jit(solution)/shard_map/ppermute | solution.py:643
  27.1 12.7 %collective-permute-start.5 = (f32[464,128]{1,0:T(8,128)}, f32[464,128]{1,0:T(8,128)}, u32[]{:S(2)}, u32[]{:S(2)}) collective-permute-start(f32[464,128]{1,0:T(8,128)} %get-tuple-element.23), channel_id=1, source_target_pairs={{4,0},{8,4},{12,8},{16,12},{20,16},{24,20},{28,24},{5,1},{9,5},{13... | collective-permute-start | bytes 712712 | tf_op jit(solution)/shard_map/ppermute | solution.py:644

commit v5 on v4

--- a/solution.py
+++ b/solution.py
@@ -250,7 +250,7 @@
     acc[pl.ds(0, PAD), :] = jnp.zeros((PAD, 4 * CZ), F32)
     parts = [
         (low[...], (CA - halo) // 4, halo // 4, CA - halo, halo, 0),
-        (high[...], 0, halo // 4, 0, halo, halo + CA),
+        (high[...], 0, halo // 4, 0, halo - REACH, halo + CA),
     ]
     read_breaks(sz, parts, out, rows_ref, cols_ref, acc)
     wide = lanes_of((PAIR, CZ))
@@ -267,7 +267,7 @@
     rows = -(-NBOND * NR // 16) * 16
     for which, (left, right) in enumerate(sources):
         first = CA - sz.halo if which == 0 else 0
-        count = CA if which == 1 else sz.halo
+        count = (sz.halo, CA, sz.halo - REACH)[which]
         cols = -(-count // PER) * CZ
         for side, codes in enumerate((left, right)):
             k, a, r, z = decode(codes)

time: 69.2 us -> 69.1 us (level)
  no operation moved by 1% of the time
where the time goes in v5:
time: 69.1 us; the launch traced here: 68.6 us
  Pallas kernels  34.9 us (51%)
  starting transfers between devices  17.4 us (25%)
  blocking collectives  7.58 us (11%)
  waiting for transfers between devices  7.46 us (11%)
  between operations  0.71 us (1%)
    pallas_call x5, Pallas kernels, call(): pl.pallas_call(kernel, name=name, out_shape=[pltpu.HBM(s, F32) if i >= le...  34.9 us
    all_to_all x1, blocking collectives, on_device(): lax.all_to_all(parts, 'axial', split_axis=0, concat_axis=0, tiled=True)  7.58 us
    all_to_all x1, starting transfers between devices, on_device(): lax.all_to_all(out_box.reshape(groups, share, CZ), 'axial', split_axis=0,...  3.87 us
    ppermute x1, waiting for transfers between devices, on_device(): side_r = lax.ppermute(left, 'azim', to_left)  3.17 us
    ppermute x1, starting transfers between devices, on_device(): low = lax.ppermute(up, 'axial', upward)  3.15 us
    ppermute x1, starting transfers between devices, on_device(): ring_lo = lax.ppermute(ring, 'axial', upward)  3.09 us
    all_to_all x1, waiting for transfers between devices, on_device(): lax.all_to_all(out_box.reshape(groups, share, CZ), 'axial', split_axis=0,...  3.08 us
    ppermute x1, starting transfers between devices, on_device(): side_l = lax.ppermute(right, 'azim', to_right)  2.46 us
  transfers between devices with their start and end apart: 7, of which 3 were waited for; matrix products, arithmetic and copies ran while one was open for 0% of the time, Pallas kernels for 17%

profile of v5, /device:TPU:0, one launch (start us, length us, event | category | flops | bytes accessed | tf_op | source)
XLA Modules:
  0.0 68.6 jit_solution(197424088703153015)
XLA Ops:
  0.6 2.4 %pack_first.1 = (f32[936,128]{1,0:T(8,128)}, f32[936,128]{1,0:T(8,128)}, f32[232,128]{1,0:T(8,128)S(1)}, f32[232,128]{1,0:T(8,128)S(1)}, f32[16,128]{1,0:T(8,128)S(1)}) custom-call(f32[576,128]{1,0:T(8,128)} %bitcast.25, f32[576,128]{1,0:T(8,128)} %bitcast.27, f32[192,128]{1,0:T(8,128)} %bitcast.29, s32[16,128]{1,0:T(8,128)} %bitcast.32, s32[1,48]{1,0:T(1,128)} %bitcast.33, ...), custom_call_target="tpu_custom_call" | custom-call | tf_op jit(solution)/shard_map/pack_first/pallas_call | solution.py:574
  3.1 3.2 %collective-permute-start.2 = (f32[936,128]{1,0:T(8,128)}, f32[936,128]{1,0:T(8,128)}, u32[]{:S(2)}, u32[]{:S(2)}) collective-permute-start(f32[936,128]{1,0:T(8,128)} %get-tuple-element.21), channel_id=1, source_target_pairs={{0,4},{4,8},{8,12},{12,16},{16,20},{20,24},{24,28},{1,5},{5,9},{9,... | collective-permute-start | bytes 1437704 | tf_op jit(solution)/shard_map/ppermute | solution.py:617
  6.2 1.3 %collective-permute-start.3 = (f32[936,128]{1,0:T(8,128)}, f32[936,128]{1,0:T(8,128)}, u32[]{:S(2)}, u32[]{:S(2)}) collective-permute-start(f32[936,128]{1,0:T(8,128)} %get-tuple-element.22), channel_id=1, source_target_pairs={{4,0},{8,4},{12,8},{16,12},{20,16},{24,20},{28,24},{5,1},{9,5},{13... | collective-permute-start | bytes 1437704 | tf_op jit(solution)/shard_map/ppermute | solution.py:618
  7.5 2.5 %collective-permute-start = (f32[232,128]{1,0:T(8,128)S(1)}, f32[232,128]{1,0:T(8,128)S(1)}, u32[]{:S(2)}, u32[]{:S(2)}) collective-permute-start(f32[232,128]{1,0:T(8,128)S(1)} %get-tuple-element.16), channel_id=1, source_target_pairs={{0,1},{1,2},{2,3},{3,0},{4,5},{5,6},{6,7},{7,4},{8,9},{9,10},{10,1... | collective-permute-start | bytes 356360 | tf_op jit(solution)/shard_map/ppermute | solution.py:616
  10.0 2.1 %collective-permute-start.1 = (f32[232,128]{1,0:T(8,128)S(1)}, f32[232,128]{1,0:T(8,128)S(1)}, u32[]{:S(2)}, u32[]{:S(2)}) collective-permute-start(f32[232,128]{1,0:T(8,128)S(1)} %get-tuple-element.17), channel_id=1, source_target_pairs={{0,3},{1,0},{2,1},{3,2},{4,7},{5,4},{6,5},{7,6},{8,11},{9,8},{10,9... | collective-permute-start | bytes 356360 | tf_op jit(solution)/shard_map/ppermute | solution.py:615
  12.1 2.1 %breaks_own.1.refs_3_ = f32[15,16,24,128]{3,2,1,0:T(8,128)S(1)} custom-call(f32[16,128]{1,0:T(8,128)S(1)} %get-tuple-element.18.refs_0_), custom_call_target="tpu_custom_call" | custom-call | tf_op jit(solution)/shard_map/breaks_own/pallas_call | solution.py:574
  14.2 1.2 %collective-permute-done.refs_1_ = f32[232,128]{1,0:T(8,128)S(1)} collective-permute-done((f32[232,128]{1,0:T(8,128)S(1)}, f32[232,128]{1,0:T(8,128)S(1)}, u32[]{:S(2)}, u32[]{:S(2)}) %collective-permute-start) | collective-permute-done | bytes 118816 | tf_op jit(solution)/shard_map/ppermute | solution.py:616
  15.4 3.2 %collective-permute-done.1.refs_2_ = f32[232,128]{1,0:T(8,128)S(1)} collective-permute-done((f32[232,128]{1,0:T(8,128)S(1)}, f32[232,128]{1,0:T(8,128)S(1)}, u32[]{:S(2)}, u32[]{:S(2)}) %collective-permute-start.1) | collective-permute-done | bytes 118816 | tf_op jit(solution)/shard_map/ppermute | solution.py:615
  18.5 1.6 %relay.1 = (f32[464,128]{1,0:T(8,128)}, f32[640,128]{1,0:T(8,128)}) custom-call(f32[24,128]{1,0:T(8,128)} %refs_0_.1, f32[232,128]{1,0:T(8,128)S(1)} %collective-permute-done.refs_1_, f32[232,128]{1,0:T(8,128)S(1)} %collective-permute-done.1.refs_2_), custom_call_target="tpu_custom_call" | custom-call | tf_op jit(solution)/shard_map/relay/pallas_call | solution.py:574
  20.1 3.9 %all-to-all-start = ((f32[8,80,128]{2,1,0:T(8,128)}), f32[8,80,128]{2,1,0:T(8,128)S(1)}, u32[]{:S(2)}, u32[]{:S(2)}) async-start(f32[8,80,128]{2,1,0:T(8,128)} %bitcast.31), calls=%async_computation | async-start | bytes 655360 | tf_op jit(solution)/shard_map/all_to_all | solution.py:645
  24.0 3.1 %collective-permute-start.4 = (f32[464,128]{1,0:T(8,128)}, f32[464,128]{1,0:T(8,128)}, u32[]{:S(2)}, u32[]{:S(2)}) collective-permute-start(f32[464,128]{1,0:T(8,128)} %get-tuple-element.23), channel_id=1, source_target_pairs={{0,4},{4,8},{8,12},{12,16},{16,20},{20,24},{24,28},{1,5},{5,9},{9,... | collective-permute-start | bytes 712712 | tf_op jit(solution)/shard_map/ppermute | solution.py:643
  27.1 1.5 %collective-permute-start.5 = (f32[464,128]{1,0:T(8,128)}, f32[464,128]{1,0:T(8,128)}, u32[]{:S(2)}, u32[]{:S(2)}) collective-permute-start(f32[464,128]{1,0:T(8,128)} %get-tuple-element.23), channel_id=1, source_target_pairs={{4,0},{8,4},{12,8},{16,12},{20,16},{24,20},{28,24},{5,1},{9,5},{13... | collective-permute-start | bytes 712712 | tf_op jit(solution)/shard_map/ppermute | solution.py:644
  28.5 3.1 %all-to-all-done = f32[8,80,128]{2,1,0:T(8,128)S(1)} async-done(((f32[8,80,128]{2,1,0:T(8,128)}), f32[8,80,128]{2,1,0:T(8,128)S(1)}, u32[]{:S(2)}, u32[]{:S(2)}) %all-to-all-start) | async-done | bytes 327712 | tf_op jit(solution)/shard_map/all_to_all | solution.py:645
  31.6 0.0 collective-permute-done.2.refs_4_.refs_6_
  31.6 0.0 collective-permute-done.3.refs_5_.refs_7_
  31.6 8.0 %breaks_all.1.refs_13_ = f32[15,40,24,128]{3,2,1,0:T(8,128)S(1)} custom-call(s32[1]{0:T(128)} %bitcast.refs_0_, f32[232,128]{1,0:T(8,128)S(1)} %collective-permute-done.refs_1_, f32[232,128]{1,0:T(8,128)S(1)} %collective-permute-done.1.refs_2_, f32[15,16,24,128]{3,2,1,0:T(8,128)S(1)} %breaks_own.1.refs_3_, ...), custom_call_target="tpu_custom_call" | custom-call | tf_op jit(solution)/shard_map/breaks_all/pallas_call | solution.py:574
  39.6 0.0 collective-permute-done.4.refs_8_
  39.6 0.0 collective-permute-done.5.refs_9_
  39.6 20.8 %march.1 = (f32[576,128]{1,0:T(8,128)}, f32[576,128]{1,0:T(8,128)}, f32[192,128]{1,0:T(8,128)S(1)}) custom-call(s32[1]{0:T(128)} %bitcast.refs_0_, f32[232,128]{1,0:T(8,128)S(1)} %collective-permute-done.refs_1_, f32[232,128]{1,0:T(8,128)S(1)} %collective-permute-done.1.refs_2_, f32[576,128]{1,0:T(8,128)} %bitcast.26, f32[576,128]{1,0:T(8,128)} %bitcast.28, ...), custom_call_target="tpu_custom_call" | custom-call | tf_op jit(solution)/shard_map/march/pallas_call | solution.py:574
  60.4 7.6 %all_to_all.10 = f32[8,24,128]{2,1,0:T(8,128)S(1)} all-to-all(f32[8,24,128]{2,1,0:T(8,128)S(1)} %bitcast.24), channel_id=1, replica_groups=mesh['axial'=8,'azim'=4] {'axial'}, dimensions={0} | all-to-all | bytes 196608 | tf_op jit(solution)/shard_map/all_to_all | solution.py:697
  68.0 0.6 reduce_sum.9
Async XLA Ops:
  3.1 28.5 %collective-permute-start.2 = (f32[936,128]{1,0:T(8,128)}, f32[936,128]{1,0:T(8,128)}, u32[]{:S(2)}, u32[]{:S(2)}) collective-permute-start(f32[936,128]{1,0:T(8,128)} %get-tuple-element.21), channel_id=1, source_target_pairs={{0,4},{4,8},{8,12},{12,16},{16,20},{20,24},{24,28},{1,5},{5,9},{9,... | collective-permute-start | bytes 1437704 | tf_op jit(solution)/shard_map/ppermute | solution.py:617
  6.2 25.4 %collective-permute-start.3 = (f32[936,128]{1,0:T(8,128)}, f32[936,128]{1,0:T(8,128)}, u32[]{:S(2)}, u32[]{:S(2)}) collective-permute-start(f32[936,128]{1,0:T(8,128)} %get-tuple-element.22), channel_id=1, source_target_pairs={{4,0},{8,4},{12,8},{16,12},{20,16},{24,20},{28,24},{5,1},{9,5},{13... | collective-permute-start | bytes 1437704 | tf_op jit(solution)/shard_map/ppermute | solution.py:618
  7.5 7.8 %collective-permute-start = (f32[232,128]{1,0:T(8,128)S(1)}, f32[232,128]{1,0:T(8,128)S(1)}, u32[]{:S(2)}, u32[]{:S(2)}) collective-permute-start(f32[232,128]{1,0:T(8,128)S(1)} %get-tuple-element.16), channel_id=1, source_target_pairs={{0,1},{1,2},{2,3},{3,0},{4,5},{5,6},{6,7},{7,4},{8,9},{9,10},{10,1... | collective-permute-start | bytes 356360 | tf_op jit(solution)/shard_map/ppermute | solution.py:616
  10.0 8.6 %collective-permute-start.1 = (f32[232,128]{1,0:T(8,128)S(1)}, f32[232,128]{1,0:T(8,128)S(1)}, u32[]{:S(2)}, u32[]{:S(2)}) collective-permute-start(f32[232,128]{1,0:T(8,128)S(1)} %get-tuple-element.17), channel_id=1, source_target_pairs={{0,3},{1,0},{2,1},{3,2},{4,7},{5,4},{6,5},{7,6},{8,11},{9,8},{10,9... | collective-permute-start | bytes 356360 | tf_op jit(solution)/shard_map/ppermute | solution.py:615
  20.1 11.5 %all-to-all-start = ((f32[8,80,128]{2,1,0:T(8,128)}), f32[8,80,128]{2,1,0:T(8,128)S(1)}, u32[]{:S(2)}, u32[]{:S(2)}) async-start(f32[8,80,128]{2,1,0:T(8,128)} %bitcast.31), calls=%async_computation | async-start | bytes 655360 | tf_op jit(solution)/shard_map/all_to_all | solution.py:645
  24.0 15.6 %collective-permute-start.4 = (f32[464,128]{1,0:T(8,128)}, f32[464,128]{1,0:T(8,128)}, u32[]{:S(2)}, u32[]{:S(2)}) collective-permute-start(f32[464,128]{1,0:T(8,128)} %get-tuple-element.23), channel_id=1, source_target_pairs={{0,4},{4,8},{8,12},{12,16},{16,20},{20,24},{24,28},{1,5},{5,9},{9,... | collective-permute-start | bytes 712712 | tf_op jit(solution)/shard_map/ppermute | solution.py:643
  27.1 12.6 %collective-permute-start.5 = (f32[464,128]{1,0:T(8,128)}, f32[464,128]{1,0:T(8,128)}, u32[]{:S(2)}, u32[]{:S(2)}) collective-permute-start(f32[464,128]{1,0:T(8,128)} %get-tuple-element.23), channel_id=1, source_target_pairs={{4,0},{8,4},{12,8},{16,12},{20,16},{24,20},{28,24},{5,1},{9,5},{13... | collective-permute-start | bytes 712712 | tf_op jit(solution)/shard_map/ppermute | solution.py:644
